TPU v7x, 512 devices: a whole 4x8x8 slice. The times are simulated.
512 devices in a mesh: spot: 128 (over y_lo, z, x, core), var: 4 (over y_hi).
Axes of the slice: x: 4, y: 8 (y_hi: 4, y_lo: 2; y = y_hi * 2 + y_lo), z: 8, core: 2. Of those that a mesh axis runs over, the one named last changes fastest.
Arguments:
- option_value: float32 [256, 64, 1024], P('spot', None, 'var'), may hold values from -6 to 6
- spot_nodes: int32 [256], replicated, may hold values from 0 to 1023, as said below
- var_nodes: int32 [1024], replicated, may hold values from 0 to 4095, as said below
- rate_nodes: int32 [64], replicated, may hold values from 0 to 255, as said below
Outputs:
- advanced: float32 [256, 64, 1024], P('spot', None, 'var')
Inputs may be any that keep to these rules, and one draw needn't show every extreme that they name: `spot_nodes`: strictly increasing, consecutive entries differ by 1 to 7, the first is 0 and the last 1023. `var_nodes`: strictly increasing, consecutive entries differ by 1 to 7, the first is 0 and the last 4095. `rate_nodes`: strictly increasing, consecutive entries differ by 1 to 7, the first is 0 and the last 255.
All inputs are finite; a program needn't handle non-finite values.
Results may differ from a plain program's by a relative error of at most 0.00045.
Values sent between devices are 32-bit elements; how exact they have to be, the bound alone decides.
A program may use at most 64 MiB of HBM per device.

v0:
```python
import jax
import jax.numpy as jnp
from jax import lax
from jax.experimental import pallas as pl
from jax.experimental.pallas import tpu as pltpu
from jax.sharding import PartitionSpec as P

time_step = 0.01
solve_scale = 0.5 * time_step
half_step = 0.5 * time_step
spot_low = 0.5
spot_high = 2.5
var_low = 0.02
var_high = 1.0
rate_low = -0.1
rate_high = 0.2
dividend_yield = 0.02
reversion_var = 2.0
long_var = 0.04
vol_var = 0.6
reversion_rate = 0.1
long_rate = 0.05
vol_rate = 0.1
coupling_sv = -0.7 * vol_var
coupling_sr = 0.2 * vol_rate
coupling_vr = 0.1 * vol_var * vol_rate


def padded_2(array, sides, width):
    for axis, dim in sides:
        devices, length = (lax.axis_size(axis), array.shape[dim])
        up = [(i, (i + 1) % devices) for i in range(devices - 1)]
        down = [(j, i) for i, j in up]
        last = lax.slice_in_dim(array, length - width, length, axis=dim)
        initial = lax.slice_in_dim(array, 0, width, axis=dim)
        before = lax.ppermute(last, axis, up)
        after = lax.ppermute(initial, axis, down)
        array = jnp.concatenate([before, array, after], axis=dim)
    return array


def coordinates(node_list, low_end, high_end):
    length = node_list.shape[0]
    extended = jnp.concatenate(
        [jnp.full((1,), -1, jnp.int32), node_list, jnp.full((1,), 4 * length, jnp.int32)]
    )
    return low_end + (high_end - low_end) * extended.astype(jnp.float32) / (4 * length - 1)


def stencil_weights(coords):
    behind = coords[1:-1] - coords[:-2]
    ahead = coords[2:] - coords[1:-1]
    spread = behind + ahead
    first_diff = (
        -ahead / (behind * spread),
        (ahead - behind) / (behind * ahead),
        behind / (ahead * spread),
    )
    second_diff = (2.0 / (behind * spread), -2.0 / (behind * ahead), 2.0 / (ahead * spread))
    return (first_diff, second_diff)


def geometry(coords, position, dim_count, offset, length):
    first_diff, second_diff = stencil_weights(coords)
    vectors = (coords[1:-1],) + first_diff + second_diff
    target = [1] * dim_count
    target[position] = length
    pieces = [
        lax.dynamic_slice_in_dim(vector, offset, length).reshape(target) for vector in vectors
    ]
    return (pieces[0], tuple(pieces[1:4]), tuple(pieces[4:7]))


def spot_terms(spot_x, var_x, rate_x):
    return (0.5 * spot_x * spot_x * var_x, (rate_x - dividend_yield) * spot_x)


def var_terms(var_x):
    return (0.5 * vol_var * vol_var * var_x, reversion_var * (long_var - var_x))


def rate_terms(rate_x):
    return (0.5 * vol_rate * vol_rate, reversion_rate * (long_rate - rate_x))


def line_coefficients(diffusion, advection, reaction, first_diff, second_diff):
    behind = diffusion * second_diff[0] + advection * first_diff[0]
    centre = diffusion * second_diff[1] + advection * first_diff[1] - reaction
    ahead = diffusion * second_diff[2] + advection * first_diff[2]
    return (behind, centre, ahead)


def explicit_terms(padded, spot_geo, var_geo, rate_geo, mixing_only):
    spot_x, spot_first, spot_second = spot_geo
    var_x, var_first, var_second = var_geo
    rate_x, rate_first, rate_second = rate_geo
    spot_rows = padded.shape[0] - 2
    planes = padded.shape[1] - 2
    var_cols = padded.shape[2] - 2
    middle = padded[1:-1, 1:-1, 1:-1]
    cross_sv = 0.0
    cross_sr = 0.0
    cross_vr = 0.0
    for outer_step in range(3):
        for inner_step in range(3):
            cross_sv = (
                cross_sv
                + spot_first[outer_step]
                * var_first[inner_step]
                * padded[
                    outer_step : outer_step + spot_rows, 1:-1, inner_step : inner_step + var_cols
                ]
            )
            cross_sr = (
                cross_sr
                + spot_first[outer_step]
                * rate_first[inner_step]
                * padded[
                    outer_step : outer_step + spot_rows, inner_step : inner_step + planes, 1:-1
                ]
            )
            cross_vr = (
                cross_vr
                + var_first[outer_step]
                * rate_first[inner_step]
                * padded[1:-1, inner_step : inner_step + planes, outer_step : outer_step + var_cols]
            )
    root_var = jnp.sqrt(var_x)
    mixing = (
        coupling_sv * spot_x * var_x * cross_sv
        + coupling_sr * spot_x * root_var * cross_sr
        + coupling_vr * root_var * cross_vr
    )
    if mixing_only:
        return mixing
    reaction = rate_x / 3.0
    diffusion, advection = spot_terms(spot_x, var_x, rate_x)
    behind, centre, ahead = line_coefficients(
        diffusion, advection, reaction, spot_first, spot_second
    )
    along_spot = behind * padded[:-2, 1:-1, 1:-1] + centre * middle + ahead * padded[2:, 1:-1, 1:-1]
    diffusion, advection = var_terms(var_x)
    behind, centre, ahead = line_coefficients(diffusion, advection, reaction, var_first, var_second)
    along_var = behind * padded[1:-1, 1:-1, :-2] + centre * middle + ahead * padded[1:-1, 1:-1, 2:]
    diffusion, advection = rate_terms(rate_x)
    behind, centre, ahead = line_coefficients(
        diffusion, advection, reaction, rate_first, rate_second
    )
    along_rate = behind * padded[1:-1, :-2, 1:-1] + centre * middle + ahead * padded[1:-1, 2:, 1:-1]
    return mixing + along_spot + along_var + along_rate


def reduce_solve(lower_band, main_band, upper_band, right_side, dimension):
    length = right_side.shape[dimension]
    if length == 1:
        return right_side / main_band

    def even_rows(source):
        return lax.slice_in_dim(source, 0, length, 2, dimension)

    def odd_rows(source):
        return lax.slice_in_dim(source, 1, length, 2, dimension)

    def onward(source, filler):
        remainder = lax.slice_in_dim(source, 1, source.shape[dimension], axis=dimension)
        return jnp.concatenate(
            [remainder, jnp.zeros_like(lax.slice_in_dim(source, 0, 1, axis=dimension)) + filler],
            axis=dimension,
        )

    lower_even, main_even, upper_even, right_even = [
        even_rows(source) for source in (lower_band, main_band, upper_band, right_side)
    ]
    lower_odd, main_odd, upper_odd, right_odd = [
        odd_rows(source) for source in (lower_band, main_band, upper_band, right_side)
    ]
    lower_next = onward(lower_even, 0.0)
    main_next = onward(main_even, 1.0)
    upper_next = onward(upper_even, 0.0)
    right_next = onward(right_even, 0.0)
    ratio_back = -lower_odd / main_even
    ratio_ahead = -upper_odd / main_next
    solved_odd = reduce_solve(
        ratio_back * lower_even,
        main_odd + ratio_back * upper_even + ratio_ahead * lower_next,
        ratio_ahead * upper_next,
        right_odd + ratio_back * right_even + ratio_ahead * right_next,
        dimension,
    )
    remainder = lax.slice_in_dim(solved_odd, 0, solved_odd.shape[dimension] - 1, axis=dimension)
    solved_even = (
        right_even
        - lower_even
        * jnp.concatenate(
            [jnp.zeros_like(lax.slice_in_dim(solved_odd, 0, 1, axis=dimension)), remainder],
            axis=dimension,
        )
        - upper_even * solved_odd
    ) / main_even
    joined = jnp.stack([solved_even, solved_odd], axis=dimension + 1)
    return joined.reshape(right_side.shape)


def cyclic_kernel(lower_ref, main_ref, upper_ref, rhs_ref, out_ref, a_s, b_s, c_s, d_s):
    count, width = rhs_ref.shape
    pad = count // 2
    for ref, fill in ((a_s, 0.0), (b_s, 1.0), (c_s, 0.0), (d_s, 0.0)):
        ref[0:pad, :] = jnp.full((pad, width), fill, jnp.float32)
        ref[pad + count : 2 * pad + count, :] = jnp.full((pad, width), fill, jnp.float32)
    row = lax.broadcasted_iota(jnp.int32, (count, width), 0)
    a_s[pad : pad + count, :] = jnp.where(row == 0, 0.0, lower_ref[...])
    b_s[pad : pad + count, :] = main_ref[...]
    c_s[pad : pad + count, :] = jnp.where(row == count - 1, 0.0, upper_ref[...])
    d_s[pad : pad + count, :] = rhs_ref[...]
    stride = 1
    while stride < count:
        centre = slice(pad, pad + count)
        before = slice(pad - stride, pad - stride + count)
        after = slice(pad + stride, pad + stride + count)
        a, b, c, d = a_s[centre, :], b_s[centre, :], c_s[centre, :], d_s[centre, :]
        ratio_back = -a / b_s[before, :]
        ratio_ahead = -c / b_s[after, :]
        new_b = b + ratio_back * c_s[before, :] + ratio_ahead * a_s[after, :]
        new_d = d + ratio_back * d_s[before, :] + ratio_ahead * d_s[after, :]
        new_a = ratio_back * a_s[before, :]
        new_c = ratio_ahead * c_s[after, :]
        a_s[centre, :] = new_a
        b_s[centre, :] = new_b
        c_s[centre, :] = new_c
        d_s[centre, :] = new_d
        stride *= 2
    out_ref[...] = d_s[pad : pad + count, :] / b_s[pad : pad + count, :]


def line_solve(lower_band, main_band, upper_band, right_side):
    count, width = right_side.shape
    scratch = pltpu.VMEM((2 * (count // 2) + count, width), jnp.float32)
    return pl.pallas_call(
        cyclic_kernel,
        out_shape=jax.ShapeDtypeStruct((count, width), jnp.float32),
        scratch_shapes=[scratch] * 4,
    )(lower_band, main_band, upper_band, right_side)


def implicit(system, right_side, dimension):
    behind, centre, ahead = system
    lower_band = jnp.broadcast_to(-solve_scale * behind, right_side.shape)
    main_band = jnp.broadcast_to(1.0 - solve_scale * centre, right_side.shape)
    upper_band = jnp.broadcast_to(-solve_scale * ahead, right_side.shape)
    return reduce_solve(lower_band, main_band, upper_band, right_side, dimension)


def shards(option_value, spot_nodes, var_nodes, rate_nodes):
    spot_rows, planes, var_cols = option_value.shape
    line_count = planes * var_cols
    spot_place = lax.axis_index("spot")
    var_place = lax.axis_index("var")
    spot_coords = coordinates(spot_nodes, spot_low, spot_high)
    var_coords = coordinates(var_nodes, var_low, var_high)
    rate_coords = coordinates(rate_nodes, rate_low, rate_high)
    spot_geo = geometry(spot_coords, 0, 3, spot_place * spot_rows, spot_rows)
    var_geo = geometry(var_coords, 2, 3, var_place * var_cols, var_cols)
    rate_geo = geometry(rate_coords, 1, 3, 0, planes)
    spot_whole = geometry(spot_coords, 0, 2, 0, spot_nodes.shape[0])
    var_whole = geometry(var_coords, 1, 2, 0, var_nodes.shape[0])
    rate_plain = rate_geo[0].reshape(planes)
    var_plain = var_geo[0].reshape(var_cols)

    def edge_terms(values, mixing_only):
        padded = padded_2(values, (("spot", 0), ("var", 2)), 1)
        padded = jnp.pad(padded, ((0, 0), (1, 1), (0, 0)))
        return explicit_terms(padded, spot_geo, var_geo, rate_geo, mixing_only)

    def spot_solve(values):
        gathered = lax.all_to_all(
            values.reshape(spot_rows, line_count), "spot", split_axis=1, concat_axis=0, tiled=True
        )
        per_device = gathered.shape[1]
        first_line = spot_place * per_device
        rate_flat = jnp.broadcast_to(rate_plain.reshape(planes, 1), (planes, var_cols)).reshape(
            line_count
        )
        var_flat = jnp.broadcast_to(var_plain.reshape(1, var_cols), (planes, var_cols)).reshape(
            line_count
        )
        rate_line = lax.dynamic_slice_in_dim(rate_flat, first_line, per_device).reshape(
            1, per_device
        )
        var_line = lax.dynamic_slice_in_dim(var_flat, first_line, per_device).reshape(1, per_device)
        diffusion, advection = spot_terms(spot_whole[0], var_line, rate_line)
        system = line_coefficients(
            diffusion, advection, rate_line / 3.0, spot_whole[1], spot_whole[2]
        )
        solved = implicit(system, gathered, 0)
        return lax.all_to_all(solved, "spot", split_axis=0, concat_axis=1, tiled=True).reshape(
            spot_rows, planes, var_cols
        )

    var_count = var_nodes.shape[0]
    blocks = var_count // var_cols
    var_vec = var_coords[1:-1]
    var_first, var_second = stencil_weights(var_coords)
    var_diffusion, var_advection = var_terms(var_vec)
    var_behind = var_diffusion * var_second[0] + var_advection * var_first[0]
    var_middle = var_diffusion * var_second[1] + var_advection * var_first[1]
    var_ahead = var_diffusion * var_second[2] + var_advection * var_first[2]
    reaction_plain = rate_plain / 3.0
    var_lower = (-solve_scale * var_behind).reshape(blocks, var_cols)
    var_upper = (-solve_scale * var_ahead).reshape(blocks, var_cols)
    var_main = (
        1.0 - solve_scale * (var_middle.reshape(var_count, 1) - reaction_plain.reshape(1, planes))
    ).reshape(blocks, var_cols, planes)

    column_shape = (var_cols, blocks, 2, planes)
    lower_cols = jnp.broadcast_to(var_lower.T.reshape(var_cols, blocks, 1, 1), column_shape)
    upper_cols = jnp.broadcast_to(var_upper.T.reshape(var_cols, blocks, 1, 1), column_shape)
    main_cols = jnp.broadcast_to(
        var_main.transpose(1, 0, 2).reshape(var_cols, blocks, 1, planes), column_shape
    )
    position = lax.broadcasted_iota(jnp.int32, column_shape, 0)
    kind = lax.broadcasted_iota(jnp.int32, column_shape, 2)
    coupling = jnp.where(
        (kind == 0) & (position == 0),
        var_lower[:, 0].reshape(1, blocks, 1, 1),
        jnp.where(
            (kind == 1) & (position == var_cols - 1),
            var_upper[:, var_cols - 1].reshape(1, blocks, 1, 1),
            0.0,
        ),
    )
    flat = (var_cols, blocks * 2 * planes)
    columns = line_solve(
        lower_cols.reshape(flat),
        main_cols.reshape(flat),
        upper_cols.reshape(flat),
        coupling.reshape(flat),
    ).reshape(column_shape)
    g_first, g_last = columns[0, :, 0, :], columns[var_cols - 1, :, 0, :]
    h_first, h_last = columns[0, :, 1, :], columns[var_cols - 1, :, 1, :]
    g_own = lax.dynamic_index_in_dim(columns[:, :, 0, :], var_place, 1, keepdims=False)
    h_own = lax.dynamic_index_in_dim(columns[:, :, 1, :], var_place, 1, keepdims=False)
    lower_own = lax.dynamic_index_in_dim(var_lower, var_place, 0, keepdims=False)
    upper_own = lax.dynamic_index_in_dim(var_upper, var_place, 0, keepdims=False)
    main_own = lax.dynamic_index_in_dim(var_main, var_place, 0, keepdims=False)

    def interface_solve(y_first, y_last):
        size = 2 * (blocks - 1)
        matrix = [[None] * size for _ in range(size)]
        rhs = [None] * size
        for b in range(blocks - 1):
            matrix[2 * b][2 * b] = 1.0
            if b >= 1:
                matrix[2 * b][2 * b - 2] = g_last[b]
            matrix[2 * b][2 * b + 1] = h_last[b]
            rhs[2 * b] = y_last[b]
            matrix[2 * b + 1][2 * b + 1] = 1.0
            matrix[2 * b + 1][2 * b] = g_first[b + 1]
            if b + 2 <= blocks - 1:
                matrix[2 * b + 1][2 * b + 3] = h_first[b + 1]
            rhs[2 * b + 1] = y_first[b + 1]
        for k in range(size):
            for i in range(k + 1, size):
                if matrix[i][k] is None:
                    continue
                factor = matrix[i][k] / matrix[k][k]
                for c in range(k + 1, size):
                    if matrix[k][c] is None:
                        continue
                    update = factor * matrix[k][c]
                    matrix[i][c] = -update if matrix[i][c] is None else matrix[i][c] - update
                rhs[i] = rhs[i] - factor * rhs[k]
                matrix[i][k] = None
        solved = [None] * size
        for k in reversed(range(size)):
            total = rhs[k]
            for c in range(k + 1, size):
                if matrix[k][c] is not None:
                    total = total - matrix[k][c] * solved[c]
            solved[k] = total / matrix[k][k]
        zero = jnp.zeros_like(y_first[0])
        left = jnp.stack([zero] + [solved[2 * b] for b in range(blocks - 1)])
        right = jnp.stack([solved[2 * b + 1] for b in range(blocks - 1)] + [zero])
        return (
            lax.dynamic_index_in_dim(left, var_place, 0, keepdims=False),
            lax.dynamic_index_in_dim(right, var_place, 0, keepdims=False),
        )

    def gather_var(ends):
        parts = [ends]
        for shift in range(1, blocks):
            pairs = [(i, (i + shift) % blocks) for i in range(blocks)]
            parts.append(lax.ppermute(ends, "var", pairs))
        stacked = jnp.stack(parts)
        order = (var_place - jnp.arange(blocks)) % blocks
        return jnp.take(stacked, order, axis=0)

    def var_solve(values):
        line_count = spot_rows * planes
        lines = values.transpose(2, 0, 1).reshape(var_cols, line_count)
        shape = lines.shape
        local = line_solve(
            jnp.broadcast_to(lower_own.reshape(var_cols, 1), shape),
            jnp.broadcast_to(main_own.reshape(var_cols, 1, planes), (var_cols, spot_rows, planes)).reshape(shape),
            jnp.broadcast_to(upper_own.reshape(var_cols, 1), shape),
            lines,
        ).reshape(var_cols, spot_rows, planes)
        ends = gather_var(jnp.stack([local[0], local[var_cols - 1]]))
        left, right = interface_solve(ends[:, 0], ends[:, 1])
        solved = (
            local
            - left.reshape(1, spot_rows, planes) * g_own.reshape(var_cols, 1, planes)
            - right.reshape(1, spot_rows, planes) * h_own.reshape(var_cols, 1, planes)
        )
        return solved.transpose(1, 2, 0)

    def rate_solve(values):
        diffusion, advection = rate_terms(rate_geo[0])
        system = line_coefficients(
            diffusion, advection, rate_geo[0] / 3.0, rate_geo[1], rate_geo[2]
        )
        return implicit(system, values, 1)

    z_zero = time_step * edge_terms(option_value, False)
    z_one = spot_solve(z_zero)
    z_two = var_solve(z_one)
    z_three = rate_solve(z_two)
    w_zero = z_zero + half_step * edge_terms(z_three, True)
    w_one = spot_solve(w_zero)
    w_two = var_solve(w_one)
    w_three = rate_solve(w_two)
    return option_value + w_three


def solution(mesh):
    in_specs = (P("spot", None, "var"), P(), P(), P())
    out_specs = P("spot", None, "var")
    return jax.shard_map(shards, mesh=mesh, in_specs=in_specs, out_specs=out_specs, check_vma=False)
```

profile of v0, /device:TPU:1, one launch (start us, length us, event | category | flops | bytes accessed | tf_op | source)
XLA Modules:
  0.0 212.1 jit_solution(2772752880371348287)
XLA Ops:
  0.9 4.5 %collective-permute-start = (f32[1,64,256]{2,1,0:T(8,128)S(1)}, f32[1,64,256]{2,1,0:T(8,128)S(1)}, u32[]{:S(2)}, u32[]{:S(2)}) collective-permute-start(f32[1,64,256]{2,1,0:T(8,128)S(1)} %get-tuple-element.120), channel_id=1, source_target_pairs={{0,4},{4,8},{8,12},{12,16},{16,20},{20,24},{24,28},{28,32},{32,36}... | collective-permute-start | bytes 196616 | tf_op jit(solution)/shard_map/ppermute | solution.py:36
  5.4 5.6 %collective-permute-start.1 = (f32[1,64,256]{2,1,0:T(8,128)S(1)}, f32[1,64,256]{2,1,0:T(8,128)S(1)}, u32[]{:S(2)}, u32[]{:S(2)}) collective-permute-start(f32[1,64,256]{2,1,0:T(8,128)S(1)} %get-tuple-element.119), channel_id=1, source_target_pairs={{4,0},{8,4},{12,8},{16,12},{20,16},{24,20},{28,24},{32,28},{36,32}... | collective-permute-start | bytes 196616 | tf_op jit(solution)/shard_map/ppermute | solution.py:37
  21.4 7.7 %shard_map.47 = f32[256,512]{1,0:T(8,128)} custom-call(f32[256,512]{1,0:T(8,128)} %copy.422.lower_ref, f32[256,512]{1,0:T(8,128)} %copy.423.main_ref, f32[256,512]{1,0:T(8,128)} %copy.424.upper_ref, f32[256,512]{1,0:T(8,128)} %select_select_fusion.rhs_ref), custom_call_target="tpu_custom_call" | custom-call | tf_op jit(solution)/shard_map/pallas_call | solution.py:238
  42.8 1.6 collective-permute-done.2
  44.4 6.4 %collective-permute-done.3 = f32[4,64,1]{2,1,0:T(8,128)S(1)} collective-permute-done((f32[4,64,1]{2,1,0:T(8,128)S(1)}, f32[4,64,1]{2,1,0:T(8,128)S(1)}, u32[]{:S(2)}, u32[]{:S(2)}) %collective-permute-start.3) | collective-permute-done | bytes 1056 | tf_op jit(solution)/shard_map/ppermute | solution.py:37
  52.7 16.5 %all-to-all-start = ((f32[2,128,128]{2,0,1:T(2,128)}), f32[2,128,128]{2,0,1:T(2,128)S(1)}, u32[]{:S(2)}, u32[]{:S(2)}) async-start(f32[2,128,128]{2,0,1:T(2,128)} %copy.404), calls=%async_computation | async-start | bytes 262144 | tf_op jit(solution)/shard_map/all_to_all | solution.py:275
  69.5 10.9 %all-to-all-done = f32[2,128,128]{2,0,1:T(2,128)S(1)} async-done(((f32[2,128,128]{2,0,1:T(2,128)}), f32[2,128,128]{2,0,1:T(2,128)S(1)}, u32[]{:S(2)}, u32[]{:S(2)}) %all-to-all-start) | async-done | bytes 131104 | tf_op jit(solution)/shard_map/all_to_all | solution.py:275
  83.0 5.6 %all-to-all-start.1 = ((f32[128,2,128]{2,1,0:T(2,128)}), f32[128,2,128]{2,1,0:T(2,128)S(1)}, u32[]{:S(2)}, u32[]{:S(2)}) async-start(f32[128,2,128]{2,1,0:T(2,128)} %copy.417), calls=%async_computation.1 | async-start | bytes 262144 | tf_op jit(solution)/shard_map/all_to_all | solution.py:295
  89.4 10.5 %all-to-all-done.1 = f32[128,2,128]{2,1,0:T(2,128)S(1)} async-done(((f32[128,2,128]{2,1,0:T(2,128)}), f32[128,2,128]{2,1,0:T(2,128)S(1)}, u32[]{:S(2)}, u32[]{:S(2)}) %all-to-all-start.1) | async-done | bytes 131104 | tf_op jit(solution)/shard_map/all_to_all | solution.py:295
  102.2 2.6 %shard_map.46 = f32[256,128]{1,0:T(8,128)} custom-call(f32[256,128]{1,0:T(8,128)} %broadcast_in_dim.207.lower_ref, f32[256,128]{1,0:T(8,128)} %copy.472.main_ref, f32[256,128]{1,0:T(8,128)} %broadcast_in_dim.211.upper_ref, f32[256,128]{1,0:T(8,128)} %copy.420.rhs_ref), custom_call_target="tpu_custom_call" | custom-call | tf_op jit(solution)/shard_map/pallas_call | solution.py:238
  105.7 5.5 %collective-permute-start.4 = (f32[2,2,64]{2,1,0:T(2,128)S(1)}, f32[2,2,64]{2,1,0:T(2,128)S(1)}, u32[]{:S(2)}, u32[]{:S(2)}) collective-permute-start(f32[2,2,64]{2,1,0:T(2,128)S(1)} %constant_dynamic-update-slice_fusion.3), channel_id=1, source_target_pairs={{0,1},{1,2},{2,3},{3,0},{4,5},{5,6},{6,7},{7,4},{8,9},{9,10},{10,1... | collective-permute-start | bytes 3080 | tf_op jit(solution)/shard_map/ppermute | solution.py:392
  111.2 1.9 collective-permute-start.5
  113.1 5.2 %collective-permute-start.6 = (f32[2,2,64]{2,1,0:T(2,128)S(1)}, f32[2,2,64]{2,1,0:T(2,128)S(1)}, u32[]{:S(2)}, u32[]{:S(2)}) collective-permute-start(f32[2,2,64]{2,1,0:T(2,128)S(1)} %constant_dynamic-update-slice_fusion.3), channel_id=1, source_target_pairs={{0,3},{1,0},{2,1},{3,2},{4,7},{5,4},{6,5},{7,6},{8,11},{9,8},{10,9... | collective-permute-start | bytes 3080 | tf_op jit(solution)/shard_map/ppermute | solution.py:392
  127.0 3.1 %collective-permute-start.7 = (f32[1,64,256]{2,1,0:T(8,128)S(1)}, f32[1,64,256]{2,1,0:T(8,128)S(1)}, u32[]{:S(2)}, u32[]{:S(2)}) collective-permute-start(f32[1,64,256]{2,1,0:T(8,128)S(1)} %copy.447), channel_id=1, source_target_pairs={{0,4},{4,8},{8,12},{12,16},{16,20},{20,24},{24,28},{28,32},{32,36}... | collective-permute-start | bytes 196616 | tf_op jit(solution)/shard_map/ppermute | solution.py:36
  130.4 1.9 collective-permute-start.8
  132.3 3.6 %collective-permute-done.8 = f32[1,64,256]{2,1,0:T(8,128)S(1)} collective-permute-done((f32[1,64,256]{2,1,0:T(8,128)S(1)}, f32[1,64,256]{2,1,0:T(8,128)S(1)}, u32[]{:S(2)}, u32[]{:S(2)}) %collective-permute-start.8) | collective-permute-done | bytes 65568 | tf_op jit(solution)/shard_map/ppermute | solution.py:37
  137.3 4.9 %collective-permute-start.9 = (f32[4,64,1]{2,1,0:T(8,128)S(1)}, f32[4,64,1]{2,1,0:T(8,128)S(1)}, u32[]{:S(2)}, u32[]{:S(2)}) collective-permute-start(f32[4,64,1]{2,1,0:T(8,128)S(1)} %get-tuple-element.111), channel_id=1, source_target_pairs={{0,1},{1,2},{2,3},{4,5},{5,6},{6,7},{8,9},{9,10},{10,11},{12,13},{... | collective-permute-start | bytes 3080 | tf_op jit(solution)/shard_map/ppermute | solution.py:36
  142.8 1.4 collective-permute-done.9
  145.3 25.5 %all_to_all.64 = f32[2,128,128]{2,0,1:T(2,128)S(1)} all-to-all(f32[2,128,128]{2,0,1:T(2,128)S(1)} %copy.457), channel_id=1, replica_groups=mesh['spot'=128,'var'=4] {'spot'}, dimensions={1} | all-to-all | bytes 262144 | tf_op jit(solution)/shard_map/all_to_all | solution.py:275
  171.8 16.6 %all_to_all.65 = f32[128,2,128]{2,1,0:T(2,128)S(1)} all-to-all(f32[128,2,128]{2,1,0:T(2,128)S(1)} %copy.470), channel_id=1, replica_groups=mesh['spot'=128,'var'=4] {'spot'}, dimensions={0} | all-to-all | bytes 262144 | tf_op jit(solution)/shard_map/all_to_all | solution.py:295
  189.2 2.6 %shard_map.48 = f32[256,128]{1,0:T(8,128)} custom-call(f32[256,128]{1,0:T(8,128)} %broadcast_in_dim.207.lower_ref, f32[256,128]{1,0:T(8,128)} %copy.472.main_ref, f32[256,128]{1,0:T(8,128)} %broadcast_in_dim.211.upper_ref, f32[256,128]{1,0:T(8,128)} %copy.473.rhs_ref), custom_call_target="tpu_custom_call" | custom-call | tf_op jit(solution)/shard_map/pallas_call | solution.py:238
  192.8 4.7 %collective-permute-start.11 = (f32[2,2,64]{2,1,0:T(2,128)S(1)}, f32[2,2,64]{2,1,0:T(2,128)S(1)}, u32[]{:S(2)}, u32[]{:S(2)}) collective-permute-start(f32[2,2,64]{2,1,0:T(2,128)S(1)} %constant_dynamic-update-slice_fusion.8), channel_id=1, source_target_pairs={{0,1},{1,2},{2,3},{3,0},{4,5},{5,6},{6,7},{7,4},{8,9},{9,10},{10,1... | collective-permute-start | bytes 3080 | tf_op jit(solution)/shard_map/ppermute | solution.py:392
  197.4 4.9 %collective-permute-start.12 = (f32[2,2,64]{2,1,0:T(2,128)S(1)}, f32[2,2,64]{2,1,0:T(2,128)S(1)}, u32[]{:S(2)}, u32[]{:S(2)}) collective-permute-start(f32[2,2,64]{2,1,0:T(2,128)S(1)} %constant_dynamic-update-slice_fusion.8), channel_id=1, source_target_pairs={{0,2},{1,3},{2,0},{3,1},{4,6},{5,7},{6,4},{7,5},{8,10},{9,11},{10,... | collective-permute-start | bytes 3080 | tf_op jit(solution)/shard_map/ppermute | solution.py:392
  202.4 4.3 %collective-permute-start.13 = (f32[2,2,64]{2,1,0:T(2,128)S(1)}, f32[2,2,64]{2,1,0:T(2,128)S(1)}, u32[]{:S(2)}, u32[]{:S(2)}) collective-permute-start(f32[2,2,64]{2,1,0:T(2,128)S(1)} %constant_dynamic-update-slice_fusion.8), channel_id=1, source_target_pairs={{0,3},{1,0},{2,1},{3,2},{4,7},{5,4},{6,5},{7,6},{8,11},{9,8},{10,9... | collective-permute-start | bytes 3080 | tf_op jit(solution)/shard_map/ppermute | solution.py:392
  (493 shorter events, 48.0 us)
Async XLA Ops:
  0.9 10.1 %copy-start.3 = (s32[64]{0:T(128)S(1)}, s32[64]{0:T(128)}, u32[]{:S(2)}) copy-start(s32[64]{0:T(128)} %param.9) | copy-start | bytes 772
  0.9 38.4 %collective-permute-start = (f32[1,64,256]{2,1,0:T(8,128)S(1)}, f32[1,64,256]{2,1,0:T(8,128)S(1)}, u32[]{:S(2)}, u32[]{:S(2)}) collective-permute-start(f32[1,64,256]{2,1,0:T(8,128)S(1)} %get-tuple-element.120), channel_id=1, source_target_pairs={{0,4},{4,8},{8,12},{12,16},{16,20},{20,24},{24,28},{28,32},{32,36}... | collective-permute-start | bytes 196616 | tf_op jit(solution)/shard_map/ppermute | solution.py:36
  5.4 34.7 %collective-permute-start.1 = (f32[1,64,256]{2,1,0:T(8,128)S(1)}, f32[1,64,256]{2,1,0:T(8,128)S(1)}, u32[]{:S(2)}, u32[]{:S(2)}) collective-permute-start(f32[1,64,256]{2,1,0:T(8,128)S(1)} %get-tuple-element.119), channel_id=1, source_target_pairs={{4,0},{8,4},{12,8},{16,12},{20,16},{24,20},{28,24},{32,28},{36,32}... | collective-permute-start | bytes 196616 | tf_op jit(solution)/shard_map/ppermute | solution.py:37
  15.4 0.7 copy-start.1
  36.5 0.7 copy-start.2
  39.2 0.9 copy-start
  40.2 4.2 %collective-permute-start.2 = (f32[4,64,1]{2,1,0:T(8,128)S(1)}, f32[4,64,1]{2,1,0:T(8,128)S(1)}, u32[]{:S(2)}, u32[]{:S(2)}) collective-permute-start(f32[4,64,1]{2,1,0:T(8,128)S(1)} %get-tuple-element.113), channel_id=1, source_target_pairs={{0,1},{1,2},{2,3},{4,5},{5,6},{6,7},{8,9},{9,10},{10,11},{12,13},{... | collective-permute-start | bytes 3080 | tf_op jit(solution)/shard_map/ppermute | solution.py:36
  41.5 9.3 %collective-permute-start.3 = (f32[4,64,1]{2,1,0:T(8,128)S(1)}, f32[4,64,1]{2,1,0:T(8,128)S(1)}, u32[]{:S(2)}, u32[]{:S(2)}) collective-permute-start(f32[4,64,1]{2,1,0:T(8,128)S(1)} %get-tuple-element.114), channel_id=1, source_target_pairs={{1,0},{2,1},{3,2},{5,4},{6,5},{7,6},{9,8},{10,9},{11,10},{13,12},{... | collective-permute-start | bytes 3080 | tf_op jit(solution)/shard_map/ppermute | solution.py:37
  52.7 27.7 %all-to-all-start = ((f32[2,128,128]{2,0,1:T(2,128)}), f32[2,128,128]{2,0,1:T(2,128)S(1)}, u32[]{:S(2)}, u32[]{:S(2)}) async-start(f32[2,128,128]{2,0,1:T(2,128)} %copy.404), calls=%async_computation | async-start | bytes 262144 | tf_op jit(solution)/shard_map/all_to_all | solution.py:275
  83.0 16.9 %all-to-all-start.1 = ((f32[128,2,128]{2,1,0:T(2,128)}), f32[128,2,128]{2,1,0:T(2,128)S(1)}, u32[]{:S(2)}, u32[]{:S(2)}) async-start(f32[128,2,128]{2,1,0:T(2,128)} %copy.417), calls=%async_computation.1 | async-start | bytes 262144 | tf_op jit(solution)/shard_map/all_to_all | solution.py:295
  105.7 17.6 %collective-permute-start.4 = (f32[2,2,64]{2,1,0:T(2,128)S(1)}, f32[2,2,64]{2,1,0:T(2,128)S(1)}, u32[]{:S(2)}, u32[]{:S(2)}) collective-permute-start(f32[2,2,64]{2,1,0:T(2,128)S(1)} %constant_dynamic-update-slice_fusion.3), channel_id=1, source_target_pairs={{0,1},{1,2},{2,3},{3,0},{4,5},{5,6},{6,7},{7,4},{8,9},{9,10},{10,1... | collective-permute-start | bytes 3080 | tf_op jit(solution)/shard_map/ppermute | solution.py:392
  111.2 12.1 %collective-permute-start.5 = (f32[2,2,64]{2,1,0:T(2,128)S(1)}, f32[2,2,64]{2,1,0:T(2,128)S(1)}, u32[]{:S(2)}, u32[]{:S(2)}) collective-permute-start(f32[2,2,64]{2,1,0:T(2,128)S(1)} %constant_dynamic-update-slice_fusion.3), channel_id=1, source_target_pairs={{0,2},{1,3},{2,0},{3,1},{4,6},{5,7},{6,4},{7,5},{8,10},{9,11},{10,... | collective-permute-start | bytes 3080 | tf_op jit(solution)/shard_map/ppermute | solution.py:392
  113.1 10.2 %collective-permute-start.6 = (f32[2,2,64]{2,1,0:T(2,128)S(1)}, f32[2,2,64]{2,1,0:T(2,128)S(1)}, u32[]{:S(2)}, u32[]{:S(2)}) collective-permute-start(f32[2,2,64]{2,1,0:T(2,128)S(1)} %constant_dynamic-update-slice_fusion.3), channel_id=1, source_target_pairs={{0,3},{1,0},{2,1},{3,2},{4,7},{5,4},{6,5},{7,6},{8,11},{9,8},{10,9... | collective-permute-start | bytes 3080 | tf_op jit(solution)/shard_map/ppermute | solution.py:392
  127.0 5.3 %collective-permute-start.7 = (f32[1,64,256]{2,1,0:T(8,128)S(1)}, f32[1,64,256]{2,1,0:T(8,128)S(1)}, u32[]{:S(2)}, u32[]{:S(2)}) collective-permute-start(f32[1,64,256]{2,1,0:T(8,128)S(1)} %copy.447), channel_id=1, source_target_pairs={{0,4},{4,8},{8,12},{12,16},{16,20},{20,24},{24,28},{28,32},{32,36}... | collective-permute-start | bytes 196616 | tf_op jit(solution)/shard_map/ppermute | solution.py:36
  130.4 5.6 %collective-permute-start.8 = (f32[1,64,256]{2,1,0:T(8,128)S(1)}, f32[1,64,256]{2,1,0:T(8,128)S(1)}, u32[]{:S(2)}, u32[]{:S(2)}) collective-permute-start(f32[1,64,256]{2,1,0:T(8,128)S(1)} %copy.450), channel_id=1, source_target_pairs={{4,0},{8,4},{12,8},{16,12},{20,16},{24,20},{28,24},{32,28},{36,32}... | collective-permute-start | bytes 196616 | tf_op jit(solution)/shard_map/ppermute | solution.py:37
  136.0 6.7 %collective-permute-start.10 = (f32[4,64,1]{2,1,0:T(8,128)S(1)}, f32[4,64,1]{2,1,0:T(8,128)S(1)}, u32[]{:S(2)}, u32[]{:S(2)}) collective-permute-start(f32[4,64,1]{2,1,0:T(8,128)S(1)} %get-tuple-element.112), channel_id=1, source_target_pairs={{1,0},{2,1},{3,2},{5,4},{6,5},{7,6},{9,8},{10,9},{11,10},{13,12},{... | collective-permute-start | bytes 3080 | tf_op jit(solution)/shard_map/ppermute | solution.py:37
  137.3 6.8 %collective-permute-start.9 = (f32[4,64,1]{2,1,0:T(8,128)S(1)}, f32[4,64,1]{2,1,0:T(8,128)S(1)}, u32[]{:S(2)}, u32[]{:S(2)}) collective-permute-start(f32[4,64,1]{2,1,0:T(8,128)S(1)} %get-tuple-element.111), channel_id=1, source_target_pairs={{0,1},{1,2},{2,3},{4,5},{5,6},{6,7},{8,9},{9,10},{10,11},{12,13},{... | collective-permute-start | bytes 3080 | tf_op jit(solution)/shard_map/ppermute | solution.py:36
  192.8 15.0 %collective-permute-start.11 = (f32[2,2,64]{2,1,0:T(2,128)S(1)}, f32[2,2,64]{2,1,0:T(2,128)S(1)}, u32[]{:S(2)}, u32[]{:S(2)}) collective-permute-start(f32[2,2,64]{2,1,0:T(2,128)S(1)} %constant_dynamic-update-slice_fusion.8), channel_id=1, source_target_pairs={{0,1},{1,2},{2,3},{3,0},{4,5},{5,6},{6,7},{7,4},{8,9},{9,10},{10,1... | collective-permute-start | bytes 3080 | tf_op jit(solution)/shard_map/ppermute | solution.py:392
  197.4 10.3 %collective-permute-start.12 = (f32[2,2,64]{2,1,0:T(2,128)S(1)}, f32[2,2,64]{2,1,0:T(2,128)S(1)}, u32[]{:S(2)}, u32[]{:S(2)}) collective-permute-start(f32[2,2,64]{2,1,0:T(2,128)S(1)} %constant_dynamic-update-slice_fusion.8), channel_id=1, source_target_pairs={{0,2},{1,3},{2,0},{3,1},{4,6},{5,7},{6,4},{7,5},{8,10},{9,11},{10,... | collective-permute-start | bytes 3080 | tf_op jit(solution)/shard_map/ppermute | solution.py:392
  202.4 5.4 %collective-permute-start.13 = (f32[2,2,64]{2,1,0:T(2,128)S(1)}, f32[2,2,64]{2,1,0:T(2,128)S(1)}, u32[]{:S(2)}, u32[]{:S(2)}) collective-permute-start(f32[2,2,64]{2,1,0:T(2,128)S(1)} %constant_dynamic-update-slice_fusion.8), channel_id=1, source_target_pairs={{0,3},{1,0},{2,1},{3,2},{4,7},{5,4},{6,5},{7,6},{8,11},{9,8},{10,9... | collective-permute-start | bytes 3080 | tf_op jit(solution)/shard_map/ppermute | solution.py:392
where the time goes:
time: 214 us; the launch traced here: 212 us
  starting transfers between devices  72.5 us (34%)
  blocking collectives  42.1 us (20%)
  waiting for transfers between devices  34.8 us (16%)
  local copies, waits for them, and re-layouts  30.5 us (14%)
  other arithmetic  13.2 us (6%)
  Pallas kernels  13 us (6%)
  between operations  6.02 us (3%)
    ppermute x6, starting transfers between devices, gather_var(): parts.append(lax.ppermute(ends, 'var', pairs))  26.5 us
    all_to_all x1, blocking collectives, spot_solve(): lax.all_to_all(values.reshape(spot_rows, line_count), 'spot', split_axis=...  25.5 us
    all_to_all x1, blocking collectives, spot_solve(): lax.all_to_all(solved, 'spot', split_axis=0, concat_axis=1, tiled=True)  16.6 us
    all_to_all x1, starting transfers between devices, spot_solve(): lax.all_to_all(values.reshape(spot_rows, line_count), 'spot', split_axis=...  16.5 us
    ppermute x4, starting transfers between devices, padded_2(): before = lax.ppermute(last, axis, up)  13.8 us
    pallas_call x3, Pallas kernels, line_solve(): pl.pallas_call(cyclic_kernel, out_shape=jax.ShapeDtypeStruct((count, widt...  13 us
    all_to_all x1, waiting for transfers between devices, spot_solve(): lax.all_to_all(values.reshape(spot_rows, line_count), 'spot', split_axis=...  10.9 us
    ppermute x4, waiting for transfers between devices, padded_2(): after = lax.ppermute(initial, axis, down)  10.5 us
  transfers between devices with their start and end apart: 16, of which 7 were waited for; matrix products, arithmetic and copies ran while one was open for 10% of the time, Pallas kernels for 4%

commit v1 on v0

--- a/solution.py
+++ b/solution.py
@@ -1,3 +1,5 @@
+import functools
+
 import jax
 import jax.numpy as jnp
 from jax import lax
@@ -242,6 +244,47 @@
     )(lower_band, main_band, upper_band, right_side)
 
 
+def gather_kernel(blocks, ends_ref, out_ref, landed, send_sem, recv_sem):
+    me = lax.axis_index("var")
+    spot = lax.axis_index("spot")
+    barrier = pltpu.get_barrier_semaphore()
+    for shift in range(1, blocks):
+        peer = lax.rem(me + shift, blocks)
+        pl.semaphore_signal(barrier, inc=1, device_id=(spot, peer), device_id_type=pl.DeviceIdType.MESH)
+    pl.semaphore_wait(barrier, blocks - 1)
+    copies = []
+    for shift in range(1, blocks):
+        peer = lax.rem(me + shift, blocks)
+        copy = pltpu.make_async_remote_copy(
+            src_ref=ends_ref,
+            dst_ref=landed.at[shift - 1],
+            send_sem=send_sem.at[shift - 1],
+            recv_sem=recv_sem.at[shift - 1],
+            device_id=(spot, peer),
+            device_id_type=pl.DeviceIdType.MESH,
+        )
+        copy.start()
+        copies.append(copy)
+    out_ref[0] = ends_ref[...]
+    for copy in copies:
+        copy.wait()
+    for shift in range(1, blocks):
+        out_ref[shift] = landed[shift - 1]
+
+
+def gather_var(ends, blocks):
+    return pl.pallas_call(
+        functools.partial(gather_kernel, blocks),
+        out_shape=jax.ShapeDtypeStruct((blocks,) + ends.shape, jnp.float32),
+        scratch_shapes=[
+            pltpu.VMEM((blocks - 1,) + ends.shape, jnp.float32),
+            pltpu.SemaphoreType.DMA((blocks - 1,)),
+            pltpu.SemaphoreType.DMA((blocks - 1,)),
+        ],
+        compiler_params=pltpu.CompilerParams(collective_id=0, has_side_effects=True),
+    )(ends)
+
+
 def implicit(system, right_side, dimension):
     behind, centre, ahead = system
     lower_band = jnp.broadcast_to(-solve_scale * behind, right_side.shape)
@@ -385,12 +428,8 @@
             lax.dynamic_index_in_dim(right, var_place, 0, keepdims=False),
         )
 
-    def gather_var(ends):
-        parts = [ends]
-        for shift in range(1, blocks):
-            pairs = [(i, (i + shift) % blocks) for i in range(blocks)]
-            parts.append(lax.ppermute(ends, "var", pairs))
-        stacked = jnp.stack(parts)
+    def gather_ends(ends):
+        stacked = gather_var(ends, blocks)
         order = (var_place - jnp.arange(blocks)) % blocks
         return jnp.take(stacked, order, axis=0)
 
@@ -404,7 +443,7 @@
             jnp.broadcast_to(upper_own.reshape(var_cols, 1), shape),
             lines,
         ).reshape(var_cols, spot_rows, planes)
-        ends = gather_var(jnp.stack([local[0], local[var_cols - 1]]))
+        ends = gather_ends(jnp.stack([local[0], local[var_cols - 1]]))
         left, right = interface_solve(ends[:, 0], ends[:, 1])
         solved = (
             local

time: 214 us -> 204 us (0.953)
  starting transfers between devices: 72.5 us -> 45.7 us
  Pallas kernels: 13 us -> 31.3 us
    ppermute x6 -> x0, starting transfers between devices: 26.5 us -> none  [gather_var(): parts.append(lax.ppermute(ends, 'var', pairs))]
    pallas_call x0 -> x2, Pallas kernels: none -> 18.3 us  [gather_var(): pl.pallas_call(functools.partial(gather_kernel, blocks), out_shape=jax.Sh...]
    ppermute x4, waiting for transfers between devices: 10.5 us -> 14.8 us  [padded_2(): after = lax.ppermute(initial, axis, down)]
    all_to_all x1, waiting for transfers between devices: 10.5 us -> 6.78 us  [spot_solve(): lax.all_to_all(solved, 'spot', split_axis=0, concat_axis=1, tiled=True)]
  transfers between devices with their start and end apart: 16 -> 10, of which waited for: 7 -> 7; matrix products, arithmetic and copies ran while one was open for 10% -> 10% of each run, Pallas kernels for 4% -> 4%
where the time goes in v1:
time: 204 us; the launch traced here: 203 us
  starting transfers between devices  45.7 us (22%)
  blocking collectives  40.1 us (20%)
  waiting for transfers between devices  34.7 us (17%)
  local copies, waits for them, and re-layouts  31.6 us (15%)
  Pallas kernels  31.3 us (15%)
  other arithmetic  14.2 us (7%)
  between operations  5.67 us (3%)
    all_to_all x1, blocking collectives, spot_solve(): lax.all_to_all(values.reshape(spot_rows, line_count), 'spot', split_axis=...  23.5 us
    pallas_call x2, Pallas kernels, gather_var(): pl.pallas_call(functools.partial(gather_kernel, blocks), out_shape=jax.Sh...  18.3 us
    all_to_all x1, blocking collectives, spot_solve(): lax.all_to_all(solved, 'spot', split_axis=0, concat_axis=1, tiled=True)  16.6 us
    all_to_all x1, starting transfers between devices, spot_solve(): lax.all_to_all(values.reshape(spot_rows, line_count), 'spot', split_axis=...  16.5 us
    ppermute x4, waiting for transfers between devices, padded_2(): after = lax.ppermute(initial, axis, down)  14.8 us
    ppermute x4, starting transfers between devices, padded_2(): before = lax.ppermute(last, axis, up)  13.5 us
    pallas_call x3, Pallas kernels, line_solve(): pl.pallas_call(cyclic_kernel, out_shape=jax.ShapeDtypeStruct((count, widt...  13 us
    all_to_all x1, waiting for transfers between devices, spot_solve(): lax.all_to_all(values.reshape(spot_rows, line_count), 'spot', split_axis=...  10.9 us
  transfers between devices with their start and end apart: 10, of which 7 were waited for; matrix products, arithmetic and copies ran while one was open for 10% of the time, Pallas kernels for 4%

profile of v1, /device:TPU:1, one launch (start us, length us, event | category | flops | bytes accessed | tf_op | source)
XLA Modules:
  0.0 203.2 jit_solution(17131773699222354780)
XLA Ops:
  0.9 4.5 %collective-permute-start = (f32[1,64,256]{2,1,0:T(8,128)S(1)}, f32[1,64,256]{2,1,0:T(8,128)S(1)}, u32[]{:S(2)}, u32[]{:S(2)}) collective-permute-start(f32[1,64,256]{2,1,0:T(8,128)S(1)} %get-tuple-element.120), channel_id=1, source_target_pairs={{0,4},{4,8},{8,12},{12,16},{16,20},{20,24},{24,28},{28,32},{32,36}... | collective-permute-start | bytes 196616 | tf_op jit(solution)/shard_map/ppermute | solution.py:38
  5.4 5.6 %collective-permute-start.1 = (f32[1,64,256]{2,1,0:T(8,128)S(1)}, f32[1,64,256]{2,1,0:T(8,128)S(1)}, u32[]{:S(2)}, u32[]{:S(2)}) collective-permute-start(f32[1,64,256]{2,1,0:T(8,128)S(1)} %get-tuple-element.119), channel_id=1, source_target_pairs={{4,0},{8,4},{12,8},{16,12},{20,16},{24,20},{28,24},{32,28},{36,32}... | collective-permute-start | bytes 196616 | tf_op jit(solution)/shard_map/ppermute | solution.py:39
  21.4 7.7 %shard_map.48 = f32[256,512]{1,0:T(8,128)} custom-call(f32[256,512]{1,0:T(8,128)} %copy.422.lower_ref, f32[256,512]{1,0:T(8,128)} %copy.423.main_ref, f32[256,512]{1,0:T(8,128)} %copy.424.upper_ref, f32[256,512]{1,0:T(8,128)} %select_select_fusion.rhs_ref), custom_call_target="tpu_custom_call" | custom-call | tf_op jit(solution)/shard_map/pallas_call | solution.py:240
  39.9 1.3 collective-permute-start.2
  41.2 1.3 collective-permute-start.3
  42.5 1.6 collective-permute-done.2
  44.1 6.4 %collective-permute-done.3 = f32[4,64,1]{2,1,0:T(8,128)S(1)} collective-permute-done((f32[4,64,1]{2,1,0:T(8,128)S(1)}, f32[4,64,1]{2,1,0:T(8,128)S(1)}, u32[]{:S(2)}, u32[]{:S(2)}) %collective-permute-start.3) | collective-permute-done | bytes 1056 | tf_op jit(solution)/shard_map/ppermute | solution.py:39
  52.4 16.5 %all-to-all-start = ((f32[2,128,128]{2,0,1:T(2,128)}), f32[2,128,128]{2,0,1:T(2,128)S(1)}, u32[]{:S(2)}, u32[]{:S(2)}) async-start(f32[2,128,128]{2,0,1:T(2,128)} %copy.404), calls=%async_computation | async-start | bytes 262144 | tf_op jit(solution)/shard_map/all_to_all | solution.py:318
  69.2 10.9 %all-to-all-done = f32[2,128,128]{2,0,1:T(2,128)S(1)} async-done(((f32[2,128,128]{2,0,1:T(2,128)}), f32[2,128,128]{2,0,1:T(2,128)S(1)}, u32[]{:S(2)}, u32[]{:S(2)}) %all-to-all-start) | async-done | bytes 131104 | tf_op jit(solution)/shard_map/all_to_all | solution.py:318
  82.7 5.6 %all-to-all-start.1 = ((f32[128,2,128]{2,1,0:T(2,128)}), f32[128,2,128]{2,1,0:T(2,128)S(1)}, u32[]{:S(2)}, u32[]{:S(2)}) async-start(f32[128,2,128]{2,1,0:T(2,128)} %copy.417), calls=%async_computation.1 | async-start | bytes 262144 | tf_op jit(solution)/shard_map/all_to_all | solution.py:338
  92.8 6.8 %all-to-all-done.1 = f32[128,2,128]{2,1,0:T(2,128)S(1)} async-done(((f32[128,2,128]{2,1,0:T(2,128)}), f32[128,2,128]{2,1,0:T(2,128)S(1)}, u32[]{:S(2)}, u32[]{:S(2)}) %all-to-all-start.1) | async-done | bytes 131104 | tf_op jit(solution)/shard_map/all_to_all | solution.py:338
  101.9 2.6 %shard_map.46 = f32[256,128]{1,0:T(8,128)} custom-call(f32[256,128]{1,0:T(8,128)} %broadcast_in_dim.207.lower_ref, f32[256,128]{1,0:T(8,128)} %copy.472.main_ref, f32[256,128]{1,0:T(8,128)} %broadcast_in_dim.211.upper_ref, f32[256,128]{1,0:T(8,128)} %copy.420.rhs_ref), custom_call_target="tpu_custom_call" | custom-call | tf_op jit(solution)/shard_map/pallas_call | solution.py:240
  107.0 9.9 %shard_map.47 = f32[4,2,2,64]{3,2,1,0:T(2,128)} custom-call(f32[2,2,64]{2,1,0:T(2,128)} %pad_maximum_fusion.33.ends_ref), custom_call_target="tpu_custom_call" | custom-call | tf_op jit(solution)/shard_map/pallas_call | solution.py:276
  116.8 1.3 gather_fusion
  121.2 3.7 %collective-permute-start.4 = (f32[1,64,256]{2,1,0:T(8,128)S(1)}, f32[1,64,256]{2,1,0:T(8,128)S(1)}, u32[]{:S(2)}, u32[]{:S(2)}) collective-permute-start(f32[1,64,256]{2,1,0:T(8,128)S(1)} %copy.447), channel_id=1, source_target_pairs={{0,4},{4,8},{8,12},{12,16},{16,20},{20,24},{24,28},{28,32},{32,36}... | collective-permute-start | bytes 196616 | tf_op jit(solution)/shard_map/ppermute | solution.py:38
  125.2 1.9 collective-permute-start.5
  127.1 3.6 %collective-permute-done.5 = f32[1,64,256]{2,1,0:T(8,128)S(1)} collective-permute-done((f32[1,64,256]{2,1,0:T(8,128)S(1)}, f32[1,64,256]{2,1,0:T(8,128)S(1)}, u32[]{:S(2)}, u32[]{:S(2)}) %collective-permute-start.5) | collective-permute-done | bytes 65568 | tf_op jit(solution)/shard_map/ppermute | solution.py:39
  130.9 4.0 %collective-permute-start.6 = (f32[4,64,1]{2,1,0:T(8,128)S(1)}, f32[4,64,1]{2,1,0:T(8,128)S(1)}, u32[]{:S(2)}, u32[]{:S(2)}) collective-permute-start(f32[4,64,1]{2,1,0:T(8,128)S(1)} %get-tuple-element.111), channel_id=1, source_target_pairs={{0,1},{1,2},{2,3},{4,5},{5,6},{6,7},{8,9},{9,10},{10,11},{12,13},{... | collective-permute-start | bytes 3080 | tf_op jit(solution)/shard_map/ppermute | solution.py:38
  134.8 1.3 collective-permute-start.7
  136.8 4.8 %collective-permute-done.7 = f32[4,64,1]{2,1,0:T(8,128)S(1)} collective-permute-done((f32[4,64,1]{2,1,0:T(8,128)S(1)}, f32[4,64,1]{2,1,0:T(8,128)S(1)}, u32[]{:S(2)}, u32[]{:S(2)}) %collective-permute-start.7) | collective-permute-done | bytes 1056 | tf_op jit(solution)/shard_map/ppermute | solution.py:39
  142.8 23.5 %all_to_all.64 = f32[2,128,128]{2,0,1:T(2,128)S(1)} all-to-all(f32[2,128,128]{2,0,1:T(2,128)S(1)} %copy.457), channel_id=1, replica_groups=mesh['spot'=128,'var'=4] {'spot'}, dimensions={1} | all-to-all | bytes 262144 | tf_op jit(solution)/shard_map/all_to_all | solution.py:318
  167.3 16.6 %all_to_all.65 = f32[128,2,128]{2,1,0:T(2,128)S(1)} all-to-all(f32[128,2,128]{2,1,0:T(2,128)S(1)} %copy.470), channel_id=1, replica_groups=mesh['spot'=128,'var'=4] {'spot'}, dimensions={0} | all-to-all | bytes 262144 | tf_op jit(solution)/shard_map/all_to_all | solution.py:338
  184.7 2.6 %shard_map.49 = f32[256,128]{1,0:T(8,128)} custom-call(f32[256,128]{1,0:T(8,128)} %broadcast_in_dim.207.lower_ref, f32[256,128]{1,0:T(8,128)} %copy.472.main_ref, f32[256,128]{1,0:T(8,128)} %broadcast_in_dim.211.upper_ref, f32[256,128]{1,0:T(8,128)} %copy.473.rhs_ref), custom_call_target="tpu_custom_call" | custom-call | tf_op jit(solution)/shard_map/pallas_call | solution.py:240
  189.8 8.4 %shard_map.50 = f32[4,2,2,64]{3,2,1,0:T(2,128)} custom-call(f32[2,2,64]{2,1,0:T(2,128)} %pad_maximum_fusion.35.ends_ref), custom_call_target="tpu_custom_call" | custom-call | tf_op jit(solution)/shard_map/pallas_call | solution.py:276
  (479 shorter events, 45.2 us)
Async XLA Ops:
  0.9 10.1 %copy-start.3 = (s32[64]{0:T(128)S(1)}, s32[64]{0:T(128)}, u32[]{:S(2)}) copy-start(s32[64]{0:T(128)} %param.9) | copy-start | bytes 772
  0.9 38.0 %collective-permute-start = (f32[1,64,256]{2,1,0:T(8,128)S(1)}, f32[1,64,256]{2,1,0:T(8,128)S(1)}, u32[]{:S(2)}, u32[]{:S(2)}) collective-permute-start(f32[1,64,256]{2,1,0:T(8,128)S(1)} %get-tuple-element.120), channel_id=1, source_target_pairs={{0,4},{4,8},{8,12},{12,16},{16,20},{20,24},{24,28},{28,32},{32,36}... | collective-permute-start | bytes 196616 | tf_op jit(solution)/shard_map/ppermute | solution.py:38
  5.4 34.3 %collective-permute-start.1 = (f32[1,64,256]{2,1,0:T(8,128)S(1)}, f32[1,64,256]{2,1,0:T(8,128)S(1)}, u32[]{:S(2)}, u32[]{:S(2)}) collective-permute-start(f32[1,64,256]{2,1,0:T(8,128)S(1)} %get-tuple-element.119), channel_id=1, source_target_pairs={{4,0},{8,4},{12,8},{16,12},{20,16},{24,20},{28,24},{32,28},{36,32}... | collective-permute-start | bytes 196616 | tf_op jit(solution)/shard_map/ppermute | solution.py:39
  15.4 0.7 copy-start.1
  36.2 0.7 copy-start.2
  38.8 0.9 copy-start
  39.9 4.2 %collective-permute-start.2 = (f32[4,64,1]{2,1,0:T(8,128)S(1)}, f32[4,64,1]{2,1,0:T(8,128)S(1)}, u32[]{:S(2)}, u32[]{:S(2)}) collective-permute-start(f32[4,64,1]{2,1,0:T(8,128)S(1)} %get-tuple-element.113), channel_id=1, source_target_pairs={{0,1},{1,2},{2,3},{4,5},{5,6},{6,7},{8,9},{9,10},{10,11},{12,13},{... | collective-permute-start | bytes 3080 | tf_op jit(solution)/shard_map/ppermute | solution.py:38
  41.2 9.3 %collective-permute-start.3 = (f32[4,64,1]{2,1,0:T(8,128)S(1)}, f32[4,64,1]{2,1,0:T(8,128)S(1)}, u32[]{:S(2)}, u32[]{:S(2)}) collective-permute-start(f32[4,64,1]{2,1,0:T(8,128)S(1)} %get-tuple-element.114), channel_id=1, source_target_pairs={{1,0},{2,1},{3,2},{5,4},{6,5},{7,6},{9,8},{10,9},{11,10},{13,12},{... | collective-permute-start | bytes 3080 | tf_op jit(solution)/shard_map/ppermute | solution.py:39
  52.4 27.7 %all-to-all-start = ((f32[2,128,128]{2,0,1:T(2,128)}), f32[2,128,128]{2,0,1:T(2,128)S(1)}, u32[]{:S(2)}, u32[]{:S(2)}) async-start(f32[2,128,128]{2,0,1:T(2,128)} %copy.404), calls=%async_computation | async-start | bytes 262144 | tf_op jit(solution)/shard_map/all_to_all | solution.py:318
  82.7 16.9 %all-to-all-start.1 = ((f32[128,2,128]{2,1,0:T(2,128)}), f32[128,2,128]{2,1,0:T(2,128)S(1)}, u32[]{:S(2)}, u32[]{:S(2)}) async-start(f32[128,2,128]{2,1,0:T(2,128)} %copy.417), calls=%async_computation.1 | async-start | bytes 262144 | tf_op jit(solution)/shard_map/all_to_all | solution.py:338
  121.2 5.9 %collective-permute-start.4 = (f32[1,64,256]{2,1,0:T(8,128)S(1)}, f32[1,64,256]{2,1,0:T(8,128)S(1)}, u32[]{:S(2)}, u32[]{:S(2)}) collective-permute-start(f32[1,64,256]{2,1,0:T(8,128)S(1)} %copy.447), channel_id=1, source_target_pairs={{0,4},{4,8},{8,12},{12,16},{16,20},{20,24},{24,28},{28,32},{32,36}... | collective-permute-start | bytes 196616 | tf_op jit(solution)/shard_map/ppermute | solution.py:38
  125.2 5.6 %collective-permute-start.5 = (f32[1,64,256]{2,1,0:T(8,128)S(1)}, f32[1,64,256]{2,1,0:T(8,128)S(1)}, u32[]{:S(2)}, u32[]{:S(2)}) collective-permute-start(f32[1,64,256]{2,1,0:T(8,128)S(1)} %copy.450), channel_id=1, source_target_pairs={{4,0},{8,4},{12,8},{16,12},{20,16},{24,20},{28,24},{32,28},{36,32}... | collective-permute-start | bytes 196616 | tf_op jit(solution)/shard_map/ppermute | solution.py:39
  130.9 5.9 %collective-permute-start.6 = (f32[4,64,1]{2,1,0:T(8,128)S(1)}, f32[4,64,1]{2,1,0:T(8,128)S(1)}, u32[]{:S(2)}, u32[]{:S(2)}) collective-permute-start(f32[4,64,1]{2,1,0:T(8,128)S(1)} %get-tuple-element.111), channel_id=1, source_target_pairs={{0,1},{1,2},{2,3},{4,5},{5,6},{6,7},{8,9},{9,10},{10,11},{12,13},{... | collective-permute-start | bytes 3080 | tf_op jit(solution)/shard_map/ppermute | solution.py:38
  134.8 6.8 %collective-permute-start.7 = (f32[4,64,1]{2,1,0:T(8,128)S(1)}, f32[4,64,1]{2,1,0:T(8,128)S(1)}, u32[]{:S(2)}, u32[]{:S(2)}) collective-permute-start(f32[4,64,1]{2,1,0:T(8,128)S(1)} %get-tuple-element.112), channel_id=1, source_target_pairs={{1,0},{2,1},{3,2},{5,4},{6,5},{7,6},{9,8},{10,9},{11,10},{13,12},{... | collective-permute-start | bytes 3080 | tf_op jit(solution)/shard_map/ppermute | solution.py:39

commit v2 on v1

--- a/solution.py
+++ b/solution.py
@@ -285,6 +285,51 @@
     )(ends)
 
 
+def exchange_kernel(count, chunks_ref, out_ref, landed, send_sem, recv_sem):
+    me = lax.axis_index("spot")
+    var = lax.axis_index("var")
+
+    def send(step, carry):
+        peer = lax.rem(me + step, count)
+        pltpu.make_async_remote_copy(
+            src_ref=chunks_ref.at[peer],
+            dst_ref=landed.at[me],
+            send_sem=send_sem,
+            recv_sem=recv_sem,
+            device_id=(peer, var),
+            device_id_type=pl.DeviceIdType.MESH,
+        ).start()
+        return carry
+
+    lax.fori_loop(1, count, send, 0)
+    landed[me] = chunks_ref[me]
+    every = pltpu.make_async_remote_copy(
+        src_ref=chunks_ref.at[pl.ds(0, count - 1)],
+        dst_ref=landed.at[pl.ds(0, count - 1)],
+        send_sem=send_sem,
+        recv_sem=recv_sem,
+        device_id=(me, var),
+        device_id_type=pl.DeviceIdType.MESH,
+    )
+    every.wait_send()
+    every.wait_recv()
+    out_ref[...] = landed[...]
+
+
+def exchange_spot(chunks):
+    count = chunks.shape[0]
+    return pl.pallas_call(
+        functools.partial(exchange_kernel, count),
+        out_shape=jax.ShapeDtypeStruct(chunks.shape, jnp.float32),
+        scratch_shapes=[
+            pltpu.VMEM(chunks.shape, jnp.float32),
+            pltpu.SemaphoreType.DMA(()),
+            pltpu.SemaphoreType.DMA(()),
+        ],
+        compiler_params=pltpu.CompilerParams(has_side_effects=True),
+    )(chunks)
+
+
 def implicit(system, right_side, dimension):
     behind, centre, ahead = system
     lower_band = jnp.broadcast_to(-solve_scale * behind, right_side.shape)
@@ -315,10 +360,10 @@
         return explicit_terms(padded, spot_geo, var_geo, rate_geo, mixing_only)
 
     def spot_solve(values):
-        gathered = lax.all_to_all(
-            values.reshape(spot_rows, line_count), "spot", split_axis=1, concat_axis=0, tiled=True
-        )
-        per_device = gathered.shape[1]
+        devices = lax.axis_size("spot")
+        per_device = line_count // devices
+        chunks = values.reshape(spot_rows, devices, per_device).transpose(1, 0, 2)
+        gathered = exchange_spot(chunks).reshape(devices * spot_rows, per_device)
         first_line = spot_place * per_device
         rate_flat = jnp.broadcast_to(rate_plain.reshape(planes, 1), (planes, var_cols)).reshape(
             line_count
@@ -335,9 +380,8 @@
             diffusion, advection, rate_line / 3.0, spot_whole[1], spot_whole[2]
         )
         solved = implicit(system, gathered, 0)
-        return lax.all_to_all(solved, "spot", split_axis=0, concat_axis=1, tiled=True).reshape(
-            spot_rows, planes, var_cols
-        )
+        returned = exchange_spot(solved.reshape(devices, spot_rows, per_device))
+        return returned.transpose(1, 0, 2).reshape(spot_rows, planes, var_cols)
 
     var_count = var_nodes.shape[0]
     blocks = var_count // var_cols

time: 204 us -> 235 us (1.15)
  Pallas kernels: 31.3 us -> 138 us
  blocking collectives: 40.1 us -> 0 us
  starting transfers between devices: 45.7 us -> 23.2 us
  waiting for transfers between devices: 34.7 us -> 15.1 us
  local copies, waits for them, and re-layouts: 31.6 us -> 36.1 us
    pallas_call x0 -> x4, Pallas kernels: none -> 107 us  [exchange_spot(): pl.pallas_call(functools.partial(exchange_kernel, count), out_shape=jax.S...]
    all_to_all x2 -> x0, blocking collectives: 40.1 us -> none  [the longest x1 23.5 us: spot_solve(): lax.all_to_all(values.reshape(spot_rows, line_count), 'spot', split_axis=...]
    all_to_all x2 -> x0, starting transfers between devices: 22.1 us -> none  [the longest x1 16.5 us: spot_solve(): lax.all_to_all(values.reshape(spot_rows, line_count), 'spot', split_axis=...]
    all_to_all x2 -> x0, waiting for transfers between devices: 17.6 us -> none  [the longest x1 10.9 us: spot_solve(): lax.all_to_all(values.reshape(spot_rows, line_count), 'spot', split_axis=...]
  transfers between devices with their start and end apart: 10 -> 8, of which waited for: 7 -> 4; matrix products, arithmetic and copies ran while one was open for 10% -> 9% of each run, Pallas kernels for 4% -> 3%
where the time goes in v2:
time: 235 us; the launch traced here: 234 us
  Pallas kernels  138 us (59%)
  local copies, waits for them, and re-layouts  36.1 us (15%)
  starting transfers between devices  23.2 us (10%)
  other arithmetic  15.2 us (6%)
  waiting for transfers between devices  15.1 us (6%)
  between operations  6 us (3%)
    pallas_call x4, Pallas kernels, exchange_spot(): pl.pallas_call(functools.partial(exchange_kernel, count), out_shape=jax.S...  107 us
    pallas_call x2, Pallas kernels, gather_var(): pl.pallas_call(functools.partial(gather_kernel, blocks), out_shape=jax.Sh...  18.7 us
    ppermute x4, waiting for transfers between devices, padded_2(): after = lax.ppermute(initial, axis, down)  14.4 us
    ppermute x4, starting transfers between devices, padded_2(): before = lax.ppermute(last, axis, up)  13.1 us
    pallas_call x3, Pallas kernels, line_solve(): pl.pallas_call(cyclic_kernel, out_shape=jax.ShapeDtypeStruct((count, widt...  13 us
    ppermute x4, starting transfers between devices, padded_2(): after = lax.ppermute(initial, axis, down)  10.1 us
  transfers between devices with their start and end apart: 8, of which 4 were waited for; matrix products, arithmetic and copies ran while one was open for 9% of the time, Pallas kernels for 3%

profile of v2, /device:TPU:1, one launch (start us, length us, event | category | flops | bytes accessed | tf_op | source)
XLA Modules:
  0.0 233.8 jit_solution(12237844990371624214)
XLA Ops:
  0.9 4.5 %collective-permute-start = (f32[1,64,256]{2,1,0:T(8,128)S(1)}, f32[1,64,256]{2,1,0:T(8,128)S(1)}, u32[]{:S(2)}, u32[]{:S(2)}) collective-permute-start(f32[1,64,256]{2,1,0:T(8,128)S(1)} %get-tuple-element.120), channel_id=1, source_target_pairs={{0,4},{4,8},{8,12},{12,16},{16,20},{20,24},{24,28},{28,32},{32,36}... | collective-permute-start | bytes 196616 | tf_op jit(solution)/shard_map/ppermute | solution.py:38
  5.4 5.6 %collective-permute-start.1 = (f32[1,64,256]{2,1,0:T(8,128)S(1)}, f32[1,64,256]{2,1,0:T(8,128)S(1)}, u32[]{:S(2)}, u32[]{:S(2)}) collective-permute-start(f32[1,64,256]{2,1,0:T(8,128)S(1)} %get-tuple-element.119), channel_id=1, source_target_pairs={{4,0},{8,4},{12,8},{16,12},{20,16},{24,20},{28,24},{32,28},{36,32}... | collective-permute-start | bytes 196616 | tf_op jit(solution)/shard_map/ppermute | solution.py:39
  23.7 7.7 %shard_map.50 = f32[256,512]{1,0:T(8,128)} custom-call(f32[256,512]{1,0:T(8,128)} %copy.240.lower_ref, f32[256,512]{1,0:T(8,128)} %copy.241.main_ref, f32[256,512]{1,0:T(8,128)} %copy.242.upper_ref, f32[256,512]{1,0:T(8,128)} %select_select_fusion.rhs_ref), custom_call_target="tpu_custom_call" | custom-call | tf_op jit(solution)/shard_map/pallas_call | solution.py:240
  34.9 1.3 pad_multiply_fusion.7
  41.2 1.3 collective-permute-start.2
  42.5 1.3 collective-permute-start.3
  47.9 3.9 %collective-permute-done.3 = f32[4,64,1]{2,1,0:T(8,128)S(1)} collective-permute-done((f32[4,64,1]{2,1,0:T(8,128)S(1)}, f32[4,64,1]{2,1,0:T(8,128)S(1)}, u32[]{:S(2)}, u32[]{:S(2)}) %collective-permute-start.3) | collective-permute-done | bytes 1056 | tf_op jit(solution)/shard_map/ppermute | solution.py:39
  53.7 32.7 %shard_map.46 = f32[128,2,128]{2,1,0:T(2,128)} custom-call(f32[128,2,128]{2,1,0:T(2,128)} %bitcast.346), custom_call_target="tpu_custom_call" | custom-call | tf_op jit(solution)/shard_map/pallas_call | solution.py:321
  90.0 23.7 %shard_map.47 = f32[128,2,128]{2,1,0:T(2,128)} custom-call(f32[128,2,128]{2,1,0:T(2,128)} %copy.235.chunks_ref), custom_call_target="tpu_custom_call" | custom-call | tf_op jit(solution)/shard_map/pallas_call | solution.py:321
  116.9 2.6 %shard_map.48 = f32[256,128]{1,0:T(8,128)} custom-call(f32[256,128]{1,0:T(8,128)} %broadcast_in_dim.207.lower_ref, f32[256,128]{1,0:T(8,128)} %copy.289.main_ref, f32[256,128]{1,0:T(8,128)} %broadcast_in_dim.211.upper_ref, f32[256,128]{1,0:T(8,128)} %copy.238.rhs_ref), custom_call_target="tpu_custom_call" | custom-call | tf_op jit(solution)/shard_map/pallas_call | solution.py:240
  122.0 9.3 %shard_map.49 = f32[4,2,2,64]{3,2,1,0:T(2,128)} custom-call(f32[2,2,64]{2,1,0:T(2,128)} %pad_maximum_fusion.33.ends_ref), custom_call_target="tpu_custom_call" | custom-call | tf_op jit(solution)/shard_map/pallas_call | solution.py:276
  131.4 1.3 gather_fusion
  133.6 1.3 divide_bitcast_fusion.19
  135.8 3.4 %collective-permute-start.4 = (f32[1,64,256]{2,1,0:T(8,128)S(1)}, f32[1,64,256]{2,1,0:T(8,128)S(1)}, u32[]{:S(2)}, u32[]{:S(2)}) collective-permute-start(f32[1,64,256]{2,1,0:T(8,128)S(1)} %copy.265), channel_id=1, source_target_pairs={{0,4},{4,8},{8,12},{12,16},{16,20},{20,24},{24,28},{28,32},{32,36}... | collective-permute-start | bytes 196616 | tf_op jit(solution)/shard_map/ppermute | solution.py:38
  139.4 1.9 collective-permute-start.5
  141.4 3.6 %collective-permute-done.5 = f32[1,64,256]{2,1,0:T(8,128)S(1)} collective-permute-done((f32[1,64,256]{2,1,0:T(8,128)S(1)}, f32[1,64,256]{2,1,0:T(8,128)S(1)}, u32[]{:S(2)}, u32[]{:S(2)}) %collective-permute-start.5) | collective-permute-done | bytes 65568 | tf_op jit(solution)/shard_map/ppermute | solution.py:39
  145.1 3.9 %collective-permute-start.6 = (f32[4,64,1]{2,1,0:T(8,128)S(1)}, f32[4,64,1]{2,1,0:T(8,128)S(1)}, u32[]{:S(2)}, u32[]{:S(2)}) collective-permute-start(f32[4,64,1]{2,1,0:T(8,128)S(1)} %get-tuple-element.111), channel_id=1, source_target_pairs={{0,1},{1,2},{2,3},{4,5},{5,6},{6,7},{8,9},{9,10},{10,11},{12,13},{... | collective-permute-start | bytes 3080 | tf_op jit(solution)/shard_map/ppermute | solution.py:38
  149.0 1.3 collective-permute-start.7
  150.9 7.0 %collective-permute-done.7 = f32[4,64,1]{2,1,0:T(8,128)S(1)} collective-permute-done((f32[4,64,1]{2,1,0:T(8,128)S(1)}, f32[4,64,1]{2,1,0:T(8,128)S(1)}, u32[]{:S(2)}, u32[]{:S(2)}) %collective-permute-start.7) | collective-permute-done | bytes 1056 | tf_op jit(solution)/shard_map/ppermute | solution.py:39
  159.7 26.5 %shard_map.51 = f32[128,2,128]{2,1,0:T(2,128)} custom-call(f32[128,2,128]{2,1,0:T(2,128)} %bitcast.349), custom_call_target="tpu_custom_call" | custom-call | tf_op jit(solution)/shard_map/pallas_call | solution.py:321
  188.8 23.7 %shard_map.52 = f32[128,2,128]{2,1,0:T(2,128)} custom-call(f32[128,2,128]{2,1,0:T(2,128)} %pad_maximum_fusion.10.chunks_ref), custom_call_target="tpu_custom_call" | custom-call | tf_op jit(solution)/shard_map/pallas_call | solution.py:321
  214.2 2.6 %shard_map.53 = f32[256,128]{1,0:T(8,128)} custom-call(f32[256,128]{1,0:T(8,128)} %broadcast_in_dim.207.lower_ref, f32[256,128]{1,0:T(8,128)} %copy.289.main_ref, f32[256,128]{1,0:T(8,128)} %broadcast_in_dim.211.upper_ref, f32[256,128]{1,0:T(8,128)} %copy.290.rhs_ref), custom_call_target="tpu_custom_call" | custom-call | tf_op jit(solution)/shard_map/pallas_call | solution.py:240
  219.3 9.3 %shard_map.54 = f32[4,2,2,64]{3,2,1,0:T(2,128)} custom-call(f32[2,2,64]{2,1,0:T(2,128)} %pad_maximum_fusion.35.ends_ref), custom_call_target="tpu_custom_call" | custom-call | tf_op jit(solution)/shard_map/pallas_call | solution.py:276
  230.9 1.3 divide_bitcast_fusion.18
  (480 shorter events, 46.7 us)
Async XLA Ops:
  0.9 10.1 %copy-start.5 = (s32[64]{0:T(128)S(1)}, s32[64]{0:T(128)}, u32[]{:S(2)}) copy-start(s32[64]{0:T(128)} %param.9) | copy-start | bytes 772
  0.9 39.4 %collective-permute-start = (f32[1,64,256]{2,1,0:T(8,128)S(1)}, f32[1,64,256]{2,1,0:T(8,128)S(1)}, u32[]{:S(2)}, u32[]{:S(2)}) collective-permute-start(f32[1,64,256]{2,1,0:T(8,128)S(1)} %get-tuple-element.120), channel_id=1, source_target_pairs={{0,4},{4,8},{8,12},{12,16},{16,20},{20,24},{24,28},{28,32},{32,36}... | collective-permute-start | bytes 196616 | tf_op jit(solution)/shard_map/ppermute | solution.py:38
  5.4 35.7 %collective-permute-start.1 = (f32[1,64,256]{2,1,0:T(8,128)S(1)}, f32[1,64,256]{2,1,0:T(8,128)S(1)}, u32[]{:S(2)}, u32[]{:S(2)}) collective-permute-start(f32[1,64,256]{2,1,0:T(8,128)S(1)} %get-tuple-element.119), channel_id=1, source_target_pairs={{4,0},{8,4},{12,8},{16,12},{20,16},{24,20},{28,24},{32,28},{36,32}... | collective-permute-start | bytes 196616 | tf_op jit(solution)/shard_map/ppermute | solution.py:39
  15.4 0.7 copy-start.3
  16.3 0.7 copy-start.4
  40.2 0.9 copy-start
  41.2 6.7 %collective-permute-start.2 = (f32[4,64,1]{2,1,0:T(8,128)S(1)}, f32[4,64,1]{2,1,0:T(8,128)S(1)}, u32[]{:S(2)}, u32[]{:S(2)}) collective-permute-start(f32[4,64,1]{2,1,0:T(8,128)S(1)} %get-tuple-element.113), channel_id=1, source_target_pairs={{0,1},{1,2},{2,3},{4,5},{5,6},{6,7},{8,9},{9,10},{10,11},{12,13},{... | collective-permute-start | bytes 3080 | tf_op jit(solution)/shard_map/ppermute | solution.py:38
  42.5 9.3 %collective-permute-start.3 = (f32[4,64,1]{2,1,0:T(8,128)S(1)}, f32[4,64,1]{2,1,0:T(8,128)S(1)}, u32[]{:S(2)}, u32[]{:S(2)}) collective-permute-start(f32[4,64,1]{2,1,0:T(8,128)S(1)} %get-tuple-element.114), channel_id=1, source_target_pairs={{1,0},{2,1},{3,2},{5,4},{6,5},{7,6},{9,8},{10,9},{11,10},{13,12},{... | collective-permute-start | bytes 3080 | tf_op jit(solution)/shard_map/ppermute | solution.py:39
  86.4 1.0 copy-start.1
  135.8 5.5 %collective-permute-start.4 = (f32[1,64,256]{2,1,0:T(8,128)S(1)}, f32[1,64,256]{2,1,0:T(8,128)S(1)}, u32[]{:S(2)}, u32[]{:S(2)}) collective-permute-start(f32[1,64,256]{2,1,0:T(8,128)S(1)} %copy.265), channel_id=1, source_target_pairs={{0,4},{4,8},{8,12},{12,16},{16,20},{20,24},{24,28},{28,32},{32,36}... | collective-permute-start | bytes 196616 | tf_op jit(solution)/shard_map/ppermute | solution.py:38
  139.4 5.6 %collective-permute-start.5 = (f32[1,64,256]{2,1,0:T(8,128)S(1)}, f32[1,64,256]{2,1,0:T(8,128)S(1)}, u32[]{:S(2)}, u32[]{:S(2)}) collective-permute-start(f32[1,64,256]{2,1,0:T(8,128)S(1)} %copy.268), channel_id=1, source_target_pairs={{4,0},{8,4},{12,8},{16,12},{20,16},{24,20},{28,24},{32,28},{36,32}... | collective-permute-start | bytes 196616 | tf_op jit(solution)/shard_map/ppermute | solution.py:39
  145.1 5.8 %collective-permute-start.6 = (f32[4,64,1]{2,1,0:T(8,128)S(1)}, f32[4,64,1]{2,1,0:T(8,128)S(1)}, u32[]{:S(2)}, u32[]{:S(2)}) collective-permute-start(f32[4,64,1]{2,1,0:T(8,128)S(1)} %get-tuple-element.111), channel_id=1, source_target_pairs={{0,1},{1,2},{2,3},{4,5},{5,6},{6,7},{8,9},{9,10},{10,11},{12,13},{... | collective-permute-start | bytes 3080 | tf_op jit(solution)/shard_map/ppermute | solution.py:38
  149.0 8.9 %collective-permute-start.7 = (f32[4,64,1]{2,1,0:T(8,128)S(1)}, f32[4,64,1]{2,1,0:T(8,128)S(1)}, u32[]{:S(2)}, u32[]{:S(2)}) collective-permute-start(f32[4,64,1]{2,1,0:T(8,128)S(1)} %get-tuple-element.112), channel_id=1, source_target_pairs={{1,0},{2,1},{3,2},{5,4},{6,5},{7,6},{9,8},{10,9},{11,10},{13,12},{... | collective-permute-start | bytes 3080 | tf_op jit(solution)/shard_map/ppermute | solution.py:39
  186.2 1.0 copy-start.2

commit v3 on v1

--- a/solution.py
+++ b/solution.py
@@ -354,39 +354,27 @@
         1.0 - solve_scale * (var_middle.reshape(var_count, 1) - reaction_plain.reshape(1, planes))
     ).reshape(blocks, var_cols, planes)
 
-    column_shape = (var_cols, blocks, 2, planes)
-    lower_cols = jnp.broadcast_to(var_lower.T.reshape(var_cols, blocks, 1, 1), column_shape)
-    upper_cols = jnp.broadcast_to(var_upper.T.reshape(var_cols, blocks, 1, 1), column_shape)
-    main_cols = jnp.broadcast_to(
-        var_main.transpose(1, 0, 2).reshape(var_cols, blocks, 1, planes), column_shape
-    )
-    position = lax.broadcasted_iota(jnp.int32, column_shape, 0)
-    kind = lax.broadcasted_iota(jnp.int32, column_shape, 2)
-    coupling = jnp.where(
-        (kind == 0) & (position == 0),
-        var_lower[:, 0].reshape(1, blocks, 1, 1),
-        jnp.where(
-            (kind == 1) & (position == var_cols - 1),
-            var_upper[:, var_cols - 1].reshape(1, blocks, 1, 1),
-            0.0,
-        ),
-    )
-    flat = (var_cols, blocks * 2 * planes)
-    columns = line_solve(
-        lower_cols.reshape(flat),
-        main_cols.reshape(flat),
-        upper_cols.reshape(flat),
-        coupling.reshape(flat),
-    ).reshape(column_shape)
-    g_first, g_last = columns[0, :, 0, :], columns[var_cols - 1, :, 0, :]
-    h_first, h_last = columns[0, :, 1, :], columns[var_cols - 1, :, 1, :]
-    g_own = lax.dynamic_index_in_dim(columns[:, :, 0, :], var_place, 1, keepdims=False)
-    h_own = lax.dynamic_index_in_dim(columns[:, :, 1, :], var_place, 1, keepdims=False)
     lower_own = lax.dynamic_index_in_dim(var_lower, var_place, 0, keepdims=False)
     upper_own = lax.dynamic_index_in_dim(var_upper, var_place, 0, keepdims=False)
     main_own = lax.dynamic_index_in_dim(var_main, var_place, 0, keepdims=False)
-
-    def interface_solve(y_first, y_last):
+    column_shape = (var_cols, 2, planes)
+    position = lax.broadcasted_iota(jnp.int32, column_shape, 0)
+    kind = lax.broadcasted_iota(jnp.int32, column_shape, 1)
+    coupling = jnp.where(
+        (kind == 0) & (position == 0),
+        lower_own[0],
+        jnp.where((kind == 1) & (position == var_cols - 1), upper_own[var_cols - 1], 0.0),
+    )
+    flat = (var_cols, 2 * planes)
+    columns = line_solve(
+        jnp.broadcast_to(lower_own.reshape(var_cols, 1), flat),
+        jnp.broadcast_to(main_own.reshape(var_cols, 1, planes), column_shape).reshape(flat),
+        jnp.broadcast_to(upper_own.reshape(var_cols, 1), flat),
+        coupling.reshape(flat),
+    ).reshape(column_shape)
+    g_own, h_own = columns[:, 0, :], columns[:, 1, :]
+    column_ends = jnp.stack([g_own[0], g_own[var_cols - 1], h_own[0], h_own[var_cols - 1]])
+    def interface_solve(y_first, y_last, g_first, g_last, h_first, h_last):
         size = 2 * (blocks - 1)
         matrix = [[None] * size for _ in range(size)]
         rhs = [None] * size
@@ -443,8 +431,18 @@
             jnp.broadcast_to(upper_own.reshape(var_cols, 1), shape),
             lines,
         ).reshape(var_cols, spot_rows, planes)
-        ends = gather_ends(jnp.stack([local[0], local[var_cols - 1]]))
-        left, right = interface_solve(ends[:, 0], ends[:, 1])
+        message = jnp.concatenate(
+            [local[0], local[var_cols - 1], column_ends], axis=0
+        )
+        ends = gather_ends(message)
+        left, right = interface_solve(
+            ends[:, :spot_rows],
+            ends[:, spot_rows : 2 * spot_rows],
+            ends[:, 2 * spot_rows],
+            ends[:, 2 * spot_rows + 1],
+            ends[:, 2 * spot_rows + 2],
+            ends[:, 2 * spot_rows + 3],
+        )
         solved = (
             local
             - left.reshape(1, spot_rows, planes) * g_own.reshape(var_cols, 1, planes)

time: 204 us -> 194 us (0.951)
  waiting for transfers between devices: 34.7 us -> 28.8 us
  Pallas kernels: 31.3 us -> 26.5 us
  starting transfers between devices: 45.7 us -> 48 us
    all_to_all x1, waiting for transfers between devices: 10.9 us -> 4.21 us  [spot_solve(): lax.all_to_all(values.reshape(spot_rows, line_count), 'spot', split_axis=...]
    pallas_call x3, Pallas kernels: 13 us -> 7.91 us  [line_solve(): pl.pallas_call(cyclic_kernel, out_shape=jax.ShapeDtypeStruct((count, widt...]
    ppermute x4, starting transfers between devices: 10.1 us -> 13.3 us  [padded_2(): after = lax.ppermute(initial, axis, down)]
    reshape x3 -> x0, local copies, waits for them, and re-layouts: 3.01 us -> none  [the longest x1 1 us: shards(): upper_cols.reshape(flat)]
    ppermute x4, starting transfers between devices: 13.5 us -> 10.8 us  [padded_2(): before = lax.ppermute(last, axis, up)]
    all_to_all x1, starting transfers between devices: 5.6 us -> 8.23 us  [spot_solve(): lax.all_to_all(solved, 'spot', split_axis=0, concat_axis=1, tiled=True)]
  transfers between devices with their start and end apart: 10 -> 10, of which waited for: 7 -> 7; matrix products, arithmetic and copies ran while one was open for 10% -> 10% of each run, Pallas kernels for 4% -> 1%
where the time goes in v3:
time: 194 us; the launch traced here: 193 us
  starting transfers between devices  48 us (25%)
  blocking collectives  40 us (21%)
  local copies, waits for them, and re-layouts  29.6 us (15%)
  waiting for transfers between devices  28.8 us (15%)
  Pallas kernels  26.5 us (14%)
  other arithmetic  14.3 us (7%)
  between operations  5.77 us (3%)
    all_to_all x1, blocking collectives, spot_solve(): lax.all_to_all(values.reshape(spot_rows, line_count), 'spot', split_axis=...  23.6 us
    pallas_call x2, Pallas kernels, gather_var(): pl.pallas_call(functools.partial(gather_kernel, blocks), out_shape=jax.Sh...  18.6 us
    all_to_all x1, blocking collectives, spot_solve(): lax.all_to_all(solved, 'spot', split_axis=0, concat_axis=1, tiled=True)  16.4 us
    all_to_all x1, starting transfers between devices, spot_solve(): lax.all_to_all(values.reshape(spot_rows, line_count), 'spot', split_axis=...  15.6 us
    ppermute x4, waiting for transfers between devices, padded_2(): after = lax.ppermute(initial, axis, down)  15.3 us
    ppermute x4, starting transfers between devices, padded_2(): after = lax.ppermute(initial, axis, down)  13.3 us
    ppermute x4, starting transfers between devices, padded_2(): before = lax.ppermute(last, axis, up)  10.8 us
    all_to_all x1, starting transfers between devices, spot_solve(): lax.all_to_all(solved, 'spot', split_axis=0, concat_axis=1, tiled=True)  8.23 us
  transfers between devices with their start and end apart: 10, of which 7 were waited for; matrix products, arithmetic and copies ran while one was open for 10% of the time, Pallas kernels for 1%

profile of v3, /device:TPU:1, one launch (start us, length us, event | category | flops | bytes accessed | tf_op | source)
XLA Modules:
  0.0 193.0 jit_solution(18381813038863144677)
XLA Ops:
  0.9 8.8 %collective-permute-start.1 = (f32[1,64,256]{2,1,0:T(8,128)S(1)}, f32[1,64,256]{2,1,0:T(8,128)S(1)}, u32[]{:S(2)}, u32[]{:S(2)}) collective-permute-start(f32[1,64,256]{2,1,0:T(8,128)S(1)} %get-tuple-element.121), channel_id=1, source_target_pairs={{4,0},{8,4},{12,8},{16,12},{20,16},{24,20},{28,24},{32,28},{36,32}... | collective-permute-start | bytes 196616 | tf_op jit(solution)/shard_map/ppermute | solution.py:39
  9.7 1.9 collective-permute-start
  25.9 2.1 %select_select_fusion.rhs_ref = f32[256,128]{1,0:T(8,128)} fusion(f32[]{:T(128)} %bitcast.35, f32[]{:T(128)} %bitcast.34, pred[128]{0:T(512)(128)(4,1)S(1)} %iota.40, pred[128]{0:T(512)(128)(4,1)S(1)} %iota.34, pred[256]{0:T(512)(128)(4,1)S(1)} %get-tuple-element.269, pred[256]{0:T(512)(128)(4,1)S(1)} %get-tuple-element.270), kind=kLoop, calls=%fused_computation.153 | loop fusion | flops 131072 | bytes 131848 | tf_op jit(solution)/shard_map/jit(_where)/select_n | solution.py:363
  28.9 1.3 collective-permute-start.2
  31.5 1.4 collective-permute-done.2
  32.9 6.8 %collective-permute-done.3 = f32[4,64,1]{2,1,0:T(8,128)S(1)} collective-permute-done((f32[4,64,1]{2,1,0:T(8,128)S(1)}, f32[4,64,1]{2,1,0:T(8,128)S(1)}, u32[]{:S(2)}, u32[]{:S(2)}) %collective-permute-start.3) | collective-permute-done | bytes 1056 | tf_op jit(solution)/shard_map/ppermute | solution.py:39
  41.6 15.6 %all-to-all-start = ((f32[2,128,128]{2,0,1:T(2,128)}), f32[2,128,128]{2,0,1:T(2,128)S(1)}, u32[]{:S(2)}, u32[]{:S(2)}) async-start(f32[2,128,128]{2,0,1:T(2,128)} %copy.397), calls=%async_computation | async-start | bytes 262144 | tf_op jit(solution)/shard_map/all_to_all | solution.py:318
  59.7 2.6 %shard_map.47 = f32[256,128]{1,0:T(8,128)} custom-call(f32[256,128]{1,0:T(8,128)} %broadcast_in_dim.181.lower_ref, f32[256,128]{1,0:T(8,128)} %copy.463.main_ref, f32[256,128]{1,0:T(8,128)} %broadcast_in_dim.185.upper_ref, f32[256,128]{1,0:T(8,128)} %select_select_fusion.rhs_ref), custom_call_target="tpu_custom_call" | custom-call | tf_op jit(solution)/shard_map/pallas_call | solution.py:240
  64.2 4.2 %all-to-all-done = f32[2,128,128]{2,0,1:T(2,128)S(1)} async-done(((f32[2,128,128]{2,0,1:T(2,128)}), f32[2,128,128]{2,0,1:T(2,128)S(1)}, u32[]{:S(2)}, u32[]{:S(2)}) %all-to-all-start) | async-done | bytes 131104 | tf_op jit(solution)/shard_map/all_to_all | solution.py:318
  71.1 8.2 %all-to-all-start.1 = ((f32[128,2,128]{2,1,0:T(2,128)}), f32[128,2,128]{2,1,0:T(2,128)S(1)}, u32[]{:S(2)}, u32[]{:S(2)}) async-start(f32[128,2,128]{2,1,0:T(2,128)} %copy.410), calls=%async_computation.1 | async-start | bytes 262144 | tf_op jit(solution)/shard_map/all_to_all | solution.py:338
  83.2 7.3 %all-to-all-done.1 = f32[128,2,128]{2,1,0:T(2,128)S(1)} async-done(((f32[128,2,128]{2,1,0:T(2,128)}), f32[128,2,128]{2,1,0:T(2,128)S(1)}, u32[]{:S(2)}, u32[]{:S(2)}) %all-to-all-start.1) | async-done | bytes 131104 | tf_op jit(solution)/shard_map/all_to_all | solution.py:338
  91.3 2.6 %shard_map.46 = f32[256,128]{1,0:T(8,128)} custom-call(f32[256,128]{1,0:T(8,128)} %broadcast_in_dim.181.lower_ref, f32[256,128]{1,0:T(8,128)} %copy.463.main_ref, f32[256,128]{1,0:T(8,128)} %broadcast_in_dim.185.upper_ref, f32[256,128]{1,0:T(8,128)} %copy.413.rhs_ref), custom_call_target="tpu_custom_call" | custom-call | tf_op jit(solution)/shard_map/pallas_call | solution.py:240
  96.4 10.2 %shard_map.48 = f32[4,8,64]{2,1,0:T(8,128)} custom-call(f32[8,64]{1,0:T(8,128)} %concatenate.393.ends_ref), custom_call_target="tpu_custom_call" | custom-call | tf_op jit(solution)/shard_map/pallas_call | solution.py:276
  108.9 1.3 divide_bitcast_fusion.20
  111.1 3.6 %collective-permute-start.4 = (f32[1,64,256]{2,1,0:T(8,128)S(1)}, f32[1,64,256]{2,1,0:T(8,128)S(1)}, u32[]{:S(2)}, u32[]{:S(2)}) collective-permute-start(f32[1,64,256]{2,1,0:T(8,128)S(1)} %copy.438), channel_id=1, source_target_pairs={{0,4},{4,8},{8,12},{12,16},{16,20},{20,24},{24,28},{28,32},{32,36}... | collective-permute-start | bytes 196616 | tf_op jit(solution)/shard_map/ppermute | solution.py:38
  115.0 1.9 collective-permute-start.5
  116.9 3.6 %collective-permute-done.5 = f32[1,64,256]{2,1,0:T(8,128)S(1)} collective-permute-done((f32[1,64,256]{2,1,0:T(8,128)S(1)}, f32[1,64,256]{2,1,0:T(8,128)S(1)}, u32[]{:S(2)}, u32[]{:S(2)}) %collective-permute-start.5) | collective-permute-done | bytes 65568 | tf_op jit(solution)/shard_map/ppermute | solution.py:39
  120.7 4.0 %collective-permute-start.6 = (f32[4,64,1]{2,1,0:T(8,128)S(1)}, f32[4,64,1]{2,1,0:T(8,128)S(1)}, u32[]{:S(2)}, u32[]{:S(2)}) collective-permute-start(f32[4,64,1]{2,1,0:T(8,128)S(1)} %get-tuple-element.111), channel_id=1, source_target_pairs={{0,1},{1,2},{2,3},{4,5},{5,6},{6,7},{8,9},{9,10},{10,11},{12,13},{... | collective-permute-start | bytes 3080 | tf_op jit(solution)/shard_map/ppermute | solution.py:38
  126.5 4.8 %collective-permute-done.7 = f32[4,64,1]{2,1,0:T(8,128)S(1)} collective-permute-done((f32[4,64,1]{2,1,0:T(8,128)S(1)}, f32[4,64,1]{2,1,0:T(8,128)S(1)}, u32[]{:S(2)}, u32[]{:S(2)}) %collective-permute-start.7) | collective-permute-done | bytes 1056 | tf_op jit(solution)/shard_map/ppermute | solution.py:39
  132.5 23.6 %all_to_all.64 = f32[2,128,128]{2,0,1:T(2,128)S(1)} all-to-all(f32[2,128,128]{2,0,1:T(2,128)S(1)} %copy.448), channel_id=1, replica_groups=mesh['spot'=128,'var'=4] {'spot'}, dimensions={1} | all-to-all | bytes 262144 | tf_op jit(solution)/shard_map/all_to_all | solution.py:318
  157.1 16.4 %all_to_all.65 = f32[128,2,128]{2,1,0:T(2,128)S(1)} all-to-all(f32[128,2,128]{2,1,0:T(2,128)S(1)} %copy.461), channel_id=1, replica_groups=mesh['spot'=128,'var'=4] {'spot'}, dimensions={0} | all-to-all | bytes 262144 | tf_op jit(solution)/shard_map/all_to_all | solution.py:338
  174.3 2.6 %shard_map.49 = f32[256,128]{1,0:T(8,128)} custom-call(f32[256,128]{1,0:T(8,128)} %broadcast_in_dim.181.lower_ref, f32[256,128]{1,0:T(8,128)} %copy.463.main_ref, f32[256,128]{1,0:T(8,128)} %broadcast_in_dim.185.upper_ref, f32[256,128]{1,0:T(8,128)} %copy.464.rhs_ref), custom_call_target="tpu_custom_call" | custom-call | tf_op jit(solution)/shard_map/pallas_call | solution.py:240
  179.4 8.4 %shard_map.50 = f32[4,8,64]{2,1,0:T(8,128)} custom-call(f32[8,64]{1,0:T(8,128)} %concatenate.439.ends_ref), custom_call_target="tpu_custom_call" | custom-call | tf_op jit(solution)/shard_map/pallas_call | solution.py:276
  190.2 1.3 divide_bitcast_fusion.19
  (470 shorter events, 42.4 us)
Async XLA Ops:
  0.9 27.9 %collective-permute-start.1 = (f32[1,64,256]{2,1,0:T(8,128)S(1)}, f32[1,64,256]{2,1,0:T(8,128)S(1)}, u32[]{:S(2)}, u32[]{:S(2)}) collective-permute-start(f32[1,64,256]{2,1,0:T(8,128)S(1)} %get-tuple-element.121), channel_id=1, source_target_pairs={{4,0},{8,4},{12,8},{16,12},{20,16},{24,20},{28,24},{32,28},{36,32}... | collective-permute-start | bytes 196616 | tf_op jit(solution)/shard_map/ppermute | solution.py:39
  9.7 19.0 %collective-permute-start = (f32[1,64,256]{2,1,0:T(8,128)S(1)}, f32[1,64,256]{2,1,0:T(8,128)S(1)}, u32[]{:S(2)}, u32[]{:S(2)}) collective-permute-start(f32[1,64,256]{2,1,0:T(8,128)S(1)} %get-tuple-element.122), channel_id=1, source_target_pairs={{0,4},{4,8},{8,12},{12,16},{16,20},{20,24},{24,28},{28,32},{32,36}... | collective-permute-start | bytes 196616 | tf_op jit(solution)/shard_map/ppermute | solution.py:38
  11.6 0.7 copy-start.3
  16.5 0.7 copy-start.1
  17.6 0.7 copy-start.2
  25.9 2.8 %copy-start = (f32[2,64,256]{2,1,0:T(8,128)S(1)}, f32[2,64,256]{2,1,0:T(8,128)}, u32[]{:S(2)}) copy-start(f32[2,64,256]{2,1,0:T(8,128)} %param.6) | copy-start | bytes 393220
  28.9 4.0 %collective-permute-start.2 = (f32[4,64,1]{2,1,0:T(8,128)S(1)}, f32[4,64,1]{2,1,0:T(8,128)S(1)}, u32[]{:S(2)}, u32[]{:S(2)}) collective-permute-start(f32[4,64,1]{2,1,0:T(8,128)S(1)} %get-tuple-element.113), channel_id=1, source_target_pairs={{0,1},{1,2},{2,3},{4,5},{5,6},{6,7},{8,9},{9,10},{10,11},{12,13},{... | collective-permute-start | bytes 3080 | tf_op jit(solution)/shard_map/ppermute | solution.py:38
  30.2 9.5 %collective-permute-start.3 = (f32[4,64,1]{2,1,0:T(8,128)S(1)}, f32[4,64,1]{2,1,0:T(8,128)S(1)}, u32[]{:S(2)}, u32[]{:S(2)}) collective-permute-start(f32[4,64,1]{2,1,0:T(8,128)S(1)} %get-tuple-element.114), channel_id=1, source_target_pairs={{1,0},{2,1},{3,2},{5,4},{6,5},{7,6},{9,8},{10,9},{11,10},{13,12},{... | collective-permute-start | bytes 3080 | tf_op jit(solution)/shard_map/ppermute | solution.py:39
  41.6 26.8 %all-to-all-start = ((f32[2,128,128]{2,0,1:T(2,128)}), f32[2,128,128]{2,0,1:T(2,128)S(1)}, u32[]{:S(2)}, u32[]{:S(2)}) async-start(f32[2,128,128]{2,0,1:T(2,128)} %copy.397), calls=%async_computation | async-start | bytes 262144 | tf_op jit(solution)/shard_map/all_to_all | solution.py:318
  71.1 19.4 %all-to-all-start.1 = ((f32[128,2,128]{2,1,0:T(2,128)}), f32[128,2,128]{2,1,0:T(2,128)S(1)}, u32[]{:S(2)}, u32[]{:S(2)}) async-start(f32[128,2,128]{2,1,0:T(2,128)} %copy.410), calls=%async_computation.1 | async-start | bytes 262144 | tf_op jit(solution)/shard_map/all_to_all | solution.py:338
  111.1 5.8 %collective-permute-start.4 = (f32[1,64,256]{2,1,0:T(8,128)S(1)}, f32[1,64,256]{2,1,0:T(8,128)S(1)}, u32[]{:S(2)}, u32[]{:S(2)}) collective-permute-start(f32[1,64,256]{2,1,0:T(8,128)S(1)} %copy.438), channel_id=1, source_target_pairs={{0,4},{4,8},{8,12},{12,16},{16,20},{20,24},{24,28},{28,32},{32,36}... | collective-permute-start | bytes 196616 | tf_op jit(solution)/shard_map/ppermute | solution.py:38
  115.0 5.6 %collective-permute-start.5 = (f32[1,64,256]{2,1,0:T(8,128)S(1)}, f32[1,64,256]{2,1,0:T(8,128)S(1)}, u32[]{:S(2)}, u32[]{:S(2)}) collective-permute-start(f32[1,64,256]{2,1,0:T(8,128)S(1)} %copy.441), channel_id=1, source_target_pairs={{4,0},{8,4},{12,8},{16,12},{20,16},{24,20},{28,24},{32,28},{36,32}... | collective-permute-start | bytes 196616 | tf_op jit(solution)/shard_map/ppermute | solution.py:39
  120.7 5.9 %collective-permute-start.6 = (f32[4,64,1]{2,1,0:T(8,128)S(1)}, f32[4,64,1]{2,1,0:T(8,128)S(1)}, u32[]{:S(2)}, u32[]{:S(2)}) collective-permute-start(f32[4,64,1]{2,1,0:T(8,128)S(1)} %get-tuple-element.111), channel_id=1, source_target_pairs={{0,1},{1,2},{2,3},{4,5},{5,6},{6,7},{8,9},{9,10},{10,11},{12,13},{... | collective-permute-start | bytes 3080 | tf_op jit(solution)/shard_map/ppermute | solution.py:38
  124.6 6.7 %collective-permute-start.7 = (f32[4,64,1]{2,1,0:T(8,128)S(1)}, f32[4,64,1]{2,1,0:T(8,128)S(1)}, u32[]{:S(2)}, u32[]{:S(2)}) collective-permute-start(f32[4,64,1]{2,1,0:T(8,128)S(1)} %get-tuple-element.112), channel_id=1, source_target_pairs={{1,0},{2,1},{3,2},{5,4},{6,5},{7,6},{9,8},{10,9},{11,10},{13,12},{... | collective-permute-start | bytes 3080 | tf_op jit(solution)/shard_map/ppermute | solution.py:39

commit v4 on v3

--- a/solution.py
+++ b/solution.py
@@ -28,17 +28,33 @@
 coupling_vr = 0.1 * vol_var * vol_rate
 
 
-def padded_2(array, sides, width):
-    for axis, dim in sides:
-        devices, length = (lax.axis_size(axis), array.shape[dim])
-        up = [(i, (i + 1) % devices) for i in range(devices - 1)]
-        down = [(j, i) for i, j in up]
-        last = lax.slice_in_dim(array, length - width, length, axis=dim)
-        initial = lax.slice_in_dim(array, 0, width, axis=dim)
-        before = lax.ppermute(last, axis, up)
-        after = lax.ppermute(initial, axis, down)
-        array = jnp.concatenate([before, array, after], axis=dim)
-    return array
+def shift_both(piece, spot_step, var_step):
+    spots, vars_ = lax.axis_size("spot"), lax.axis_size("var")
+    pairs = []
+    for s in range(spots):
+        for v in range(vars_):
+            ts, tv = s + spot_step, v + var_step
+            if 0 <= ts < spots and 0 <= tv < vars_:
+                pairs.append((s * vars_ + v, ts * vars_ + tv))
+    return lax.ppermute(piece, ("spot", "var"), pairs)
+
+
+def padded_2(array):
+    rows, cols = array.shape[0], array.shape[2]
+    first_row, last_row = array[0:1], array[rows - 1 : rows]
+    first_col, last_col = array[:, :, 0:1], array[:, :, cols - 1 : cols]
+    above = shift_both(last_row, 1, 0)
+    below = shift_both(first_row, -1, 0)
+    left = shift_both(last_col, 0, 1)
+    right = shift_both(first_col, 0, -1)
+    corner_above_left = shift_both(last_row[:, :, cols - 1 : cols], 1, 1)
+    corner_above_right = shift_both(last_row[:, :, 0:1], 1, -1)
+    corner_below_left = shift_both(first_row[:, :, cols - 1 : cols], -1, 1)
+    corner_below_right = shift_both(first_row[:, :, 0:1], -1, -1)
+    top = jnp.concatenate([corner_above_left, above, corner_above_right], axis=2)
+    middle = jnp.concatenate([left, array, right], axis=2)
+    bottom = jnp.concatenate([corner_below_left, below, corner_below_right], axis=2)
+    return jnp.concatenate([top, middle, bottom], axis=0)
 
 
 def coordinates(node_list, low_end, high_end):
@@ -310,7 +326,7 @@
     var_plain = var_geo[0].reshape(var_cols)
 
     def edge_terms(values, mixing_only):
-        padded = padded_2(values, (("spot", 0), ("var", 2)), 1)
+        padded = padded_2(values)
         padded = jnp.pad(padded, ((0, 0), (1, 1), (0, 0)))
         return explicit_terms(padded, spot_geo, var_geo, rate_geo, mixing_only)
 

time: 194 us -> 223 us (1.15)
  starting transfers between devices: 48 us -> 83.3 us
  waiting for transfers between devices: 28.8 us -> 16.5 us
  Pallas kernels: 26.5 us -> 31.7 us
    ppermute x8 -> x16, starting transfers between devices: 24.1 us -> 54.9 us  [shift_both(): return lax.ppermute(piece, ('spot', 'var'), pairs)]
    ppermute x8 -> x16, waiting for transfers between devices: 17.3 us -> 4.89 us  [shift_both(): return lax.ppermute(piece, ('spot', 'var'), pairs)]
    pallas_call x2, Pallas kernels: 18.6 us -> 23.8 us  [gather_var(): pl.pallas_call(functools.partial(gather_kernel, blocks), out_shape=jax.Sh...]
    all_to_all x1, starting transfers between devices: 15.6 us -> 20.3 us  [spot_solve(): lax.all_to_all(values.reshape(spot_rows, line_count), 'spot', split_axis=...]
  transfers between devices with their start and end apart: 10 -> 18, of which waited for: 7 -> 5; matrix products, arithmetic and copies ran while one was open for 10% -> 9% of each run, Pallas kernels for 1% -> 1%
where the time goes in v4:
time: 223 us; the launch traced here: 221 us
  starting transfers between devices  83.3 us (37%)
  blocking collectives  40.8 us (18%)
  Pallas kernels  31.7 us (14%)
  local copies, waits for them, and re-layouts  28.6 us (13%)
  waiting for transfers between devices  16.5 us (7%)
  other arithmetic  14.5 us (7%)
  between operations  5.78 us (3%)
    ppermute x16, starting transfers between devices, shift_both(): return lax.ppermute(piece, ('spot', 'var'), pairs)  54.9 us
    all_to_all x1, blocking collectives, spot_solve(): lax.all_to_all(values.reshape(spot_rows, line_count), 'spot', split_axis=...  24.5 us
    pallas_call x2, Pallas kernels, gather_var(): pl.pallas_call(functools.partial(gather_kernel, blocks), out_shape=jax.Sh...  23.8 us
    all_to_all x1, starting transfers between devices, spot_solve(): lax.all_to_all(values.reshape(spot_rows, line_count), 'spot', split_axis=...  20.3 us
    all_to_all x1, blocking collectives, spot_solve(): lax.all_to_all(solved, 'spot', split_axis=0, concat_axis=1, tiled=True)  16.4 us
    all_to_all x1, starting transfers between devices, spot_solve(): lax.all_to_all(solved, 'spot', split_axis=0, concat_axis=1, tiled=True)  8.22 us
    pallas_call x3, Pallas kernels, line_solve(): pl.pallas_call(cyclic_kernel, out_shape=jax.ShapeDtypeStruct((count, widt...  7.91 us
    all_to_all x1, waiting for transfers between devices, spot_solve(): lax.all_to_all(solved, 'spot', split_axis=0, concat_axis=1, tiled=True)  7.41 us
  transfers between devices with their start and end apart: 18, of which 5 were waited for; matrix products, arithmetic and copies ran while one was open for 9% of the time, Pallas kernels for 1%

profile of v4, /device:TPU:1, one launch (start us, length us, event | category | flops | bytes accessed | tf_op | source)
XLA Modules:
  0.0 221.3 jit_solution(16347783642282267446)
XLA Ops:
  0.9 6.5 %collective-permute-start = (f32[1,64,1]{2,1,0:T(8,128)S(1)}, f32[1,64,1]{2,1,0:T(8,128)S(1)}, u32[]{:S(2)}, u32[]{:S(2)}) collective-permute-start(f32[1,64,1]{2,1,0:T(8,128)S(1)} %get-tuple-element.121), channel_id=1, source_target_pairs={{0,5},{1,6},{2,7},{4,9},{5,10},{6,11},{8,13},{9,14},{10,15},{12,17... | collective-permute-start | bytes 776 | tf_op jit(solution)/shard_map/ppermute | solution.py:39
  8.8 5.2 %collective-permute-start.5 = (f32[1,64,1]{2,1,0:T(8,128)S(1)}, f32[1,64,1]{2,1,0:T(8,128)S(1)}, u32[]{:S(2)}, u32[]{:S(2)}) collective-permute-start(f32[1,64,1]{2,1,0:T(8,128)S(1)} %get-tuple-element.122), channel_id=1, source_target_pairs={{4,1},{5,2},{6,3},{8,5},{9,6},{10,7},{12,9},{13,10},{14,11},{16,13... | collective-permute-start | bytes 776 | tf_op jit(solution)/shard_map/ppermute | solution.py:39
  15.3 7.4 %collective-permute-start.3 = (f32[2,64,1]{2,1,0:T(8,128)S(1)}, f32[2,64,1]{2,1,0:T(8,128)S(1)}, u32[]{:S(2)}, u32[]{:S(2)}) collective-permute-start(f32[2,64,1]{2,1,0:T(8,128)S(1)} %get-tuple-element.127), channel_id=1, source_target_pairs={{0,1},{1,2},{2,3},{4,5},{5,6},{6,7},{8,9},{9,10},{10,11},{12,13},{... | collective-permute-start | bytes 1544 | tf_op jit(solution)/shard_map/ppermute | solution.py:39
  30.0 1.3 pad_multiply_fusion.7
  36.8 2.0 select_select_fusion.rhs_ref
  40.8 3.1 %collective-permute-start.1 = (f32[1,64,256]{2,1,0:T(8,128)S(1)}, f32[1,64,256]{2,1,0:T(8,128)S(1)}, u32[]{:S(2)}, u32[]{:S(2)}) collective-permute-start(f32[1,64,256]{2,1,0:T(8,128)S(1)} %get-tuple-element.125), channel_id=1, source_target_pairs={{0,4},{1,5},{2,6},{3,7},{4,8},{5,9},{6,10},{7,11},{8,12},{9,13},{1... | collective-permute-start | bytes 196616 | tf_op jit(solution)/shard_map/ppermute | solution.py:39
  43.9 1.9 collective-permute-start.6
  45.9 3.6 %collective-permute-done.6 = f32[1,64,256]{2,1,0:T(8,128)S(1)} collective-permute-done((f32[1,64,256]{2,1,0:T(8,128)S(1)}, f32[1,64,256]{2,1,0:T(8,128)S(1)}, u32[]{:S(2)}, u32[]{:S(2)}) %collective-permute-start.6) | collective-permute-done | bytes 65568 | tf_op jit(solution)/shard_map/ppermute | solution.py:39
  51.6 20.3 %all-to-all-start = ((f32[2,128,128]{2,0,1:T(2,128)}), f32[2,128,128]{2,0,1:T(2,128)S(1)}, u32[]{:S(2)}, u32[]{:S(2)}) async-start(f32[2,128,128]{2,0,1:T(2,128)} %copy.415), calls=%async_computation | async-start | bytes 262144 | tf_op jit(solution)/shard_map/all_to_all | solution.py:334
  74.4 2.6 %shard_map.47 = f32[256,128]{1,0:T(8,128)} custom-call(f32[256,128]{1,0:T(8,128)} %broadcast_in_dim.181.lower_ref, f32[256,128]{1,0:T(8,128)} %copy.487.main_ref, f32[256,128]{1,0:T(8,128)} %broadcast_in_dim.185.upper_ref, f32[256,128]{1,0:T(8,128)} %select_select_fusion.rhs_ref), custom_call_target="tpu_custom_call" | custom-call | tf_op jit(solution)/shard_map/pallas_call | solution.py:256
  78.8 4.2 %all-to-all-done = f32[2,128,128]{2,0,1:T(2,128)S(1)} async-done(((f32[2,128,128]{2,0,1:T(2,128)}), f32[2,128,128]{2,0,1:T(2,128)S(1)}, u32[]{:S(2)}, u32[]{:S(2)}) %all-to-all-start) | async-done | bytes 131104 | tf_op jit(solution)/shard_map/all_to_all | solution.py:334
  85.7 8.2 %all-to-all-start.1 = ((f32[128,2,128]{2,1,0:T(2,128)}), f32[128,2,128]{2,1,0:T(2,128)S(1)}, u32[]{:S(2)}, u32[]{:S(2)}) async-start(f32[128,2,128]{2,1,0:T(2,128)} %copy.428), calls=%async_computation.1 | async-start | bytes 262144 | tf_op jit(solution)/shard_map/all_to_all | solution.py:354
  97.7 7.4 %all-to-all-done.1 = f32[128,2,128]{2,1,0:T(2,128)S(1)} async-done(((f32[128,2,128]{2,1,0:T(2,128)}), f32[128,2,128]{2,1,0:T(2,128)S(1)}, u32[]{:S(2)}, u32[]{:S(2)}) %all-to-all-start.1) | async-done | bytes 131104 | tf_op jit(solution)/shard_map/all_to_all | solution.py:354
  105.9 2.6 %shard_map.46 = f32[256,128]{1,0:T(8,128)} custom-call(f32[256,128]{1,0:T(8,128)} %broadcast_in_dim.181.lower_ref, f32[256,128]{1,0:T(8,128)} %copy.487.main_ref, f32[256,128]{1,0:T(8,128)} %broadcast_in_dim.185.upper_ref, f32[256,128]{1,0:T(8,128)} %copy.431.rhs_ref), custom_call_target="tpu_custom_call" | custom-call | tf_op jit(solution)/shard_map/pallas_call | solution.py:256
  110.1 11.3 %shard_map.48 = f32[4,8,64]{2,1,0:T(8,128)} custom-call(f32[8,64]{1,0:T(8,128)} %concatenate.407.ends_ref), custom_call_target="tpu_custom_call" | custom-call | tf_op jit(solution)/shard_map/pallas_call | solution.py:292
  126.0 3.3 %collective-permute-start.9 = (f32[1,64,256]{2,1,0:T(8,128)S(1)}, f32[1,64,256]{2,1,0:T(8,128)S(1)}, u32[]{:S(2)}, u32[]{:S(2)}) collective-permute-start(f32[1,64,256]{2,1,0:T(8,128)S(1)} %copy.456), channel_id=1, source_target_pairs={{0,4},{1,5},{2,6},{3,7},{4,8},{5,9},{6,10},{7,11},{8,12},{9,13},{1... | collective-permute-start | bytes 196616 | tf_op jit(solution)/shard_map/ppermute | solution.py:39
  131.0 1.9 collective-permute-start.14
  133.0 4.5 %collective-permute-start.13 = (f32[1,64,1]{2,1,0:T(8,128)S(1)}, f32[1,64,1]{2,1,0:T(8,128)S(1)}, u32[]{:S(2)}, u32[]{:S(2)}) collective-permute-start(f32[1,64,1]{2,1,0:T(8,128)S(1)} %get-tuple-element.131), channel_id=1, source_target_pairs={{4,1},{5,2},{6,3},{8,5},{9,6},{10,7},{12,9},{13,10},{14,11},{16,13... | collective-permute-start | bytes 776 | tf_op jit(solution)/shard_map/ppermute | solution.py:39
  138.8 5.9 %collective-permute-start.11 = (f32[2,64,1]{2,1,0:T(8,128)S(1)}, f32[2,64,1]{2,1,0:T(8,128)S(1)}, u32[]{:S(2)}, u32[]{:S(2)}) collective-permute-start(f32[2,64,1]{2,1,0:T(8,128)S(1)} %get-tuple-element.115), channel_id=1, source_target_pairs={{0,1},{1,2},{2,3},{4,5},{5,6},{6,7},{8,9},{9,10},{10,11},{12,13},{... | collective-permute-start | bytes 1544 | tf_op jit(solution)/shard_map/ppermute | solution.py:39
  146.3 7.3 %collective-permute-start.8 = (f32[1,64,1]{2,1,0:T(8,128)S(1)}, f32[1,64,1]{2,1,0:T(8,128)S(1)}, u32[]{:S(2)}, u32[]{:S(2)}) collective-permute-start(f32[1,64,1]{2,1,0:T(8,128)S(1)} %get-tuple-element.129), channel_id=1, source_target_pairs={{0,5},{1,6},{2,7},{4,9},{5,10},{6,11},{8,13},{9,14},{10,15},{12,17... | collective-permute-start | bytes 776 | tf_op jit(solution)/shard_map/ppermute | solution.py:39
  156.1 24.5 %all_to_all.64 = f32[2,128,128]{2,0,1:T(2,128)S(1)} all-to-all(f32[2,128,128]{2,0,1:T(2,128)S(1)} %copy.472), channel_id=1, replica_groups=mesh['spot'=128,'var'=4] {'spot'}, dimensions={1} | all-to-all | bytes 262144 | tf_op jit(solution)/shard_map/all_to_all | solution.py:334
  181.5 16.4 %all_to_all.65 = f32[128,2,128]{2,1,0:T(2,128)S(1)} all-to-all(f32[128,2,128]{2,1,0:T(2,128)S(1)} %copy.485), channel_id=1, replica_groups=mesh['spot'=128,'var'=4] {'spot'}, dimensions={0} | all-to-all | bytes 262144 | tf_op jit(solution)/shard_map/all_to_all | solution.py:354
  198.7 2.6 %shard_map.49 = f32[256,128]{1,0:T(8,128)} custom-call(f32[256,128]{1,0:T(8,128)} %broadcast_in_dim.181.lower_ref, f32[256,128]{1,0:T(8,128)} %copy.487.main_ref, f32[256,128]{1,0:T(8,128)} %broadcast_in_dim.185.upper_ref, f32[256,128]{1,0:T(8,128)} %copy.488.rhs_ref), custom_call_target="tpu_custom_call" | custom-call | tf_op jit(solution)/shard_map/pallas_call | solution.py:256
  202.8 12.5 %shard_map.50 = f32[4,8,64]{2,1,0:T(8,128)} custom-call(f32[8,64]{1,0:T(8,128)} %concatenate.455.ends_ref), custom_call_target="tpu_custom_call" | custom-call | tf_op jit(solution)/shard_map/pallas_call | solution.py:292
  (488 shorter events, 48.8 us)
Async XLA Ops:
  0.0 15.2 %copy-start = (f32[2,64,256]{2,1,0:T(8,128)S(1)}, f32[2,64,256]{2,1,0:T(8,128)}, u32[]{:S(2)}) copy-start(f32[2,64,256]{2,1,0:T(8,128)} %param.6) | copy-start | bytes 393220
  0.9 38.5 %collective-permute-start = (f32[1,64,1]{2,1,0:T(8,128)S(1)}, f32[1,64,1]{2,1,0:T(8,128)S(1)}, u32[]{:S(2)}, u32[]{:S(2)}) collective-permute-start(f32[1,64,1]{2,1,0:T(8,128)S(1)} %get-tuple-element.121), channel_id=1, source_target_pairs={{0,5},{1,6},{2,7},{4,9},{5,10},{6,11},{8,13},{9,14},{10,15},{12,17... | collective-permute-start | bytes 776 | tf_op jit(solution)/shard_map/ppermute | solution.py:39
  7.5 33.3 %collective-permute-start.2 = (f32[1,64,1]{2,1,0:T(8,128)S(1)}, f32[1,64,1]{2,1,0:T(8,128)S(1)}, u32[]{:S(2)}, u32[]{:S(2)}) collective-permute-start(f32[1,64,1]{2,1,0:T(8,128)S(1)} %get-tuple-element.124), channel_id=1, source_target_pairs={{1,4},{2,5},{3,6},{5,8},{6,9},{7,10},{9,12},{10,13},{11,14},{13,16... | collective-permute-start | bytes 776 | tf_op jit(solution)/shard_map/ppermute | solution.py:39
  8.8 35.1 %collective-permute-start.5 = (f32[1,64,1]{2,1,0:T(8,128)S(1)}, f32[1,64,1]{2,1,0:T(8,128)S(1)}, u32[]{:S(2)}, u32[]{:S(2)}) collective-permute-start(f32[1,64,1]{2,1,0:T(8,128)S(1)} %get-tuple-element.122), channel_id=1, source_target_pairs={{4,1},{5,2},{6,3},{8,5},{9,6},{10,7},{12,9},{13,10},{14,11},{16,13... | collective-permute-start | bytes 776 | tf_op jit(solution)/shard_map/ppermute | solution.py:39
  13.9 31.9 %collective-permute-start.7 = (f32[1,64,1]{2,1,0:T(8,128)S(1)}, f32[1,64,1]{2,1,0:T(8,128)S(1)}, u32[]{:S(2)}, u32[]{:S(2)}) collective-permute-start(f32[1,64,1]{2,1,0:T(8,128)S(1)} %get-tuple-element.123), channel_id=1, source_target_pairs={{5,0},{6,1},{7,2},{9,4},{10,5},{11,6},{13,8},{14,9},{15,10},{17,12... | collective-permute-start | bytes 776 | tf_op jit(solution)/shard_map/ppermute | solution.py:39
  15.3 7.4 %copy-start.4 = (s32[64]{0:T(128)S(1)}, s32[64]{0:T(128)}, u32[]{:S(2)}) copy-start(s32[64]{0:T(128)} %param.9) | copy-start | bytes 772
  15.3 30.5 %collective-permute-start.3 = (f32[2,64,1]{2,1,0:T(8,128)S(1)}, f32[2,64,1]{2,1,0:T(8,128)S(1)}, u32[]{:S(2)}, u32[]{:S(2)}) collective-permute-start(f32[2,64,1]{2,1,0:T(8,128)S(1)} %get-tuple-element.127), channel_id=1, source_target_pairs={{0,1},{1,2},{2,3},{4,5},{5,6},{6,7},{8,9},{9,10},{10,11},{12,13},{... | collective-permute-start | bytes 1544 | tf_op jit(solution)/shard_map/ppermute | solution.py:39
  27.1 0.7 copy-start.2
  32.6 0.7 copy-start.3
  39.5 6.4 %collective-permute-start.4 = (f32[2,64,1]{2,1,0:T(8,128)S(1)}, f32[2,64,1]{2,1,0:T(8,128)S(1)}, u32[]{:S(2)}, u32[]{:S(2)}) collective-permute-start(f32[2,64,1]{2,1,0:T(8,128)S(1)} %get-tuple-element.128), channel_id=1, source_target_pairs={{1,0},{2,1},{3,2},{5,4},{6,5},{7,6},{9,8},{10,9},{11,10},{13,12},{... | collective-permute-start | bytes 1544 | tf_op jit(solution)/shard_map/ppermute | solution.py:39
  40.8 5.1 %collective-permute-start.1 = (f32[1,64,256]{2,1,0:T(8,128)S(1)}, f32[1,64,256]{2,1,0:T(8,128)S(1)}, u32[]{:S(2)}, u32[]{:S(2)}) collective-permute-start(f32[1,64,256]{2,1,0:T(8,128)S(1)} %get-tuple-element.125), channel_id=1, source_target_pairs={{0,4},{1,5},{2,6},{3,7},{4,8},{5,9},{6,10},{7,11},{8,12},{9,13},{1... | collective-permute-start | bytes 196616 | tf_op jit(solution)/shard_map/ppermute | solution.py:39
  43.9 5.6 %collective-permute-start.6 = (f32[1,64,256]{2,1,0:T(8,128)S(1)}, f32[1,64,256]{2,1,0:T(8,128)S(1)}, u32[]{:S(2)}, u32[]{:S(2)}) collective-permute-start(f32[1,64,256]{2,1,0:T(8,128)S(1)} %get-tuple-element.126), channel_id=1, source_target_pairs={{4,0},{5,1},{6,2},{7,3},{8,4},{9,5},{10,6},{11,7},{12,8},{13,9},{1... | collective-permute-start | bytes 196616 | tf_op jit(solution)/shard_map/ppermute | solution.py:39
  51.6 31.4 %all-to-all-start = ((f32[2,128,128]{2,0,1:T(2,128)}), f32[2,128,128]{2,0,1:T(2,128)S(1)}, u32[]{:S(2)}, u32[]{:S(2)}) async-start(f32[2,128,128]{2,0,1:T(2,128)} %copy.415), calls=%async_computation | async-start | bytes 262144 | tf_op jit(solution)/shard_map/all_to_all | solution.py:334
  85.7 19.4 %all-to-all-start.1 = ((f32[128,2,128]{2,1,0:T(2,128)}), f32[128,2,128]{2,1,0:T(2,128)S(1)}, u32[]{:S(2)}, u32[]{:S(2)}) async-start(f32[128,2,128]{2,1,0:T(2,128)} %copy.428), calls=%async_computation.1 | async-start | bytes 262144 | tf_op jit(solution)/shard_map/all_to_all | solution.py:354
  108.5 14.3 %copy-start.1 = (f32[256,128]{1,0:T(8,128)S(1)}, f32[256,128]{1,0:T(8,128)}, u32[]{:S(2)}) copy-start(f32[256,128]{1,0:T(8,128)} %shard_map.46) | copy-start | bytes 393220
  126.0 28.6 %collective-permute-start.9 = (f32[1,64,256]{2,1,0:T(8,128)S(1)}, f32[1,64,256]{2,1,0:T(8,128)S(1)}, u32[]{:S(2)}, u32[]{:S(2)}) collective-permute-start(f32[1,64,256]{2,1,0:T(8,128)S(1)} %copy.456), channel_id=1, source_target_pairs={{0,4},{1,5},{2,6},{3,7},{4,8},{5,9},{6,10},{7,11},{8,12},{9,13},{1... | collective-permute-start | bytes 196616 | tf_op jit(solution)/shard_map/ppermute | solution.py:39
  129.6 9.2 %collective-permute-start.10 = (f32[1,64,1]{2,1,0:T(8,128)S(1)}, f32[1,64,1]{2,1,0:T(8,128)S(1)}, u32[]{:S(2)}, u32[]{:S(2)}) collective-permute-start(f32[1,64,1]{2,1,0:T(8,128)S(1)} %get-tuple-element.130), channel_id=1, source_target_pairs={{1,4},{2,5},{3,6},{5,8},{6,9},{7,10},{9,12},{10,13},{11,14},{13,16... | collective-permute-start | bytes 776 | tf_op jit(solution)/shard_map/ppermute | solution.py:39
  131.0 23.7 %collective-permute-start.14 = (f32[1,64,256]{2,1,0:T(8,128)S(1)}, f32[1,64,256]{2,1,0:T(8,128)S(1)}, u32[]{:S(2)}, u32[]{:S(2)}) collective-permute-start(f32[1,64,256]{2,1,0:T(8,128)S(1)} %copy.467), channel_id=1, source_target_pairs={{4,0},{5,1},{6,2},{7,3},{8,4},{9,5},{10,6},{11,7},{12,8},{13,9},{1... | collective-permute-start | bytes 196616 | tf_op jit(solution)/shard_map/ppermute | solution.py:39
  133.0 11.8 %collective-permute-start.13 = (f32[1,64,1]{2,1,0:T(8,128)S(1)}, f32[1,64,1]{2,1,0:T(8,128)S(1)}, u32[]{:S(2)}, u32[]{:S(2)}) collective-permute-start(f32[1,64,1]{2,1,0:T(8,128)S(1)} %get-tuple-element.131), channel_id=1, source_target_pairs={{4,1},{5,2},{6,3},{8,5},{9,6},{10,7},{12,9},{13,10},{14,11},{16,13... | collective-permute-start | bytes 776 | tf_op jit(solution)/shard_map/ppermute | solution.py:39
  137.5 8.8 %collective-permute-start.15 = (f32[1,64,1]{2,1,0:T(8,128)S(1)}, f32[1,64,1]{2,1,0:T(8,128)S(1)}, u32[]{:S(2)}, u32[]{:S(2)}) collective-permute-start(f32[1,64,1]{2,1,0:T(8,128)S(1)} %get-tuple-element.132), channel_id=1, source_target_pairs={{5,0},{6,1},{7,2},{9,4},{10,5},{11,6},{13,8},{14,9},{15,10},{17,12... | collective-permute-start | bytes 776 | tf_op jit(solution)/shard_map/ppermute | solution.py:39
  138.8 15.8 %collective-permute-start.11 = (f32[2,64,1]{2,1,0:T(8,128)S(1)}, f32[2,64,1]{2,1,0:T(8,128)S(1)}, u32[]{:S(2)}, u32[]{:S(2)}) collective-permute-start(f32[2,64,1]{2,1,0:T(8,128)S(1)} %get-tuple-element.115), channel_id=1, source_target_pairs={{0,1},{1,2},{2,3},{4,5},{5,6},{6,7},{8,9},{9,10},{10,11},{12,13},{... | collective-permute-start | bytes 1544 | tf_op jit(solution)/shard_map/ppermute | solution.py:39
  144.7 9.9 %collective-permute-start.12 = (f32[2,64,1]{2,1,0:T(8,128)S(1)}, f32[2,64,1]{2,1,0:T(8,128)S(1)}, u32[]{:S(2)}, u32[]{:S(2)}) collective-permute-start(f32[2,64,1]{2,1,0:T(8,128)S(1)} %get-tuple-element.116), channel_id=1, source_target_pairs={{1,0},{2,1},{3,2},{5,4},{6,5},{7,6},{9,8},{10,9},{11,10},{13,12},{... | collective-permute-start | bytes 1544 | tf_op jit(solution)/shard_map/ppermute | solution.py:39
  146.3 8.3 %collective-permute-start.8 = (f32[1,64,1]{2,1,0:T(8,128)S(1)}, f32[1,64,1]{2,1,0:T(8,128)S(1)}, u32[]{:S(2)}, u32[]{:S(2)}) collective-permute-start(f32[1,64,1]{2,1,0:T(8,128)S(1)} %get-tuple-element.129), channel_id=1, source_target_pairs={{0,5},{1,6},{2,7},{4,9},{5,10},{6,11},{8,13},{9,14},{10,15},{12,17... | collective-permute-start | bytes 776 | tf_op jit(solution)/shard_map/ppermute | solution.py:39

commit v5 on v3

--- a/solution.py
+++ b/solution.py
@@ -252,24 +252,33 @@
         peer = lax.rem(me + shift, blocks)
         pl.semaphore_signal(barrier, inc=1, device_id=(spot, peer), device_id_type=pl.DeviceIdType.MESH)
     pl.semaphore_wait(barrier, blocks - 1)
-    copies = []
+    sends = []
     for shift in range(1, blocks):
         peer = lax.rem(me + shift, blocks)
         copy = pltpu.make_async_remote_copy(
             src_ref=ends_ref,
-            dst_ref=landed.at[shift - 1],
+            dst_ref=landed.at[me],
             send_sem=send_sem.at[shift - 1],
-            recv_sem=recv_sem.at[shift - 1],
+            recv_sem=recv_sem.at[me],
             device_id=(spot, peer),
             device_id_type=pl.DeviceIdType.MESH,
         )
         copy.start()
-        copies.append(copy)
-    out_ref[0] = ends_ref[...]
-    for copy in copies:
-        copy.wait()
+        sends.append(copy)
+    out_ref[me] = ends_ref[...]
+    for copy in sends:
+        copy.wait_send()
     for shift in range(1, blocks):
-        out_ref[shift] = landed[shift - 1]
+        source = lax.rem(me + blocks - shift, blocks)
+        pltpu.make_async_remote_copy(
+            src_ref=ends_ref,
+            dst_ref=landed.at[source],
+            send_sem=send_sem.at[shift - 1],
+            recv_sem=recv_sem.at[source],
+            device_id=(spot, source),
+            device_id_type=pl.DeviceIdType.MESH,
+        ).wait_recv()
+        out_ref[source] = landed[source]
 
 
 def gather_var(ends, blocks):
@@ -277,9 +286,9 @@
         functools.partial(gather_kernel, blocks),
         out_shape=jax.ShapeDtypeStruct((blocks,) + ends.shape, jnp.float32),
         scratch_shapes=[
-            pltpu.VMEM((blocks - 1,) + ends.shape, jnp.float32),
+            pltpu.VMEM((blocks,) + ends.shape, jnp.float32),
             pltpu.SemaphoreType.DMA((blocks - 1,)),
-            pltpu.SemaphoreType.DMA((blocks - 1,)),
+            pltpu.SemaphoreType.DMA((blocks,)),
         ],
         compiler_params=pltpu.CompilerParams(collective_id=0, has_side_effects=True),
     )(ends)
@@ -416,11 +425,6 @@
             lax.dynamic_index_in_dim(right, var_place, 0, keepdims=False),
         )
 
-    def gather_ends(ends):
-        stacked = gather_var(ends, blocks)
-        order = (var_place - jnp.arange(blocks)) % blocks
-        return jnp.take(stacked, order, axis=0)
-
     def var_solve(values):
         line_count = spot_rows * planes
         lines = values.transpose(2, 0, 1).reshape(var_cols, line_count)
@@ -434,7 +438,7 @@
         message = jnp.concatenate(
             [local[0], local[var_cols - 1], column_ends], axis=0
         )
-        ends = gather_ends(message)
+        ends = gather_var(message, blocks)
         left, right = interface_solve(
             ends[:, :spot_rows],
             ends[:, spot_rows : 2 * spot_rows],

time: 194 us -> 200 us (1.031)
  other arithmetic: 14.3 us -> 18.7 us
  waiting for transfers between devices: 28.8 us -> 32.5 us
  starting transfers between devices: 48 us -> 45.4 us
    all_to_all x1, waiting for transfers between devices: 4.21 us -> 8.97 us  [spot_solve(): lax.all_to_all(values.reshape(spot_rows, line_count), 'spot', split_axis=...]
    sub x4, other arithmetic: 0.06 us -> 3.35 us  [interface_solve(): matrix[i][c] = -update if matrix[i][c] is None else matrix[i][c] - update]
    all_to_all x1, starting transfers between devices: 8.23 us -> 5.59 us  [spot_solve(): lax.all_to_all(solved, 'spot', split_axis=0, concat_axis=1, tiled=True)]
    gather x2 -> x0, local copies, waits for them, and re-layouts: 2.53 us -> none  [gather_ends(): return jnp.take(stacked, order, axis=0)]
where the time goes in v5:
time: 200 us; the launch traced here: 198 us
  starting transfers between devices  45.4 us (23%)
  blocking collectives  39.8 us (20%)
  waiting for transfers between devices  32.5 us (16%)
  local copies, waits for them, and re-layouts  29.5 us (15%)
  Pallas kernels  26.5 us (13%)
  other arithmetic  18.7 us (9%)
  between operations  5.72 us (3%)
    all_to_all x1, blocking collectives, spot_solve(): lax.all_to_all(values.reshape(spot_rows, line_count), 'spot', split_axis=...  23.5 us
    pallas_call x2, Pallas kernels, gather_var(): pl.pallas_call(functools.partial(gather_kernel, blocks), out_shape=jax.Sh...  18.6 us
    all_to_all x1, blocking collectives, spot_solve(): lax.all_to_all(solved, 'spot', split_axis=0, concat_axis=1, tiled=True)  16.4 us
    all_to_all x1, starting transfers between devices, spot_solve(): lax.all_to_all(values.reshape(spot_rows, line_count), 'spot', split_axis=...  15.6 us
    ppermute x4, waiting for transfers between devices, padded_2(): after = lax.ppermute(initial, axis, down)  15.3 us
    ppermute x4, starting transfers between devices, padded_2(): after = lax.ppermute(initial, axis, down)  13.3 us
    ppermute x4, starting transfers between devices, padded_2(): before = lax.ppermute(last, axis, up)  10.9 us
    all_to_all x1, waiting for transfers between devices, spot_solve(): lax.all_to_all(values.reshape(spot_rows, line_count), 'spot', split_axis=...  8.97 us
  transfers between devices with their start and end apart: 10, of which 7 were waited for; matrix products, arithmetic and copies ran while one was open for 10% of the time, Pallas kernels for 1%

profile of v5, /device:TPU:1, one launch (start us, length us, event | category | flops | bytes accessed | tf_op | source)
XLA Modules:
  0.0 198.3 jit_solution(10255560589340475162)
XLA Ops:
  0.9 8.8 %collective-permute-start.1 = (f32[1,64,256]{2,1,0:T(8,128)S(1)}, f32[1,64,256]{2,1,0:T(8,128)S(1)}, u32[]{:S(2)}, u32[]{:S(2)}) collective-permute-start(f32[1,64,256]{2,1,0:T(8,128)S(1)} %get-tuple-element.120), channel_id=1, source_target_pairs={{4,0},{8,4},{12,8},{16,12},{20,16},{24,20},{28,24},{32,28},{36,32}... | collective-permute-start | bytes 196616 | tf_op jit(solution)/shard_map/ppermute | solution.py:39
  9.7 1.9 collective-permute-start
  22.6 2.0 %select_select_fusion.rhs_ref = f32[256,128]{1,0:T(8,128)} fusion(f32[]{:T(128)} %bitcast.35, f32[]{:T(128)} %bitcast.34, pred[128]{0:T(512)(128)(4,1)S(1)} %iota.36, pred[128]{0:T(512)(128)(4,1)S(1)} %iota.30, pred[256]{0:T(512)(128)(4,1)S(1)} %get-tuple-element.268, pred[256]{0:T(512)(128)(4,1)S(1)} %get-tuple-element.269), kind=kLoop, calls=%fused_computation.151 | loop fusion | flops 131072 | bytes 131848 | tf_op jit(solution)/shard_map/jit(_where)/select_n | solution.py:372
  26.2 2.6 %shard_map.47 = f32[256,128]{1,0:T(8,128)} custom-call(f32[256,128]{1,0:T(8,128)} %broadcast_in_dim.172.lower_ref, f32[256,128]{1,0:T(8,128)} %copy.463.main_ref, f32[256,128]{1,0:T(8,128)} %broadcast_in_dim.176.upper_ref, f32[256,128]{1,0:T(8,128)} %select_select_fusion.rhs_ref), custom_call_target="tpu_custom_call" | custom-call | tf_op jit(solution)/shard_map/pallas_call | solution.py:240
  33.1 1.3 collective-permute-start.2
  34.4 1.3 collective-permute-start.3
  37.1 6.8 %collective-permute-done.3 = f32[4,64,1]{2,1,0:T(8,128)S(1)} collective-permute-done((f32[4,64,1]{2,1,0:T(8,128)S(1)}, f32[4,64,1]{2,1,0:T(8,128)S(1)}, u32[]{:S(2)}, u32[]{:S(2)}) %collective-permute-start.3) | collective-permute-done | bytes 1056 | tf_op jit(solution)/shard_map/ppermute | solution.py:39
  45.8 15.6 %all-to-all-start = ((f32[2,128,128]{2,0,1:T(2,128)}), f32[2,128,128]{2,0,1:T(2,128)S(1)}, u32[]{:S(2)}, u32[]{:S(2)}) async-start(f32[2,128,128]{2,0,1:T(2,128)} %copy.397), calls=%async_computation | async-start | bytes 262144 | tf_op jit(solution)/shard_map/all_to_all | solution.py:327
  63.7 9.0 %all-to-all-done = f32[2,128,128]{2,0,1:T(2,128)S(1)} async-done(((f32[2,128,128]{2,0,1:T(2,128)}), f32[2,128,128]{2,0,1:T(2,128)S(1)}, u32[]{:S(2)}, u32[]{:S(2)}) %all-to-all-start) | async-done | bytes 131104 | tf_op jit(solution)/shard_map/all_to_all | solution.py:327
  75.3 5.6 %all-to-all-start.1 = ((f32[128,2,128]{2,1,0:T(2,128)}), f32[128,2,128]{2,1,0:T(2,128)S(1)}, u32[]{:S(2)}, u32[]{:S(2)}) async-start(f32[128,2,128]{2,1,0:T(2,128)} %copy.410), calls=%async_computation.1 | async-start | bytes 262144 | tf_op jit(solution)/shard_map/all_to_all | solution.py:347
  85.3 6.8 %all-to-all-done.1 = f32[128,2,128]{2,1,0:T(2,128)S(1)} async-done(((f32[128,2,128]{2,1,0:T(2,128)}), f32[128,2,128]{2,1,0:T(2,128)S(1)}, u32[]{:S(2)}, u32[]{:S(2)}) %all-to-all-start.1) | async-done | bytes 131104 | tf_op jit(solution)/shard_map/all_to_all | solution.py:347
  93.0 2.6 %shard_map.46 = f32[256,128]{1,0:T(8,128)} custom-call(f32[256,128]{1,0:T(8,128)} %broadcast_in_dim.172.lower_ref, f32[256,128]{1,0:T(8,128)} %copy.463.main_ref, f32[256,128]{1,0:T(8,128)} %broadcast_in_dim.176.upper_ref, f32[256,128]{1,0:T(8,128)} %copy.413.rhs_ref), custom_call_target="tpu_custom_call" | custom-call | tf_op jit(solution)/shard_map/pallas_call | solution.py:240
  98.1 10.2 %shard_map.48 = f32[4,8,64]{2,1,0:T(8,128)} custom-call(f32[8,64]{1,0:T(8,128)} %concatenate.393.ends_ref), custom_call_target="tpu_custom_call" | custom-call | tf_op jit(solution)/shard_map/pallas_call | solution.py:285
  112.4 1.3 divide_bitcast_fusion.20
  114.6 3.7 %collective-permute-start.4 = (f32[1,64,256]{2,1,0:T(8,128)S(1)}, f32[1,64,256]{2,1,0:T(8,128)S(1)}, u32[]{:S(2)}, u32[]{:S(2)}) collective-permute-start(f32[1,64,256]{2,1,0:T(8,128)S(1)} %copy.438), channel_id=1, source_target_pairs={{0,4},{4,8},{8,12},{12,16},{16,20},{20,24},{24,28},{28,32},{32,36}... | collective-permute-start | bytes 196616 | tf_op jit(solution)/shard_map/ppermute | solution.py:38
  118.5 1.9 collective-permute-start.5
  120.5 3.6 %collective-permute-done.5 = f32[1,64,256]{2,1,0:T(8,128)S(1)} collective-permute-done((f32[1,64,256]{2,1,0:T(8,128)S(1)}, f32[1,64,256]{2,1,0:T(8,128)S(1)}, u32[]{:S(2)}, u32[]{:S(2)}) %collective-permute-start.5) | collective-permute-done | bytes 65568 | tf_op jit(solution)/shard_map/ppermute | solution.py:39
  124.2 3.9 %collective-permute-start.6 = (f32[4,64,1]{2,1,0:T(8,128)S(1)}, f32[4,64,1]{2,1,0:T(8,128)S(1)}, u32[]{:S(2)}, u32[]{:S(2)}) collective-permute-start(f32[4,64,1]{2,1,0:T(8,128)S(1)} %get-tuple-element.110), channel_id=1, source_target_pairs={{0,1},{1,2},{2,3},{4,5},{5,6},{6,7},{8,9},{9,10},{10,11},{12,13},{... | collective-permute-start | bytes 3080 | tf_op jit(solution)/shard_map/ppermute | solution.py:38
  128.2 1.3 collective-permute-start.7
  130.1 4.9 %collective-permute-done.7 = f32[4,64,1]{2,1,0:T(8,128)S(1)} collective-permute-done((f32[4,64,1]{2,1,0:T(8,128)S(1)}, f32[4,64,1]{2,1,0:T(8,128)S(1)}, u32[]{:S(2)}, u32[]{:S(2)}) %collective-permute-start.7) | collective-permute-done | bytes 1056 | tf_op jit(solution)/shard_map/ppermute | solution.py:39
  136.1 23.5 %all_to_all.64 = f32[2,128,128]{2,0,1:T(2,128)S(1)} all-to-all(f32[2,128,128]{2,0,1:T(2,128)S(1)} %copy.448), channel_id=1, replica_groups=mesh['spot'=128,'var'=4] {'spot'}, dimensions={1} | all-to-all | bytes 262144 | tf_op jit(solution)/shard_map/all_to_all | solution.py:327
  160.6 16.4 %all_to_all.65 = f32[128,2,128]{2,1,0:T(2,128)S(1)} all-to-all(f32[128,2,128]{2,1,0:T(2,128)S(1)} %copy.461), channel_id=1, replica_groups=mesh['spot'=128,'var'=4] {'spot'}, dimensions={0} | all-to-all | bytes 262144 | tf_op jit(solution)/shard_map/all_to_all | solution.py:347
  177.8 2.6 %shard_map.49 = f32[256,128]{1,0:T(8,128)} custom-call(f32[256,128]{1,0:T(8,128)} %broadcast_in_dim.172.lower_ref, f32[256,128]{1,0:T(8,128)} %copy.463.main_ref, f32[256,128]{1,0:T(8,128)} %broadcast_in_dim.176.upper_ref, f32[256,128]{1,0:T(8,128)} %copy.464.rhs_ref), custom_call_target="tpu_custom_call" | custom-call | tf_op jit(solution)/shard_map/pallas_call | solution.py:240
  182.9 8.5 %shard_map.50 = f32[4,8,64]{2,1,0:T(8,128)} custom-call(f32[8,64]{1,0:T(8,128)} %concatenate.439.ends_ref), custom_call_target="tpu_custom_call" | custom-call | tf_op jit(solution)/shard_map/pallas_call | solution.py:285
  (463 shorter events, 46.4 us)
Async XLA Ops:
  0.9 32.1 %collective-permute-start.1 = (f32[1,64,256]{2,1,0:T(8,128)S(1)}, f32[1,64,256]{2,1,0:T(8,128)S(1)}, u32[]{:S(2)}, u32[]{:S(2)}) collective-permute-start(f32[1,64,256]{2,1,0:T(8,128)S(1)} %get-tuple-element.120), channel_id=1, source_target_pairs={{4,0},{8,4},{12,8},{16,12},{20,16},{24,20},{28,24},{32,28},{36,32}... | collective-permute-start | bytes 196616 | tf_op jit(solution)/shard_map/ppermute | solution.py:39
  9.7 22.6 %collective-permute-start = (f32[1,64,256]{2,1,0:T(8,128)S(1)}, f32[1,64,256]{2,1,0:T(8,128)S(1)}, u32[]{:S(2)}, u32[]{:S(2)}) collective-permute-start(f32[1,64,256]{2,1,0:T(8,128)S(1)} %get-tuple-element.121), channel_id=1, source_target_pairs={{0,4},{4,8},{8,12},{12,16},{16,20},{20,24},{24,28},{28,32},{32,36}... | collective-permute-start | bytes 196616 | tf_op jit(solution)/shard_map/ppermute | solution.py:38
  11.6 0.7 copy-start.3
  16.3 0.7 copy-start.1
  17.4 0.7 copy-start.2
  32.0 0.9 copy-start
  33.1 4.0 %collective-permute-start.2 = (f32[4,64,1]{2,1,0:T(8,128)S(1)}, f32[4,64,1]{2,1,0:T(8,128)S(1)}, u32[]{:S(2)}, u32[]{:S(2)}) collective-permute-start(f32[4,64,1]{2,1,0:T(8,128)S(1)} %get-tuple-element.112), channel_id=1, source_target_pairs={{0,1},{1,2},{2,3},{4,5},{5,6},{6,7},{8,9},{9,10},{10,11},{12,13},{... | collective-permute-start | bytes 3080 | tf_op jit(solution)/shard_map/ppermute | solution.py:38
  34.4 9.5 %collective-permute-start.3 = (f32[4,64,1]{2,1,0:T(8,128)S(1)}, f32[4,64,1]{2,1,0:T(8,128)S(1)}, u32[]{:S(2)}, u32[]{:S(2)}) collective-permute-start(f32[4,64,1]{2,1,0:T(8,128)S(1)} %get-tuple-element.113), channel_id=1, source_target_pairs={{1,0},{2,1},{3,2},{5,4},{6,5},{7,6},{9,8},{10,9},{11,10},{13,12},{... | collective-permute-start | bytes 3080 | tf_op jit(solution)/shard_map/ppermute | solution.py:39
  45.8 26.8 %all-to-all-start = ((f32[2,128,128]{2,0,1:T(2,128)}), f32[2,128,128]{2,0,1:T(2,128)S(1)}, u32[]{:S(2)}, u32[]{:S(2)}) async-start(f32[2,128,128]{2,0,1:T(2,128)} %copy.397), calls=%async_computation | async-start | bytes 262144 | tf_op jit(solution)/shard_map/all_to_all | solution.py:327
  75.3 16.9 %all-to-all-start.1 = ((f32[128,2,128]{2,1,0:T(2,128)}), f32[128,2,128]{2,1,0:T(2,128)S(1)}, u32[]{:S(2)}, u32[]{:S(2)}) async-start(f32[128,2,128]{2,1,0:T(2,128)} %copy.410), calls=%async_computation.1 | async-start | bytes 262144 | tf_op jit(solution)/shard_map/all_to_all | solution.py:347
  114.6 5.9 %collective-permute-start.4 = (f32[1,64,256]{2,1,0:T(8,128)S(1)}, f32[1,64,256]{2,1,0:T(8,128)S(1)}, u32[]{:S(2)}, u32[]{:S(2)}) collective-permute-start(f32[1,64,256]{2,1,0:T(8,128)S(1)} %copy.438), channel_id=1, source_target_pairs={{0,4},{4,8},{8,12},{12,16},{16,20},{20,24},{24,28},{28,32},{32,36}... | collective-permute-start | bytes 196616 | tf_op jit(solution)/shard_map/ppermute | solution.py:38
  118.5 5.6 %collective-permute-start.5 = (f32[1,64,256]{2,1,0:T(8,128)S(1)}, f32[1,64,256]{2,1,0:T(8,128)S(1)}, u32[]{:S(2)}, u32[]{:S(2)}) collective-permute-start(f32[1,64,256]{2,1,0:T(8,128)S(1)} %copy.441), channel_id=1, source_target_pairs={{4,0},{8,4},{12,8},{16,12},{20,16},{24,20},{28,24},{32,28},{36,32}... | collective-permute-start | bytes 196616 | tf_op jit(solution)/shard_map/ppermute | solution.py:39
  124.2 5.9 %collective-permute-start.6 = (f32[4,64,1]{2,1,0:T(8,128)S(1)}, f32[4,64,1]{2,1,0:T(8,128)S(1)}, u32[]{:S(2)}, u32[]{:S(2)}) collective-permute-start(f32[4,64,1]{2,1,0:T(8,128)S(1)} %get-tuple-element.110), channel_id=1, source_target_pairs={{0,1},{1,2},{2,3},{4,5},{5,6},{6,7},{8,9},{9,10},{10,11},{12,13},{... | collective-permute-start | bytes 3080 | tf_op jit(solution)/shard_map/ppermute | solution.py:38
  128.2 6.8 %collective-permute-start.7 = (f32[4,64,1]{2,1,0:T(8,128)S(1)}, f32[4,64,1]{2,1,0:T(8,128)S(1)}, u32[]{:S(2)}, u32[]{:S(2)}) collective-permute-start(f32[4,64,1]{2,1,0:T(8,128)S(1)} %get-tuple-element.111), channel_id=1, source_target_pairs={{1,0},{2,1},{3,2},{5,4},{6,5},{7,6},{9,8},{10,9},{11,10},{13,12},{... | collective-permute-start | bytes 3080 | tf_op jit(solution)/shard_map/ppermute | solution.py:39

commit v6 on v3

--- a/solution.py
+++ b/solution.py
@@ -448,7 +448,7 @@
             - left.reshape(1, spot_rows, planes) * g_own.reshape(var_cols, 1, planes)
             - right.reshape(1, spot_rows, planes) * h_own.reshape(var_cols, 1, planes)
         )
-        return solved.transpose(1, 2, 0)
+        return solved.transpose(1, 2, 0), left, right
 
     def rate_solve(values):
         diffusion, advection = rate_terms(rate_geo[0])
@@ -457,13 +457,26 @@
         )
         return implicit(system, values, 1)
 
+    def spot_pad(array):
+        devices, rows = lax.axis_size("spot"), array.shape[0]
+        up = [(i, i + 1) for i in range(devices - 1)]
+        down = [(j, i) for i, j in up]
+        before = lax.ppermute(array[rows - 1 : rows], "spot", up)
+        after = lax.ppermute(array[0:1], "spot", down)
+        return jnp.concatenate([before, array, after], axis=0)
+
     z_zero = time_step * edge_terms(option_value, False)
     z_one = spot_solve(z_zero)
-    z_two = var_solve(z_one)
-    z_three = rate_solve(z_two)
-    w_zero = z_zero + half_step * edge_terms(z_three, True)
+    z_two, edge_left, edge_right = var_solve(z_one)
+    z_two_wide = jnp.concatenate(
+        [edge_left.reshape(spot_rows, planes, 1), z_two, edge_right.reshape(spot_rows, planes, 1)],
+        axis=2,
+    )
+    z_three_wide = rate_solve(z_two_wide)
+    padded = jnp.pad(spot_pad(z_three_wide), ((0, 0), (1, 1), (0, 0)))
+    w_zero = z_zero + half_step * explicit_terms(padded, spot_geo, var_geo, rate_geo, True)
     w_one = spot_solve(w_zero)
-    w_two = var_solve(w_one)
+    w_two, _, _ = var_solve(w_one)
     w_three = rate_solve(w_two)
     return option_value + w_three
 

time: 194 us -> 184 us (0.948)
  starting transfers between devices: 48 us -> 42.8 us
  waiting for transfers between devices: 28.8 us -> 23.6 us
    ppermute x4 -> x2, waiting for transfers between devices: 15.3 us -> 6.84 us  [padded_2(): after = lax.ppermute(initial, axis, down)]
    ppermute x4 -> x2, starting transfers between devices: 10.8 us -> 3.22 us  [padded_2(): before = lax.ppermute(last, axis, up)]
    ppermute x0 -> x2, starting transfers between devices: none -> 5.57 us  [the longest x1 3.65 us: spot_pad(): before = lax.ppermute(array[rows - 1:rows], 'spot', up)]
    ppermute x0 -> x2, waiting for transfers between devices: none -> 3.93 us  [the longest x1 3.93 us: spot_pad(): after = lax.ppermute(array[0:1], 'spot', down)]
    ppermute x4 -> x2, starting transfers between devices: 13.3 us -> 10.1 us  [padded_2(): after = lax.ppermute(initial, axis, down)]
  transfers between devices with their start and end apart: 10 -> 8, of which waited for: 7 -> 5; matrix products, arithmetic and copies ran while one was open for 10% -> 11% of each run, Pallas kernels for 1% -> 1%
where the time goes in v6:
time: 184 us; the launch traced here: 183 us
  starting transfers between devices  42.8 us (23%)
  blocking collectives  40.2 us (22%)
  local copies, waits for them, and re-layouts  30.2 us (16%)
  Pallas kernels  26.5 us (14%)
  waiting for transfers between devices  23.6 us (13%)
  other arithmetic  14.1 us (8%)
  between operations  5.91 us (3%)
    all_to_all x1, blocking collectives, spot_solve(): lax.all_to_all(values.reshape(spot_rows, line_count), 'spot', split_axis=...  23.8 us
    pallas_call x2, Pallas kernels, gather_var(): pl.pallas_call(functools.partial(gather_kernel, blocks), out_shape=jax.Sh...  18.6 us
    all_to_all x1, blocking collectives, spot_solve(): lax.all_to_all(solved, 'spot', split_axis=0, concat_axis=1, tiled=True)  16.4 us
    all_to_all x1, starting transfers between devices, spot_solve(): lax.all_to_all(values.reshape(spot_rows, line_count), 'spot', split_axis=...  15.6 us
    ppermute x2, starting transfers between devices, padded_2(): after = lax.ppermute(initial, axis, down)  10.1 us
    all_to_all x1, starting transfers between devices, spot_solve(): lax.all_to_all(solved, 'spot', split_axis=0, concat_axis=1, tiled=True)  8.27 us
    pallas_call x3, Pallas kernels, line_solve(): pl.pallas_call(cyclic_kernel, out_shape=jax.ShapeDtypeStruct((count, widt...  7.94 us
    all_to_all x1, waiting for transfers between devices, spot_solve(): lax.all_to_all(solved, 'spot', split_axis=0, concat_axis=1, tiled=True)  7.26 us
  transfers between devices with their start and end apart: 8, of which 5 were waited for; matrix products, arithmetic and copies ran while one was open for 11% of the time, Pallas kernels for 1%

profile of v6, /device:TPU:1, one launch (start us, length us, event | category | flops | bytes accessed | tf_op | source)
XLA Modules:
  0.0 183.3 jit_solution(10611008967335406386)
XLA Ops:
  0.9 8.8 %collective-permute-start.1 = (f32[1,64,256]{2,1,0:T(8,128)S(1)}, f32[1,64,256]{2,1,0:T(8,128)S(1)}, u32[]{:S(2)}, u32[]{:S(2)}) collective-permute-start(f32[1,64,256]{2,1,0:T(8,128)S(1)} %get-tuple-element.120), channel_id=1, source_target_pairs={{4,0},{8,4},{12,8},{16,12},{20,16},{24,20},{28,24},{32,28},{36,32}... | collective-permute-start | bytes 196616 | tf_op jit(solution)/shard_map/ppermute | solution.py:39
  9.7 1.9 %collective-permute-start = (f32[1,64,256]{2,1,0:T(8,128)S(1)}, f32[1,64,256]{2,1,0:T(8,128)S(1)}, u32[]{:S(2)}, u32[]{:S(2)}) collective-permute-start(f32[1,64,256]{2,1,0:T(8,128)S(1)} %get-tuple-element.121), channel_id=1, source_target_pairs={{0,4},{4,8},{8,12},{12,16},{16,20},{20,24},{24,28},{28,32},{32,36}... | collective-permute-start | bytes 196616 | tf_op jit(solution)/shard_map/ppermute | solution.py:38
  20.9 1.3 pad_multiply_fusion.7
  26.1 2.0 %select_select_fusion.rhs_ref = f32[256,128]{1,0:T(8,128)} fusion(f32[]{:T(128)} %bitcast.34, f32[]{:T(128)} %bitcast.33, pred[128]{0:T(512)(128)(4,1)S(1)} %iota.40, pred[128]{0:T(512)(128)(4,1)S(1)} %iota.34, pred[256]{0:T(512)(128)(4,1)S(1)} %get-tuple-element.266, pred[256]{0:T(512)(128)(4,1)S(1)} %get-tuple-element.267), kind=kLoop, calls=%fused_computation.138 | loop fusion | flops 131072 | bytes 131848 | tf_op jit(solution)/shard_map/jit(_where)/select_n | solution.py:363
  29.0 1.3 collective-permute-start.2
  30.3 1.3 collective-permute-start.3
  31.6 1.4 collective-permute-done.2
  33.0 6.8 %collective-permute-done.3 = f32[4,64,1]{2,1,0:T(8,128)S(1)} collective-permute-done((f32[4,64,1]{2,1,0:T(8,128)S(1)}, f32[4,64,1]{2,1,0:T(8,128)S(1)}, u32[]{:S(2)}, u32[]{:S(2)}) %collective-permute-start.3) | collective-permute-done | bytes 1056 | tf_op jit(solution)/shard_map/ppermute | solution.py:39
  41.8 15.6 %all-to-all-start = ((f32[2,128,128]{2,0,1:T(2,128)}), f32[2,128,128]{2,0,1:T(2,128)S(1)}, u32[]{:S(2)}, u32[]{:S(2)}) async-start(f32[2,128,128]{2,0,1:T(2,128)} %copy.388), calls=%async_computation | async-start | bytes 262144 | tf_op jit(solution)/shard_map/all_to_all | solution.py:318
  59.9 2.6 %shard_map.47 = f32[256,128]{1,0:T(8,128)} custom-call(f32[256,128]{1,0:T(8,128)} %broadcast_in_dim.243.lower_ref, f32[256,128]{1,0:T(8,128)} %copy.457.main_ref, f32[256,128]{1,0:T(8,128)} %broadcast_in_dim.247.upper_ref, f32[256,128]{1,0:T(8,128)} %select_select_fusion.rhs_ref), custom_call_target="tpu_custom_call" | custom-call | tf_op jit(solution)/shard_map/pallas_call | solution.py:240
  64.4 4.2 %all-to-all-done = f32[2,128,128]{2,0,1:T(2,128)S(1)} async-done(((f32[2,128,128]{2,0,1:T(2,128)}), f32[2,128,128]{2,0,1:T(2,128)S(1)}, u32[]{:S(2)}, u32[]{:S(2)}) %all-to-all-start) | async-done | bytes 131104 | tf_op jit(solution)/shard_map/all_to_all | solution.py:318
  71.3 8.3 %all-to-all-start.1 = ((f32[128,2,128]{2,1,0:T(2,128)}), f32[128,2,128]{2,1,0:T(2,128)S(1)}, u32[]{:S(2)}, u32[]{:S(2)}) async-start(f32[128,2,128]{2,1,0:T(2,128)} %copy.401), calls=%async_computation.1 | async-start | bytes 262144 | tf_op jit(solution)/shard_map/all_to_all | solution.py:338
  83.4 7.3 %all-to-all-done.1 = f32[128,2,128]{2,1,0:T(2,128)S(1)} async-done(((f32[128,2,128]{2,1,0:T(2,128)}), f32[128,2,128]{2,1,0:T(2,128)S(1)}, u32[]{:S(2)}, u32[]{:S(2)}) %all-to-all-start.1) | async-done | bytes 131104 | tf_op jit(solution)/shard_map/all_to_all | solution.py:338
  91.5 2.7 %shard_map.46 = f32[256,128]{1,0:T(8,128)} custom-call(f32[256,128]{1,0:T(8,128)} %broadcast_in_dim.243.lower_ref, f32[256,128]{1,0:T(8,128)} %copy.457.main_ref, f32[256,128]{1,0:T(8,128)} %broadcast_in_dim.247.upper_ref, f32[256,128]{1,0:T(8,128)} %copy.404.rhs_ref), custom_call_target="tpu_custom_call" | custom-call | tf_op jit(solution)/shard_map/pallas_call | solution.py:240
  96.7 10.2 %shard_map.48 = f32[4,8,64]{2,1,0:T(8,128)} custom-call(f32[8,64]{1,0:T(8,128)} %concatenate.387.ends_ref), custom_call_target="tpu_custom_call" | custom-call | tf_op jit(solution)/shard_map/pallas_call | solution.py:276
  106.8 1.3 gather_fusion
  111.8 3.6 %collective-permute-start.4 = (f32[1,64,258]{2,1,0:T(8,128)S(1)}, f32[1,64,258]{2,1,0:T(8,128)S(1)}, u32[]{:S(2)}, u32[]{:S(2)}) collective-permute-start(f32[1,64,258]{2,1,0:T(8,128)S(1)} %copy.432), channel_id=1, source_target_pairs={{0,4},{4,8},{8,12},{12,16},{16,20},{20,24},{24,28},{28,32},{32,36}... | collective-permute-start | bytes 198152 | tf_op jit(solution)/shard_map/ppermute | solution.py:464
  115.8 1.9 %collective-permute-start.5 = (f32[1,64,258]{2,1,0:T(8,128)S(1)}, f32[1,64,258]{2,1,0:T(8,128)S(1)}, u32[]{:S(2)}, u32[]{:S(2)}) collective-permute-start(f32[1,64,258]{2,1,0:T(8,128)S(1)} %copy.439), channel_id=1, source_target_pairs={{4,0},{8,4},{12,8},{16,12},{20,16},{24,20},{28,24},{32,28},{36,32}... | collective-permute-start | bytes 198152 | tf_op jit(solution)/shard_map/ppermute | solution.py:465
  117.8 3.9 %collective-permute-done.5 = f32[1,64,258]{2,1,0:T(8,128)S(1)} collective-permute-done((f32[1,64,258]{2,1,0:T(8,128)S(1)}, f32[1,64,258]{2,1,0:T(8,128)S(1)}, u32[]{:S(2)}, u32[]{:S(2)}) %collective-permute-start.5) | collective-permute-done | bytes 66080 | tf_op jit(solution)/shard_map/ppermute | solution.py:465
  122.6 23.8 %all_to_all.64 = f32[2,128,128]{2,0,1:T(2,128)S(1)} all-to-all(f32[2,128,128]{2,0,1:T(2,128)S(1)} %copy.442), channel_id=1, replica_groups=mesh['spot'=128,'var'=4] {'spot'}, dimensions={1} | all-to-all | bytes 262144 | tf_op jit(solution)/shard_map/all_to_all | solution.py:318
  147.5 16.4 %all_to_all.65 = f32[128,2,128]{2,1,0:T(2,128)S(1)} all-to-all(f32[128,2,128]{2,1,0:T(2,128)S(1)} %copy.455), channel_id=1, replica_groups=mesh['spot'=128,'var'=4] {'spot'}, dimensions={0} | all-to-all | bytes 262144 | tf_op jit(solution)/shard_map/all_to_all | solution.py:338
  164.6 2.7 %shard_map.49 = f32[256,128]{1,0:T(8,128)} custom-call(f32[256,128]{1,0:T(8,128)} %broadcast_in_dim.243.lower_ref, f32[256,128]{1,0:T(8,128)} %copy.457.main_ref, f32[256,128]{1,0:T(8,128)} %broadcast_in_dim.247.upper_ref, f32[256,128]{1,0:T(8,128)} %copy.458.rhs_ref), custom_call_target="tpu_custom_call" | custom-call | tf_op jit(solution)/shard_map/pallas_call | solution.py:240
  169.8 8.4 %shard_map.50 = f32[4,8,64]{2,1,0:T(8,128)} custom-call(f32[8,64]{1,0:T(8,128)} %concatenate.431.ends_ref), custom_call_target="tpu_custom_call" | custom-call | tf_op jit(solution)/shard_map/pallas_call | solution.py:276
  178.3 1.3 gather_fusion.1
  (471 shorter events, 38.4 us)
Async XLA Ops:
  0.9 28.0 %collective-permute-start.1 = (f32[1,64,256]{2,1,0:T(8,128)S(1)}, f32[1,64,256]{2,1,0:T(8,128)S(1)}, u32[]{:S(2)}, u32[]{:S(2)}) collective-permute-start(f32[1,64,256]{2,1,0:T(8,128)S(1)} %get-tuple-element.120), channel_id=1, source_target_pairs={{4,0},{8,4},{12,8},{16,12},{20,16},{24,20},{28,24},{32,28},{36,32}... | collective-permute-start | bytes 196616 | tf_op jit(solution)/shard_map/ppermute | solution.py:39
  9.7 19.2 %collective-permute-start = (f32[1,64,256]{2,1,0:T(8,128)S(1)}, f32[1,64,256]{2,1,0:T(8,128)S(1)}, u32[]{:S(2)}, u32[]{:S(2)}) collective-permute-start(f32[1,64,256]{2,1,0:T(8,128)S(1)} %get-tuple-element.121), channel_id=1, source_target_pairs={{0,4},{4,8},{8,12},{12,16},{16,20},{20,24},{24,28},{28,32},{32,36}... | collective-permute-start | bytes 196616 | tf_op jit(solution)/shard_map/ppermute | solution.py:38
  11.6 0.7 copy-start.3
  16.5 0.7 copy-start.1
  17.6 0.7 copy-start.2
  26.1 2.8 %copy-start = (f32[2,64,256]{2,1,0:T(8,128)S(1)}, f32[2,64,256]{2,1,0:T(8,128)}, u32[]{:S(2)}) copy-start(f32[2,64,256]{2,1,0:T(8,128)} %param.6) | copy-start | bytes 393220
  29.0 4.0 %collective-permute-start.2 = (f32[4,64,1]{2,1,0:T(8,128)S(1)}, f32[4,64,1]{2,1,0:T(8,128)S(1)}, u32[]{:S(2)}, u32[]{:S(2)}) collective-permute-start(f32[4,64,1]{2,1,0:T(8,128)S(1)} %get-tuple-element.111), channel_id=1, source_target_pairs={{0,1},{1,2},{2,3},{4,5},{5,6},{6,7},{8,9},{9,10},{10,11},{12,13},{... | collective-permute-start | bytes 3080 | tf_op jit(solution)/shard_map/ppermute | solution.py:38
  30.3 9.5 %collective-permute-start.3 = (f32[4,64,1]{2,1,0:T(8,128)S(1)}, f32[4,64,1]{2,1,0:T(8,128)S(1)}, u32[]{:S(2)}, u32[]{:S(2)}) collective-permute-start(f32[4,64,1]{2,1,0:T(8,128)S(1)} %get-tuple-element.112), channel_id=1, source_target_pairs={{1,0},{2,1},{3,2},{5,4},{6,5},{7,6},{9,8},{10,9},{11,10},{13,12},{... | collective-permute-start | bytes 3080 | tf_op jit(solution)/shard_map/ppermute | solution.py:39
  41.8 26.8 %all-to-all-start = ((f32[2,128,128]{2,0,1:T(2,128)}), f32[2,128,128]{2,0,1:T(2,128)S(1)}, u32[]{:S(2)}, u32[]{:S(2)}) async-start(f32[2,128,128]{2,0,1:T(2,128)} %copy.388), calls=%async_computation | async-start | bytes 262144 | tf_op jit(solution)/shard_map/all_to_all | solution.py:318
  71.3 19.4 %all-to-all-start.1 = ((f32[128,2,128]{2,1,0:T(2,128)}), f32[128,2,128]{2,1,0:T(2,128)S(1)}, u32[]{:S(2)}, u32[]{:S(2)}) async-start(f32[128,2,128]{2,1,0:T(2,128)} %copy.401), calls=%async_computation.1 | async-start | bytes 262144 | tf_op jit(solution)/shard_map/all_to_all | solution.py:338
  111.8 5.9 %collective-permute-start.4 = (f32[1,64,258]{2,1,0:T(8,128)S(1)}, f32[1,64,258]{2,1,0:T(8,128)S(1)}, u32[]{:S(2)}, u32[]{:S(2)}) collective-permute-start(f32[1,64,258]{2,1,0:T(8,128)S(1)} %copy.432), channel_id=1, source_target_pairs={{0,4},{4,8},{8,12},{12,16},{16,20},{20,24},{24,28},{28,32},{32,36}... | collective-permute-start | bytes 198152 | tf_op jit(solution)/shard_map/ppermute | solution.py:464
  115.8 5.9 %collective-permute-start.5 = (f32[1,64,258]{2,1,0:T(8,128)S(1)}, f32[1,64,258]{2,1,0:T(8,128)S(1)}, u32[]{:S(2)}, u32[]{:S(2)}) collective-permute-start(f32[1,64,258]{2,1,0:T(8,128)S(1)} %copy.439), channel_id=1, source_target_pairs={{4,0},{8,4},{12,8},{16,12},{20,16},{24,20},{28,24},{32,28},{36,32}... | collective-permute-start | bytes 198152 | tf_op jit(solution)/shard_map/ppermute | solution.py:465

commit v7 on v6

--- a/solution.py
+++ b/solution.py
@@ -309,8 +309,23 @@
     rate_plain = rate_geo[0].reshape(planes)
     var_plain = var_geo[0].reshape(var_cols)
 
+    def spot_pad(array):
+        devices, rows = lax.axis_size("spot"), array.shape[0]
+        up = [(i, i + 1) for i in range(devices - 1)]
+        down = [(j, i) for i, j in up]
+        before = lax.ppermute(array[rows - 1 : rows], "spot", up)
+        after = lax.ppermute(array[0:1], "spot", down)
+        return jnp.concatenate([before, array, after], axis=0)
+
     def edge_terms(values, mixing_only):
-        padded = padded_2(values, (("spot", 0), ("var", 2)), 1)
+        devices, cols = lax.axis_size("var"), values.shape[2]
+        up = [(i, i + 1) for i in range(devices - 1)]
+        down = [(j, i) for i, j in up]
+        left = lax.ppermute(values[:, :, cols - 1 : cols], "var", up)
+        right = lax.ppermute(values[:, :, 0:1], "var", down)
+        rows = spot_pad(values)
+        sides = spot_pad(jnp.concatenate([left, right], axis=2))
+        padded = jnp.concatenate([sides[:, :, 0:1], rows, sides[:, :, 1:2]], axis=2)
         padded = jnp.pad(padded, ((0, 0), (1, 1), (0, 0)))
         return explicit_terms(padded, spot_geo, var_geo, rate_geo, mixing_only)
 
@@ -457,14 +472,6 @@
         )
         return implicit(system, values, 1)
 
-    def spot_pad(array):
-        devices, rows = lax.axis_size("spot"), array.shape[0]
-        up = [(i, i + 1) for i in range(devices - 1)]
-        down = [(j, i) for i, j in up]
-        before = lax.ppermute(array[rows - 1 : rows], "spot", up)
-        after = lax.ppermute(array[0:1], "spot", down)
-        return jnp.concatenate([before, array, after], axis=0)
-
     z_zero = time_step * edge_terms(option_value, False)
     z_one = spot_solve(z_zero)
     z_two, edge_left, edge_right = var_solve(z_one)

time: 184 us -> 191 us (1.038)
  starting transfers between devices: 42.8 us -> 55.4 us
  waiting for transfers between devices: 23.6 us -> 16.4 us
    ppermute x1 -> x3, starting transfers between devices: 1.92 us -> 13.1 us  [spot_pad(): after = lax.ppermute(array[0:1], 'spot', down)]
    ppermute x4 -> x2, starting transfers between devices: 13.3 us -> 2.58 us  [the longest x1 1.29 us: edge_terms(): left = lax.ppermute(values[:, :, cols - 1:cols], 'var', up)]
    ppermute x4 -> x2, waiting for transfers between devices: 8.23 us -> 0.01 us  [the longest x1 0.01 us: edge_terms(): left = lax.ppermute(values[:, :, cols - 1:cols], 'var', up)]
    all_to_all x1, starting transfers between devices: 15.6 us -> 23 us  [spot_solve(): lax.all_to_all(values.reshape(spot_rows, line_count), 'spot', split_axis=...]
    ppermute x1 -> x3, starting transfers between devices: 3.65 us -> 8.43 us  [spot_pad(): before = lax.ppermute(array[rows - 1:rows], 'spot', up)]
    ppermute x1 -> x3, waiting for transfers between devices: 3.93 us -> 3.94 us  [spot_pad(): after = lax.ppermute(array[0:1], 'spot', down)]
  transfers between devices with their start and end apart: 8 -> 10, of which waited for: 5 -> 4; matrix products, arithmetic and copies ran while one was open for 11% -> 11% of each run, Pallas kernels for 1% -> 1%
where the time goes in v7:
time: 191 us; the launch traced here: 190 us
  starting transfers between devices  55.4 us (29%)
  blocking collectives  40.3 us (21%)
  local copies, waits for them, and re-layouts  30.6 us (16%)
  Pallas kernels  27.6 us (14%)
  waiting for transfers between devices  16.4 us (9%)
  other arithmetic  14.3 us (7%)
  between operations  5.87 us (3%)
    all_to_all x1, blocking collectives, spot_solve(): lax.all_to_all(values.reshape(spot_rows, line_count), 'spot', split_axis=...  23.9 us
    all_to_all x1, starting transfers between devices, spot_solve(): lax.all_to_all(values.reshape(spot_rows, line_count), 'spot', split_axis=...  23 us
    pallas_call x2, Pallas kernels, gather_var(): pl.pallas_call(functools.partial(gather_kernel, blocks), out_shape=jax.Sh...  19.7 us
    all_to_all x1, blocking collectives, spot_solve(): lax.all_to_all(solved, 'spot', split_axis=0, concat_axis=1, tiled=True)  16.4 us
    ppermute x3, starting transfers between devices, spot_pad(): after = lax.ppermute(array[0:1], 'spot', down)  13.1 us
    ppermute x3, starting transfers between devices, spot_pad(): before = lax.ppermute(array[rows - 1:rows], 'spot', up)  8.43 us
    all_to_all x1, starting transfers between devices, spot_solve(): lax.all_to_all(solved, 'spot', split_axis=0, concat_axis=1, tiled=True)  8.23 us
    pallas_call x3, Pallas kernels, line_solve(): pl.pallas_call(cyclic_kernel, out_shape=jax.ShapeDtypeStruct((count, widt...  7.91 us
  transfers between devices with their start and end apart: 10, of which 4 were waited for; matrix products, arithmetic and copies ran while one was open for 11% of the time, Pallas kernels for 1%

profile of v7, /device:TPU:1, one launch (start us, length us, event | category | flops | bytes accessed | tf_op | source)
XLA Modules:
  0.0 190.4 jit_solution(5916937642147279377)
XLA Ops:
  0.9 8.8 %collective-permute-start.5 = (f32[1,64,256]{2,1,0:T(8,128)S(1)}, f32[1,64,256]{2,1,0:T(8,128)S(1)}, u32[]{:S(2)}, u32[]{:S(2)}) collective-permute-start(f32[1,64,256]{2,1,0:T(8,128)S(1)} %get-tuple-element.120), channel_id=1, source_target_pairs={{4,0},{8,4},{12,8},{16,12},{20,16},{24,20},{28,24},{32,28},{36,32}... | collective-permute-start | bytes 196616 | tf_op jit(solution)/shard_map/ppermute | solution.py:317
  9.7 1.9 %collective-permute-start.4 = (f32[1,64,256]{2,1,0:T(8,128)S(1)}, f32[1,64,256]{2,1,0:T(8,128)S(1)}, u32[]{:S(2)}, u32[]{:S(2)}) collective-permute-start(f32[1,64,256]{2,1,0:T(8,128)S(1)} %get-tuple-element.121), channel_id=1, source_target_pairs={{0,4},{4,8},{8,12},{12,16},{16,20},{20,24},{24,28},{28,32},{32,36}... | collective-permute-start | bytes 196616 | tf_op jit(solution)/shard_map/ppermute | solution.py:316
  11.8 1.3 collective-permute-start
  13.2 1.3 collective-permute-start.1
  23.8 1.3 pad_multiply_fusion.7
  29.5 2.1 %select_select_fusion.rhs_ref = f32[256,128]{1,0:T(8,128)} fusion(f32[]{:T(128)} %bitcast.34, f32[]{:T(128)} %bitcast.33, pred[128]{0:T(512)(128)(4,1)S(1)} %iota.40, pred[128]{0:T(512)(128)(4,1)S(1)} %iota.34, pred[256]{0:T(512)(128)(4,1)S(1)} %get-tuple-element.271, pred[256]{0:T(512)(128)(4,1)S(1)} %get-tuple-element.272), kind=kLoop, calls=%fused_computation.139 | loop fusion | flops 131072 | bytes 131848 | tf_op jit(solution)/shard_map/jit(_where)/select_n | solution.py:378
  31.8 2.4 %collective-permute-start.3 = (f32[1,64,2]{2,1,0:T(8,128)S(1)}, f32[1,64,2]{2,1,0:T(8,128)S(1)}, u32[]{:S(2)}, u32[]{:S(2)}) collective-permute-start(f32[1,64,2]{2,1,0:T(8,128)S(1)} %copy.507), channel_id=1, source_target_pairs={{4,0},{8,4},{12,8},{16,12},{20,16},{24,20},{28,24},{32,28},{36,32}... | collective-permute-start | bytes 1544 | tf_op jit(solution)/shard_map/ppermute | solution.py:317
  34.2 3.2 %collective-permute-start.2 = (f32[1,64,2]{2,1,0:T(8,128)S(1)}, f32[1,64,2]{2,1,0:T(8,128)S(1)}, u32[]{:S(2)}, u32[]{:S(2)}) collective-permute-start(f32[1,64,2]{2,1,0:T(8,128)S(1)} %copy.506), channel_id=1, source_target_pairs={{0,4},{4,8},{8,12},{12,16},{16,20},{20,24},{24,28},{28,32},{32,36}... | collective-permute-start | bytes 1544 | tf_op jit(solution)/shard_map/ppermute | solution.py:316
  40.5 23.0 %all-to-all-start = ((f32[2,128,128]{2,0,1:T(2,128)}), f32[2,128,128]{2,0,1:T(2,128)S(1)}, u32[]{:S(2)}, u32[]{:S(2)}) async-start(f32[2,128,128]{2,0,1:T(2,128)} %copy.509), calls=%async_computation | async-start | bytes 262144 | tf_op jit(solution)/shard_map/all_to_all | solution.py:333
  66.0 2.6 %shard_map.47 = f32[256,128]{1,0:T(8,128)} custom-call(f32[256,128]{1,0:T(8,128)} %broadcast_in_dim.243.lower_ref, f32[256,128]{1,0:T(8,128)} %copy.578.main_ref, f32[256,128]{1,0:T(8,128)} %broadcast_in_dim.247.upper_ref, f32[256,128]{1,0:T(8,128)} %select_select_fusion.rhs_ref), custom_call_target="tpu_custom_call" | custom-call | tf_op jit(solution)/shard_map/pallas_call | solution.py:240
  70.5 4.2 %all-to-all-done = f32[2,128,128]{2,0,1:T(2,128)S(1)} async-done(((f32[2,128,128]{2,0,1:T(2,128)}), f32[2,128,128]{2,0,1:T(2,128)S(1)}, u32[]{:S(2)}, u32[]{:S(2)}) %all-to-all-start) | async-done | bytes 131104 | tf_op jit(solution)/shard_map/all_to_all | solution.py:333
  77.4 8.2 %all-to-all-start.1 = ((f32[128,2,128]{2,1,0:T(2,128)}), f32[128,2,128]{2,1,0:T(2,128)S(1)}, u32[]{:S(2)}, u32[]{:S(2)}) async-start(f32[128,2,128]{2,1,0:T(2,128)} %copy.522), calls=%async_computation.1 | async-start | bytes 262144 | tf_op jit(solution)/shard_map/all_to_all | solution.py:353
  89.4 7.3 %all-to-all-done.1 = f32[128,2,128]{2,1,0:T(2,128)S(1)} async-done(((f32[128,2,128]{2,1,0:T(2,128)}), f32[128,2,128]{2,1,0:T(2,128)S(1)}, u32[]{:S(2)}, u32[]{:S(2)}) %all-to-all-start.1) | async-done | bytes 131104 | tf_op jit(solution)/shard_map/all_to_all | solution.py:353
  97.6 2.6 %shard_map.46 = f32[256,128]{1,0:T(8,128)} custom-call(f32[256,128]{1,0:T(8,128)} %broadcast_in_dim.243.lower_ref, f32[256,128]{1,0:T(8,128)} %copy.578.main_ref, f32[256,128]{1,0:T(8,128)} %broadcast_in_dim.247.upper_ref, f32[256,128]{1,0:T(8,128)} %copy.525.rhs_ref), custom_call_target="tpu_custom_call" | custom-call | tf_op jit(solution)/shard_map/pallas_call | solution.py:240
  102.7 11.0 %shard_map.48 = f32[4,8,64]{2,1,0:T(8,128)} custom-call(f32[8,64]{1,0:T(8,128)} %concatenate.395.ends_ref), custom_call_target="tpu_custom_call" | custom-call | tf_op jit(solution)/shard_map/pallas_call | solution.py:276
  116.5 1.3 divide_bitcast_fusion.18
  118.8 3.3 %collective-permute-start.6 = (f32[1,64,258]{2,1,0:T(8,128)S(1)}, f32[1,64,258]{2,1,0:T(8,128)S(1)}, u32[]{:S(2)}, u32[]{:S(2)}) collective-permute-start(f32[1,64,258]{2,1,0:T(8,128)S(1)} %copy.553), channel_id=1, source_target_pairs={{0,4},{4,8},{8,12},{12,16},{16,20},{20,24},{24,28},{28,32},{32,36}... | collective-permute-start | bytes 198152 | tf_op jit(solution)/shard_map/ppermute | solution.py:316
  122.5 1.9 %collective-permute-start.7 = (f32[1,64,258]{2,1,0:T(8,128)S(1)}, f32[1,64,258]{2,1,0:T(8,128)S(1)}, u32[]{:S(2)}, u32[]{:S(2)}) collective-permute-start(f32[1,64,258]{2,1,0:T(8,128)S(1)} %copy.560), channel_id=1, source_target_pairs={{4,0},{8,4},{12,8},{16,12},{20,16},{24,20},{28,24},{32,28},{36,32}... | collective-permute-start | bytes 198152 | tf_op jit(solution)/shard_map/ppermute | solution.py:317
  124.5 3.9 %collective-permute-done.7 = f32[1,64,258]{2,1,0:T(8,128)S(1)} collective-permute-done((f32[1,64,258]{2,1,0:T(8,128)S(1)}, f32[1,64,258]{2,1,0:T(8,128)S(1)}, u32[]{:S(2)}, u32[]{:S(2)}) %collective-permute-start.7) | collective-permute-done | bytes 66080 | tf_op jit(solution)/shard_map/ppermute | solution.py:317
  129.4 23.9 %all_to_all.64 = f32[2,128,128]{2,0,1:T(2,128)S(1)} all-to-all(f32[2,128,128]{2,0,1:T(2,128)S(1)} %copy.563), channel_id=1, replica_groups=mesh['spot'=128,'var'=4] {'spot'}, dimensions={1} | all-to-all | bytes 262144 | tf_op jit(solution)/shard_map/all_to_all | solution.py:333
  154.3 16.4 %all_to_all.65 = f32[128,2,128]{2,1,0:T(2,128)S(1)} all-to-all(f32[128,2,128]{2,1,0:T(2,128)S(1)} %copy.576), channel_id=1, replica_groups=mesh['spot'=128,'var'=4] {'spot'}, dimensions={0} | all-to-all | bytes 262144 | tf_op jit(solution)/shard_map/all_to_all | solution.py:353
  171.5 2.6 %shard_map.49 = f32[256,128]{1,0:T(8,128)} custom-call(f32[256,128]{1,0:T(8,128)} %broadcast_in_dim.243.lower_ref, f32[256,128]{1,0:T(8,128)} %copy.578.main_ref, f32[256,128]{1,0:T(8,128)} %broadcast_in_dim.247.upper_ref, f32[256,128]{1,0:T(8,128)} %copy.579.rhs_ref), custom_call_target="tpu_custom_call" | custom-call | tf_op jit(solution)/shard_map/pallas_call | solution.py:240
  176.6 8.6 %shard_map.50 = f32[4,8,64]{2,1,0:T(8,128)} custom-call(f32[8,64]{1,0:T(8,128)} %concatenate.439.ends_ref), custom_call_target="tpu_custom_call" | custom-call | tf_op jit(solution)/shard_map/pallas_call | solution.py:276
  187.5 1.3 divide_bitcast_fusion.19
  (485 shorter events, 39.8 us)
Async XLA Ops:
  0.0 11.7 %copy-start = (f32[2,64,256]{2,1,0:T(8,128)S(1)}, f32[2,64,256]{2,1,0:T(8,128)}, u32[]{:S(2)}) copy-start(f32[2,64,256]{2,1,0:T(8,128)} %param.6) | copy-start | bytes 393220
  0.9 37.6 %collective-permute-start.5 = (f32[1,64,256]{2,1,0:T(8,128)S(1)}, f32[1,64,256]{2,1,0:T(8,128)S(1)}, u32[]{:S(2)}, u32[]{:S(2)}) collective-permute-start(f32[1,64,256]{2,1,0:T(8,128)S(1)} %get-tuple-element.120), channel_id=1, source_target_pairs={{4,0},{8,4},{12,8},{16,12},{20,16},{24,20},{28,24},{32,28},{36,32}... | collective-permute-start | bytes 196616 | tf_op jit(solution)/shard_map/ppermute | solution.py:317
  9.7 28.8 %collective-permute-start.4 = (f32[1,64,256]{2,1,0:T(8,128)S(1)}, f32[1,64,256]{2,1,0:T(8,128)S(1)}, u32[]{:S(2)}, u32[]{:S(2)}) collective-permute-start(f32[1,64,256]{2,1,0:T(8,128)S(1)} %get-tuple-element.121), channel_id=1, source_target_pairs={{0,4},{4,8},{8,12},{12,16},{16,20},{20,24},{24,28},{28,32},{32,36}... | collective-permute-start | bytes 196616 | tf_op jit(solution)/shard_map/ppermute | solution.py:316
  11.8 19.8 %collective-permute-start = (f32[2,64,1]{1,2,0:T(1,128)S(1)}, f32[2,64,1]{1,2,0:T(1,128)S(1)}, u32[]{:S(2)}, u32[]{:S(2)}) collective-permute-start(f32[2,64,1]{1,2,0:T(1,128)S(1)} %copy.606), channel_id=1, source_target_pairs={{0,1},{1,2},{2,3},{4,5},{5,6},{6,7},{8,9},{9,10},{10,11},{12,13},{... | collective-permute-start | bytes 1544 | tf_op jit(solution)/shard_map/ppermute | solution.py:324
  13.2 18.4 %collective-permute-start.1 = (f32[2,64,1]{1,2,0:T(1,128)S(1)}, f32[2,64,1]{1,2,0:T(1,128)S(1)}, u32[]{:S(2)}, u32[]{:S(2)}) collective-permute-start(f32[2,64,1]{1,2,0:T(1,128)S(1)} %copy.607), channel_id=1, source_target_pairs={{1,0},{2,1},{3,2},{5,4},{6,5},{7,6},{9,8},{10,9},{11,10},{13,12},{... | collective-permute-start | bytes 1544 | tf_op jit(solution)/shard_map/ppermute | solution.py:325
  14.5 0.7 copy-start.3
  19.4 0.7 copy-start.1
  20.5 0.7 copy-start.2
  31.8 5.7 %collective-permute-start.3 = (f32[1,64,2]{2,1,0:T(8,128)S(1)}, f32[1,64,2]{2,1,0:T(8,128)S(1)}, u32[]{:S(2)}, u32[]{:S(2)}) collective-permute-start(f32[1,64,2]{2,1,0:T(8,128)S(1)} %copy.507), channel_id=1, source_target_pairs={{4,0},{8,4},{12,8},{16,12},{20,16},{24,20},{28,24},{32,28},{36,32}... | collective-permute-start | bytes 1544 | tf_op jit(solution)/shard_map/ppermute | solution.py:317
  34.2 4.2 %collective-permute-start.2 = (f32[1,64,2]{2,1,0:T(8,128)S(1)}, f32[1,64,2]{2,1,0:T(8,128)S(1)}, u32[]{:S(2)}, u32[]{:S(2)}) collective-permute-start(f32[1,64,2]{2,1,0:T(8,128)S(1)} %copy.506), channel_id=1, source_target_pairs={{0,4},{4,8},{8,12},{12,16},{16,20},{20,24},{24,28},{28,32},{32,36}... | collective-permute-start | bytes 1544 | tf_op jit(solution)/shard_map/ppermute | solution.py:316
  40.5 34.2 %all-to-all-start = ((f32[2,128,128]{2,0,1:T(2,128)}), f32[2,128,128]{2,0,1:T(2,128)S(1)}, u32[]{:S(2)}, u32[]{:S(2)}) async-start(f32[2,128,128]{2,0,1:T(2,128)} %copy.509), calls=%async_computation | async-start | bytes 262144 | tf_op jit(solution)/shard_map/all_to_all | solution.py:333
  77.4 19.4 %all-to-all-start.1 = ((f32[128,2,128]{2,1,0:T(2,128)}), f32[128,2,128]{2,1,0:T(2,128)S(1)}, u32[]{:S(2)}, u32[]{:S(2)}) async-start(f32[128,2,128]{2,1,0:T(2,128)} %copy.522), calls=%async_computation.1 | async-start | bytes 262144 | tf_op jit(solution)/shard_map/all_to_all | solution.py:353
  118.8 5.6 %collective-permute-start.6 = (f32[1,64,258]{2,1,0:T(8,128)S(1)}, f32[1,64,258]{2,1,0:T(8,128)S(1)}, u32[]{:S(2)}, u32[]{:S(2)}) collective-permute-start(f32[1,64,258]{2,1,0:T(8,128)S(1)} %copy.553), channel_id=1, source_target_pairs={{0,4},{4,8},{8,12},{12,16},{16,20},{20,24},{24,28},{28,32},{32,36}... | collective-permute-start | bytes 198152 | tf_op jit(solution)/shard_map/ppermute | solution.py:316
  122.5 5.9 %collective-permute-start.7 = (f32[1,64,258]{2,1,0:T(8,128)S(1)}, f32[1,64,258]{2,1,0:T(8,128)S(1)}, u32[]{:S(2)}, u32[]{:S(2)}) collective-permute-start(f32[1,64,258]{2,1,0:T(8,128)S(1)} %copy.560), channel_id=1, source_target_pairs={{4,0},{8,4},{12,8},{16,12},{20,16},{24,20},{28,24},{32,28},{36,32}... | collective-permute-start | bytes 198152 | tf_op jit(solution)/shard_map/ppermute | solution.py:317

commit v8 on v6

--- a/solution.py
+++ b/solution.py
@@ -310,7 +310,7 @@
     var_plain = var_geo[0].reshape(var_cols)
 
     def edge_terms(values, mixing_only):
-        padded = padded_2(values, (("spot", 0), ("var", 2)), 1)
+        padded = padded_2(values, (("var", 2), ("spot", 0)), 1)
         padded = jnp.pad(padded, ((0, 0), (1, 1), (0, 0)))
         return explicit_terms(padded, spot_geo, var_geo, rate_geo, mixing_only)
 

time: 184 us -> 181 us (0.984)
  waiting for transfers between devices: 23.6 us -> 19.1 us
    ppermute x2, starting transfers between devices: 10.1 us -> 3.66 us  [padded_2(): after = lax.ppermute(initial, axis, down)]
    ppermute x2, starting transfers between devices: 3.22 us -> 9 us  [padded_2(): before = lax.ppermute(last, axis, up)]
    ppermute x2, waiting for transfers between devices: 6.84 us -> 3.53 us  [padded_2(): after = lax.ppermute(initial, axis, down)]
  transfers between devices with their start and end apart: 8 -> 8, of which waited for: 5 -> 4; matrix products, arithmetic and copies ran while one was open for 11% -> 11% of each run, Pallas kernels for 1% -> 1%
where the time goes in v8:
time: 181 us; the launch traced here: 180 us
  starting transfers between devices  43.3 us (24%)
  blocking collectives  40.3 us (22%)
  local copies, waits for them, and re-layouts  30 us (17%)
  Pallas kernels  27 us (15%)
  waiting for transfers between devices  19.1 us (11%)
  other arithmetic  14.3 us (8%)
  between operations  5.77 us (3%)
    all_to_all x1, blocking collectives, spot_solve(): lax.all_to_all(values.reshape(spot_rows, line_count), 'spot', split_axis=...  23.9 us
    pallas_call x2, Pallas kernels, gather_var(): pl.pallas_call(functools.partial(gather_kernel, blocks), out_shape=jax.Sh...  19 us
    all_to_all x1, starting transfers between devices, spot_solve(): lax.all_to_all(values.reshape(spot_rows, line_count), 'spot', split_axis=...  17.3 us
    all_to_all x1, blocking collectives, spot_solve(): lax.all_to_all(solved, 'spot', split_axis=0, concat_axis=1, tiled=True)  16.4 us
    ppermute x2, starting transfers between devices, padded_2(): before = lax.ppermute(last, axis, up)  9 us
    all_to_all x1, starting transfers between devices, spot_solve(): lax.all_to_all(solved, 'spot', split_axis=0, concat_axis=1, tiled=True)  8.17 us
    pallas_call x3, Pallas kernels, line_solve(): pl.pallas_call(cyclic_kernel, out_shape=jax.ShapeDtypeStruct((count, widt...  7.92 us
    all_to_all x1, waiting for transfers between devices, spot_solve(): lax.all_to_all(solved, 'spot', split_axis=0, concat_axis=1, tiled=True)  7.38 us
  transfers between devices with their start and end apart: 8, of which 4 were waited for; matrix products, arithmetic and copies ran while one was open for 11% of the time, Pallas kernels for 1%

profile of v8, /device:TPU:1, one launch (start us, length us, event | category | flops | bytes accessed | tf_op | source)
XLA Modules:
  0.0 179.8 jit_solution(3296608504237531548)
XLA Ops:
  1.0 5.0 %collective-permute-start = (f32[2,64,1]{2,1,0:T(8,128)S(1)}, f32[2,64,1]{2,1,0:T(8,128)S(1)}, u32[]{:S(2)}, u32[]{:S(2)}) collective-permute-start(f32[2,64,1]{2,1,0:T(8,128)S(1)} %get-tuple-element.122), channel_id=1, source_target_pairs={{0,1},{1,2},{2,3},{4,5},{5,6},{6,7},{8,9},{9,10},{10,11},{12,13},{... | collective-permute-start | bytes 1544 | tf_op jit(solution)/shard_map/ppermute | solution.py:38
  6.0 1.3 collective-permute-start.1
  21.7 2.1 %select_select_fusion.rhs_ref = f32[256,128]{1,0:T(8,128)} fusion(f32[]{:T(128)} %bitcast.34, f32[]{:T(128)} %bitcast.33, pred[128]{0:T(512)(128)(4,1)S(1)} %iota.40, pred[128]{0:T(512)(128)(4,1)S(1)} %iota.34, pred[256]{0:T(512)(128)(4,1)S(1)} %get-tuple-element.268, pred[256]{0:T(512)(128)(4,1)S(1)} %get-tuple-element.269), kind=kLoop, calls=%fused_computation.130 | loop fusion | flops 131072 | bytes 131848 | tf_op jit(solution)/shard_map/jit(_where)/select_n | solution.py:363
  24.6 4.0 %collective-permute-start.2 = (f32[1,64,258]{2,1,0:T(8,128)S(1)}, f32[1,64,258]{2,1,0:T(8,128)S(1)}, u32[]{:S(2)}, u32[]{:S(2)}) collective-permute-start(f32[1,64,258]{2,1,0:T(8,128)S(1)} %get-tuple-element.118), channel_id=1, source_target_pairs={{0,4},{4,8},{8,12},{12,16},{16,20},{20,24},{24,28},{28,32},{32,36}... | collective-permute-start | bytes 198152 | tf_op jit(solution)/shard_map/ppermute | solution.py:38
  28.6 2.4 %collective-permute-start.3 = (f32[1,64,258]{2,1,0:T(8,128)S(1)}, f32[1,64,258]{2,1,0:T(8,128)S(1)}, u32[]{:S(2)}, u32[]{:S(2)}) collective-permute-start(f32[1,64,258]{2,1,0:T(8,128)S(1)} %get-tuple-element.119), channel_id=1, source_target_pairs={{4,0},{8,4},{12,8},{16,12},{20,16},{24,20},{28,24},{32,28},{36,32}... | collective-permute-start | bytes 198152 | tf_op jit(solution)/shard_map/ppermute | solution.py:39
  31.0 3.5 %collective-permute-done.3 = f32[1,64,258]{2,1,0:T(8,128)S(1)} collective-permute-done((f32[1,64,258]{2,1,0:T(8,128)S(1)}, f32[1,64,258]{2,1,0:T(8,128)S(1)}, u32[]{:S(2)}, u32[]{:S(2)}) %collective-permute-start.3) | collective-permute-done | bytes 66080 | tf_op jit(solution)/shard_map/ppermute | solution.py:39
  36.6 17.3 %all-to-all-start = ((f32[2,128,128]{2,0,1:T(2,128)}), f32[2,128,128]{2,0,1:T(2,128)S(1)}, u32[]{:S(2)}, u32[]{:S(2)}) async-start(f32[2,128,128]{2,0,1:T(2,128)} %copy.388), calls=%async_computation | async-start | bytes 262144 | tf_op jit(solution)/shard_map/all_to_all | solution.py:318
  56.2 2.6 %shard_map.47 = f32[256,128]{1,0:T(8,128)} custom-call(f32[256,128]{1,0:T(8,128)} %broadcast_in_dim.243.lower_ref, f32[256,128]{1,0:T(8,128)} %copy.457.main_ref, f32[256,128]{1,0:T(8,128)} %broadcast_in_dim.247.upper_ref, f32[256,128]{1,0:T(8,128)} %select_select_fusion.rhs_ref), custom_call_target="tpu_custom_call" | custom-call | tf_op jit(solution)/shard_map/pallas_call | solution.py:240
  60.7 4.3 %all-to-all-done = f32[2,128,128]{2,0,1:T(2,128)S(1)} async-done(((f32[2,128,128]{2,0,1:T(2,128)}), f32[2,128,128]{2,0,1:T(2,128)S(1)}, u32[]{:S(2)}, u32[]{:S(2)}) %all-to-all-start) | async-done | bytes 131104 | tf_op jit(solution)/shard_map/all_to_all | solution.py:318
  67.6 8.2 %all-to-all-start.1 = ((f32[128,2,128]{2,1,0:T(2,128)}), f32[128,2,128]{2,1,0:T(2,128)S(1)}, u32[]{:S(2)}, u32[]{:S(2)}) async-start(f32[128,2,128]{2,1,0:T(2,128)} %copy.401), calls=%async_computation.1 | async-start | bytes 262144 | tf_op jit(solution)/shard_map/all_to_all | solution.py:338
  79.6 7.4 %all-to-all-done.1 = f32[128,2,128]{2,1,0:T(2,128)S(1)} async-done(((f32[128,2,128]{2,1,0:T(2,128)}), f32[128,2,128]{2,1,0:T(2,128)S(1)}, u32[]{:S(2)}, u32[]{:S(2)}) %all-to-all-start.1) | async-done | bytes 131104 | tf_op jit(solution)/shard_map/all_to_all | solution.py:338
  87.7 2.6 %shard_map.46 = f32[256,128]{1,0:T(8,128)} custom-call(f32[256,128]{1,0:T(8,128)} %broadcast_in_dim.243.lower_ref, f32[256,128]{1,0:T(8,128)} %copy.457.main_ref, f32[256,128]{1,0:T(8,128)} %broadcast_in_dim.247.upper_ref, f32[256,128]{1,0:T(8,128)} %copy.404.rhs_ref), custom_call_target="tpu_custom_call" | custom-call | tf_op jit(solution)/shard_map/pallas_call | solution.py:240
  92.9 10.4 %shard_map.48 = f32[4,8,64]{2,1,0:T(8,128)} custom-call(f32[8,64]{1,0:T(8,128)} %concatenate.387.ends_ref), custom_call_target="tpu_custom_call" | custom-call | tf_op jit(solution)/shard_map/pallas_call | solution.py:276
  103.3 1.3 gather_fusion
  106.0 1.3 divide_bitcast_fusion.18
  108.3 3.3 %collective-permute-start.4 = (f32[1,64,258]{2,1,0:T(8,128)S(1)}, f32[1,64,258]{2,1,0:T(8,128)S(1)}, u32[]{:S(2)}, u32[]{:S(2)}) collective-permute-start(f32[1,64,258]{2,1,0:T(8,128)S(1)} %copy.432), channel_id=1, source_target_pairs={{0,4},{4,8},{8,12},{12,16},{16,20},{20,24},{24,28},{28,32},{32,36}... | collective-permute-start | bytes 198152 | tf_op jit(solution)/shard_map/ppermute | solution.py:464
  111.9 1.9 %collective-permute-start.5 = (f32[1,64,258]{2,1,0:T(8,128)S(1)}, f32[1,64,258]{2,1,0:T(8,128)S(1)}, u32[]{:S(2)}, u32[]{:S(2)}) collective-permute-start(f32[1,64,258]{2,1,0:T(8,128)S(1)} %copy.439), channel_id=1, source_target_pairs={{4,0},{8,4},{12,8},{16,12},{20,16},{24,20},{28,24},{32,28},{36,32}... | collective-permute-start | bytes 198152 | tf_op jit(solution)/shard_map/ppermute | solution.py:465
  114.0 3.9 %collective-permute-done.5 = f32[1,64,258]{2,1,0:T(8,128)S(1)} collective-permute-done((f32[1,64,258]{2,1,0:T(8,128)S(1)}, f32[1,64,258]{2,1,0:T(8,128)S(1)}, u32[]{:S(2)}, u32[]{:S(2)}) %collective-permute-start.5) | collective-permute-done | bytes 66080 | tf_op jit(solution)/shard_map/ppermute | solution.py:465
  118.8 23.9 %all_to_all.64 = f32[2,128,128]{2,0,1:T(2,128)S(1)} all-to-all(f32[2,128,128]{2,0,1:T(2,128)S(1)} %copy.442), channel_id=1, replica_groups=mesh['spot'=128,'var'=4] {'spot'}, dimensions={1} | all-to-all | bytes 262144 | tf_op jit(solution)/shard_map/all_to_all | solution.py:318
  143.7 16.4 %all_to_all.65 = f32[128,2,128]{2,1,0:T(2,128)S(1)} all-to-all(f32[128,2,128]{2,1,0:T(2,128)S(1)} %copy.455), channel_id=1, replica_groups=mesh['spot'=128,'var'=4] {'spot'}, dimensions={0} | all-to-all | bytes 262144 | tf_op jit(solution)/shard_map/all_to_all | solution.py:338
  160.9 2.6 %shard_map.49 = f32[256,128]{1,0:T(8,128)} custom-call(f32[256,128]{1,0:T(8,128)} %broadcast_in_dim.243.lower_ref, f32[256,128]{1,0:T(8,128)} %copy.457.main_ref, f32[256,128]{1,0:T(8,128)} %broadcast_in_dim.247.upper_ref, f32[256,128]{1,0:T(8,128)} %copy.458.rhs_ref), custom_call_target="tpu_custom_call" | custom-call | tf_op jit(solution)/shard_map/pallas_call | solution.py:240
  166.0 8.6 %shard_map.50 = f32[4,8,64]{2,1,0:T(8,128)} custom-call(f32[8,64]{1,0:T(8,128)} %concatenate.431.ends_ref), custom_call_target="tpu_custom_call" | custom-call | tf_op jit(solution)/shard_map/pallas_call | solution.py:276
  174.7 1.3 gather_fusion.1
  177.0 1.2 divide_bitcast_fusion.19
  (470 shorter events, 37.2 us)
Async XLA Ops:
  1.0 23.5 %collective-permute-start = (f32[2,64,1]{2,1,0:T(8,128)S(1)}, f32[2,64,1]{2,1,0:T(8,128)S(1)}, u32[]{:S(2)}, u32[]{:S(2)}) collective-permute-start(f32[2,64,1]{2,1,0:T(8,128)S(1)} %get-tuple-element.122), channel_id=1, source_target_pairs={{0,1},{1,2},{2,3},{4,5},{5,6},{6,7},{8,9},{9,10},{10,11},{12,13},{... | collective-permute-start | bytes 1544 | tf_op jit(solution)/shard_map/ppermute | solution.py:38
  6.0 18.5 %collective-permute-start.1 = (f32[2,64,1]{2,1,0:T(8,128)S(1)}, f32[2,64,1]{2,1,0:T(8,128)S(1)}, u32[]{:S(2)}, u32[]{:S(2)}) collective-permute-start(f32[2,64,1]{2,1,0:T(8,128)S(1)} %get-tuple-element.123), channel_id=1, source_target_pairs={{1,0},{2,1},{3,2},{5,4},{6,5},{7,6},{9,8},{10,9},{11,10},{13,12},{... | collective-permute-start | bytes 1544 | tf_op jit(solution)/shard_map/ppermute | solution.py:39
  7.3 0.7 copy-start.3
  12.2 0.7 copy-start.1
  13.3 0.7 copy-start.2
  21.6 2.8 %copy-start = (f32[2,64,256]{2,1,0:T(8,128)S(1)}, f32[2,64,256]{2,1,0:T(8,128)}, u32[]{:S(2)}) copy-start(f32[2,64,256]{2,1,0:T(8,128)} %param.6) | copy-start | bytes 393220
  24.6 6.4 %collective-permute-start.2 = (f32[1,64,258]{2,1,0:T(8,128)S(1)}, f32[1,64,258]{2,1,0:T(8,128)S(1)}, u32[]{:S(2)}, u32[]{:S(2)}) collective-permute-start(f32[1,64,258]{2,1,0:T(8,128)S(1)} %get-tuple-element.118), channel_id=1, source_target_pairs={{0,4},{4,8},{8,12},{12,16},{16,20},{20,24},{24,28},{28,32},{32,36}... | collective-permute-start | bytes 198152 | tf_op jit(solution)/shard_map/ppermute | solution.py:38
  28.6 5.9 %collective-permute-start.3 = (f32[1,64,258]{2,1,0:T(8,128)S(1)}, f32[1,64,258]{2,1,0:T(8,128)S(1)}, u32[]{:S(2)}, u32[]{:S(2)}) collective-permute-start(f32[1,64,258]{2,1,0:T(8,128)S(1)} %get-tuple-element.119), channel_id=1, source_target_pairs={{4,0},{8,4},{12,8},{16,12},{20,16},{24,20},{28,24},{32,28},{36,32}... | collective-permute-start | bytes 198152 | tf_op jit(solution)/shard_map/ppermute | solution.py:39
  36.6 28.4 %all-to-all-start = ((f32[2,128,128]{2,0,1:T(2,128)}), f32[2,128,128]{2,0,1:T(2,128)S(1)}, u32[]{:S(2)}, u32[]{:S(2)}) async-start(f32[2,128,128]{2,0,1:T(2,128)} %copy.388), calls=%async_computation | async-start | bytes 262144 | tf_op jit(solution)/shard_map/all_to_all | solution.py:318
  67.6 19.3 %all-to-all-start.1 = ((f32[128,2,128]{2,1,0:T(2,128)}), f32[128,2,128]{2,1,0:T(2,128)S(1)}, u32[]{:S(2)}, u32[]{:S(2)}) async-start(f32[128,2,128]{2,1,0:T(2,128)} %copy.401), calls=%async_computation.1 | async-start | bytes 262144 | tf_op jit(solution)/shard_map/all_to_all | solution.py:338
  108.3 5.6 %collective-permute-start.4 = (f32[1,64,258]{2,1,0:T(8,128)S(1)}, f32[1,64,258]{2,1,0:T(8,128)S(1)}, u32[]{:S(2)}, u32[]{:S(2)}) collective-permute-start(f32[1,64,258]{2,1,0:T(8,128)S(1)} %copy.432), channel_id=1, source_target_pairs={{0,4},{4,8},{8,12},{12,16},{16,20},{20,24},{24,28},{28,32},{32,36}... | collective-permute-start | bytes 198152 | tf_op jit(solution)/shard_map/ppermute | solution.py:464
  111.9 5.9 %collective-permute-start.5 = (f32[1,64,258]{2,1,0:T(8,128)S(1)}, f32[1,64,258]{2,1,0:T(8,128)S(1)}, u32[]{:S(2)}, u32[]{:S(2)}) collective-permute-start(f32[1,64,258]{2,1,0:T(8,128)S(1)} %copy.439), channel_id=1, source_target_pairs={{4,0},{8,4},{12,8},{16,12},{20,16},{24,20},{28,24},{32,28},{36,32}... | collective-permute-start | bytes 198152 | tf_op jit(solution)/shard_map/ppermute | solution.py:465

commit v9 on v8

--- a/solution.py
+++ b/solution.py
@@ -334,7 +334,14 @@
         system = line_coefficients(
             diffusion, advection, rate_line / 3.0, spot_whole[1], spot_whole[2]
         )
-        solved = implicit(system, gathered, 0)
+        behind, centre, ahead = system
+        shape = gathered.shape
+        solved = line_solve(
+            jnp.broadcast_to(-solve_scale * behind, shape),
+            jnp.broadcast_to(1.0 - solve_scale * centre, shape),
+            jnp.broadcast_to(-solve_scale * ahead, shape),
+            gathered,
+        )
         return lax.all_to_all(solved, "spot", split_axis=0, concat_axis=1, tiled=True).reshape(
             spot_rows, planes, var_cols
         )

time: 181 us -> 189 us (1.044)
  waiting for transfers between devices: 19.1 us -> 24.8 us
  Pallas kernels: 27 us -> 32.3 us
  starting transfers between devices: 43.3 us -> 40.8 us
    all_to_all x1, waiting for transfers between devices: 4.27 us -> 9.88 us  [spot_solve(): lax.all_to_all(values.reshape(spot_rows, line_count), 'spot', split_axis=...]
    pallas_call x3 -> x5, Pallas kernels: 7.92 us -> 13.2 us  [line_solve(): pl.pallas_call(cyclic_kernel, out_shape=jax.ShapeDtypeStruct((count, widt...]
    all_to_all x1, starting transfers between devices: 8.17 us -> 5.59 us  [spot_solve(): lax.all_to_all(solved, 'spot', split_axis=0, concat_axis=1, tiled=True)]
    slice x63 -> x28, local copies, waits for them, and re-layouts: 4.15 us -> 3.61 us  [odd_rows(): return lax.slice_in_dim(source, 1, length, 2, dimension)]
where the time goes in v9:
time: 189 us; the launch traced here: 187 us
  blocking collectives  41.1 us (22%)
  starting transfers between devices  40.8 us (22%)
  Pallas kernels  32.3 us (17%)
  local copies, waits for them, and re-layouts  29.1 us (15%)
  waiting for transfers between devices  24.8 us (13%)
  other arithmetic  14.4 us (8%)
  between operations  4.93 us (3%)
    all_to_all x1, blocking collectives, spot_solve(): lax.all_to_all(values.reshape(spot_rows, line_count), 'spot', split_axis=...  24.1 us
    pallas_call x2, Pallas kernels, gather_var(): pl.pallas_call(functools.partial(gather_kernel, blocks), out_shape=jax.Sh...  19 us
    all_to_all x1, starting transfers between devices, spot_solve(): lax.all_to_all(values.reshape(spot_rows, line_count), 'spot', split_axis=...  17.3 us
    all_to_all x1, blocking collectives, spot_solve(): lax.all_to_all(solved, 'spot', split_axis=0, concat_axis=1, tiled=True)  17 us
    pallas_call x5, Pallas kernels, line_solve(): pl.pallas_call(cyclic_kernel, out_shape=jax.ShapeDtypeStruct((count, widt...  13.2 us
    all_to_all x1, waiting for transfers between devices, spot_solve(): lax.all_to_all(values.reshape(spot_rows, line_count), 'spot', split_axis=...  9.88 us
    ppermute x2, starting transfers between devices, padded_2(): before = lax.ppermute(last, axis, up)  9 us
    all_to_all x1, waiting for transfers between devices, spot_solve(): lax.all_to_all(solved, 'spot', split_axis=0, concat_axis=1, tiled=True)  7.44 us
  transfers between devices with their start and end apart: 8, of which 4 were waited for; matrix products, arithmetic and copies ran while one was open for 11% of the time, Pallas kernels for 1%

profile of v9, /device:TPU:1, one launch (start us, length us, event | category | flops | bytes accessed | tf_op | source)
XLA Modules:
  0.0 187.4 jit_solution(6138083996365330147)
XLA Ops:
  1.0 5.0 %collective-permute-start = (f32[2,64,1]{2,1,0:T(8,128)S(1)}, f32[2,64,1]{2,1,0:T(8,128)S(1)}, u32[]{:S(2)}, u32[]{:S(2)}) collective-permute-start(f32[2,64,1]{2,1,0:T(8,128)S(1)} %get-tuple-element.96), channel_id=1, source_target_pairs={{0,1},{1,2},{2,3},{4,5},{5,6},{6,7},{8,9},{9,10},{10,11},{12,13},{... | collective-permute-start | bytes 1544 | tf_op jit(solution)/shard_map/ppermute | solution.py:38
  6.0 1.3 collective-permute-start.1
  22.4 2.1 %select_select_fusion.rhs_ref = f32[256,128]{1,0:T(8,128)} fusion(f32[]{:T(128)} %bitcast.11, f32[]{:T(128)} %bitcast.10, pred[128]{0:T(512)(128)(4,1)S(1)} %iota.40, pred[128]{0:T(512)(128)(4,1)S(1)} %iota.34, pred[256]{0:T(512)(128)(4,1)S(1)} %get-tuple-element.223, pred[256]{0:T(512)(128)(4,1)S(1)} %get-tuple-element.224), kind=kLoop, calls=%fused_computation.128 | loop fusion | flops 131072 | bytes 131848 | tf_op jit(solution)/shard_map/jit(_where)/select_n | solution.py:370
  26.0 2.6 %shard_map.48 = f32[256,128]{1,0:T(8,128)} custom-call(f32[256,128]{1,0:T(8,128)} %broadcast_in_dim.243.lower_ref, f32[256,128]{1,0:T(8,128)} %copy.264.main_ref, f32[256,128]{1,0:T(8,128)} %broadcast_in_dim.247.upper_ref, f32[256,128]{1,0:T(8,128)} %select_select_fusion.rhs_ref), custom_call_target="tpu_custom_call" | custom-call | tf_op jit(solution)/shard_map/pallas_call | solution.py:240
  31.4 4.0 %collective-permute-start.2 = (f32[1,64,258]{2,1,0:T(8,128)S(1)}, f32[1,64,258]{2,1,0:T(8,128)S(1)}, u32[]{:S(2)}, u32[]{:S(2)}) collective-permute-start(f32[1,64,258]{2,1,0:T(8,128)S(1)} %get-tuple-element.92), channel_id=1, source_target_pairs={{0,4},{4,8},{8,12},{12,16},{16,20},{20,24},{24,28},{28,32},{32,36}... | collective-permute-start | bytes 198152 | tf_op jit(solution)/shard_map/ppermute | solution.py:38
  35.4 2.4 %collective-permute-start.3 = (f32[1,64,258]{2,1,0:T(8,128)S(1)}, f32[1,64,258]{2,1,0:T(8,128)S(1)}, u32[]{:S(2)}, u32[]{:S(2)}) collective-permute-start(f32[1,64,258]{2,1,0:T(8,128)S(1)} %get-tuple-element.93), channel_id=1, source_target_pairs={{4,0},{8,4},{12,8},{16,12},{20,16},{24,20},{28,24},{32,28},{36,32}... | collective-permute-start | bytes 198152 | tf_op jit(solution)/shard_map/ppermute | solution.py:39
  37.8 3.5 %collective-permute-done.3 = f32[1,64,258]{2,1,0:T(8,128)S(1)} collective-permute-done((f32[1,64,258]{2,1,0:T(8,128)S(1)}, f32[1,64,258]{2,1,0:T(8,128)S(1)}, u32[]{:S(2)}, u32[]{:S(2)}) %collective-permute-start.3) | collective-permute-done | bytes 66080 | tf_op jit(solution)/shard_map/ppermute | solution.py:39
  43.4 17.3 %all-to-all-start = ((f32[2,128,128]{2,0,1:T(2,128)}), f32[2,128,128]{2,0,1:T(2,128)S(1)}, u32[]{:S(2)}, u32[]{:S(2)}) async-start(f32[2,128,128]{2,0,1:T(2,128)} %copy.221), calls=%async_computation | async-start | bytes 262144 | tf_op jit(solution)/shard_map/all_to_all | solution.py:318
  61.9 9.9 %all-to-all-done = f32[2,128,128]{2,0,1:T(2,128)S(1)} async-done(((f32[2,128,128]{2,0,1:T(2,128)}), f32[2,128,128]{2,0,1:T(2,128)S(1)}, u32[]{:S(2)}, u32[]{:S(2)}) %all-to-all-start) | async-done | bytes 131104 | tf_op jit(solution)/shard_map/all_to_all | solution.py:318
  72.4 2.7 %shard_map.46 = f32[256,128]{1,0:T(8,128)} custom-call(f32[256,128]{1,0:T(8,128)} %get-tuple-element.139.lower_ref, f32[256,128]{1,0:T(8,128)} %get-tuple-element.138.main_ref, f32[256,128]{1,0:T(8,128)} %get-tuple-element.137.upper_ref, f32[256,128]{1,0:T(8,128)} %bitcast.236), custom_call_target="tpu_custom_call" | custom-call | tf_op jit(solution)/shard_map/pallas_call | solution.py:240
  75.1 5.6 %all-to-all-start.1 = ((f32[128,2,128]{2,1,0:T(2,128)}), f32[128,2,128]{2,1,0:T(2,128)S(1)}, u32[]{:S(2)}, u32[]{:S(2)}) async-start(f32[128,2,128]{2,1,0:T(2,128)} %bitcast.237), calls=%async_computation.1 | async-start | bytes 262144 | tf_op jit(solution)/shard_map/all_to_all | solution.py:345
  84.5 7.4 %all-to-all-done.1 = f32[128,2,128]{2,1,0:T(2,128)S(1)} async-done(((f32[128,2,128]{2,1,0:T(2,128)}), f32[128,2,128]{2,1,0:T(2,128)S(1)}, u32[]{:S(2)}, u32[]{:S(2)}) %all-to-all-start.1) | async-done | bytes 131104 | tf_op jit(solution)/shard_map/all_to_all | solution.py:345
  92.8 2.6 %shard_map.47 = f32[256,128]{1,0:T(8,128)} custom-call(f32[256,128]{1,0:T(8,128)} %broadcast_in_dim.243.lower_ref, f32[256,128]{1,0:T(8,128)} %copy.264.main_ref, f32[256,128]{1,0:T(8,128)} %broadcast_in_dim.247.upper_ref, f32[256,128]{1,0:T(8,128)} %copy.224.rhs_ref), custom_call_target="tpu_custom_call" | custom-call | tf_op jit(solution)/shard_map/pallas_call | solution.py:240
  97.9 10.4 %shard_map.49 = f32[4,8,64]{2,1,0:T(8,128)} custom-call(f32[8,64]{1,0:T(8,128)} %concatenate.184.ends_ref), custom_call_target="tpu_custom_call" | custom-call | tf_op jit(solution)/shard_map/pallas_call | solution.py:276
  111.0 1.3 divide_bitcast_fusion.8
  113.3 3.4 %collective-permute-start.4 = (f32[1,64,258]{2,1,0:T(8,128)S(1)}, f32[1,64,258]{2,1,0:T(8,128)S(1)}, u32[]{:S(2)}, u32[]{:S(2)}) collective-permute-start(f32[1,64,258]{2,1,0:T(8,128)S(1)} %copy.252), channel_id=1, source_target_pairs={{0,4},{4,8},{8,12},{12,16},{16,20},{20,24},{24,28},{28,32},{32,36}... | collective-permute-start | bytes 198152 | tf_op jit(solution)/shard_map/ppermute | solution.py:471
  117.1 1.9 %collective-permute-start.5 = (f32[1,64,258]{2,1,0:T(8,128)S(1)}, f32[1,64,258]{2,1,0:T(8,128)S(1)}, u32[]{:S(2)}, u32[]{:S(2)}) collective-permute-start(f32[1,64,258]{2,1,0:T(8,128)S(1)} %copy.259), channel_id=1, source_target_pairs={{4,0},{8,4},{12,8},{16,12},{20,16},{24,20},{28,24},{32,28},{36,32}... | collective-permute-start | bytes 198152 | tf_op jit(solution)/shard_map/ppermute | solution.py:472
  119.1 3.9 %collective-permute-done.5 = f32[1,64,258]{2,1,0:T(8,128)S(1)} collective-permute-done((f32[1,64,258]{2,1,0:T(8,128)S(1)}, f32[1,64,258]{2,1,0:T(8,128)S(1)}, u32[]{:S(2)}, u32[]{:S(2)}) %collective-permute-start.5) | collective-permute-done | bytes 66080 | tf_op jit(solution)/shard_map/ppermute | solution.py:472
  124.0 24.1 %all_to_all.70 = f32[2,128,128]{2,0,1:T(2,128)} all-to-all(f32[2,128,128]{2,0,1:T(2,128)S(1)} %copy.262), channel_id=1, replica_groups=mesh['spot'=128,'var'=4] {'spot'}, dimensions={1} | all-to-all | bytes 262144 | tf_op jit(solution)/shard_map/all_to_all | solution.py:318
  148.0 2.6 %shard_map.50 = f32[256,128]{1,0:T(8,128)} custom-call(f32[256,128]{1,0:T(8,128)} %get-tuple-element.139.lower_ref, f32[256,128]{1,0:T(8,128)} %get-tuple-element.138.main_ref, f32[256,128]{1,0:T(8,128)} %get-tuple-element.137.upper_ref, f32[256,128]{1,0:T(8,128)} %bitcast.238), custom_call_target="tpu_custom_call" | custom-call | tf_op jit(solution)/shard_map/pallas_call | solution.py:240
  150.7 17.0 %all_to_all.71 = f32[128,2,128]{2,1,0:T(2,128)S(1)} all-to-all(f32[128,2,128]{2,1,0:T(2,128)} %bitcast.239), channel_id=1, replica_groups=mesh['spot'=128,'var'=4] {'spot'}, dimensions={0} | all-to-all | bytes 262144 | tf_op jit(solution)/shard_map/all_to_all | solution.py:345
  168.5 2.6 %shard_map.51 = f32[256,128]{1,0:T(8,128)} custom-call(f32[256,128]{1,0:T(8,128)} %broadcast_in_dim.243.lower_ref, f32[256,128]{1,0:T(8,128)} %copy.264.main_ref, f32[256,128]{1,0:T(8,128)} %broadcast_in_dim.247.upper_ref, f32[256,128]{1,0:T(8,128)} %copy.265.rhs_ref), custom_call_target="tpu_custom_call" | custom-call | tf_op jit(solution)/shard_map/pallas_call | solution.py:240
  173.6 8.6 %shard_map.52 = f32[4,8,64]{2,1,0:T(8,128)} custom-call(f32[8,64]{1,0:T(8,128)} %concatenate.214.ends_ref), custom_call_target="tpu_custom_call" | custom-call | tf_op jit(solution)/shard_map/pallas_call | solution.py:276
  184.6 1.3 divide_bitcast_fusion.9
  (300 shorter events, 38.9 us)
Async XLA Ops:
  1.0 29.6 %collective-permute-start = (f32[2,64,1]{2,1,0:T(8,128)S(1)}, f32[2,64,1]{2,1,0:T(8,128)S(1)}, u32[]{:S(2)}, u32[]{:S(2)}) collective-permute-start(f32[2,64,1]{2,1,0:T(8,128)S(1)} %get-tuple-element.96), channel_id=1, source_target_pairs={{0,1},{1,2},{2,3},{4,5},{5,6},{6,7},{8,9},{9,10},{10,11},{12,13},{... | collective-permute-start | bytes 1544 | tf_op jit(solution)/shard_map/ppermute | solution.py:38
  6.0 24.5 %collective-permute-start.1 = (f32[2,64,1]{2,1,0:T(8,128)S(1)}, f32[2,64,1]{2,1,0:T(8,128)S(1)}, u32[]{:S(2)}, u32[]{:S(2)}) collective-permute-start(f32[2,64,1]{2,1,0:T(8,128)S(1)} %get-tuple-element.97), channel_id=1, source_target_pairs={{1,0},{2,1},{3,2},{5,4},{6,5},{7,6},{9,8},{10,9},{11,10},{13,12},{... | collective-permute-start | bytes 1544 | tf_op jit(solution)/shard_map/ppermute | solution.py:39
  7.3 0.7 copy-start.4
  12.2 0.7 copy-start.2
  13.3 0.7 copy-start.3
  30.4 0.9 copy-start
  31.4 6.4 %collective-permute-start.2 = (f32[1,64,258]{2,1,0:T(8,128)S(1)}, f32[1,64,258]{2,1,0:T(8,128)S(1)}, u32[]{:S(2)}, u32[]{:S(2)}) collective-permute-start(f32[1,64,258]{2,1,0:T(8,128)S(1)} %get-tuple-element.92), channel_id=1, source_target_pairs={{0,4},{4,8},{8,12},{12,16},{16,20},{20,24},{24,28},{28,32},{32,36}... | collective-permute-start | bytes 198152 | tf_op jit(solution)/shard_map/ppermute | solution.py:38
  35.4 5.9 %collective-permute-start.3 = (f32[1,64,258]{2,1,0:T(8,128)S(1)}, f32[1,64,258]{2,1,0:T(8,128)S(1)}, u32[]{:S(2)}, u32[]{:S(2)}) collective-permute-start(f32[1,64,258]{2,1,0:T(8,128)S(1)} %get-tuple-element.93), channel_id=1, source_target_pairs={{4,0},{8,4},{12,8},{16,12},{20,16},{24,20},{28,24},{32,28},{36,32}... | collective-permute-start | bytes 198152 | tf_op jit(solution)/shard_map/ppermute | solution.py:39
  43.4 28.4 %all-to-all-start = ((f32[2,128,128]{2,0,1:T(2,128)}), f32[2,128,128]{2,0,1:T(2,128)S(1)}, u32[]{:S(2)}, u32[]{:S(2)}) async-start(f32[2,128,128]{2,0,1:T(2,128)} %copy.221), calls=%async_computation | async-start | bytes 262144 | tf_op jit(solution)/shard_map/all_to_all | solution.py:318
  71.8 0.7 copy-start.1
  75.1 16.9 %all-to-all-start.1 = ((f32[128,2,128]{2,1,0:T(2,128)}), f32[128,2,128]{2,1,0:T(2,128)S(1)}, u32[]{:S(2)}, u32[]{:S(2)}) async-start(f32[128,2,128]{2,1,0:T(2,128)} %bitcast.237), calls=%async_computation.1 | async-start | bytes 262144 | tf_op jit(solution)/shard_map/all_to_all | solution.py:345
  113.3 5.7 %collective-permute-start.4 = (f32[1,64,258]{2,1,0:T(8,128)S(1)}, f32[1,64,258]{2,1,0:T(8,128)S(1)}, u32[]{:S(2)}, u32[]{:S(2)}) collective-permute-start(f32[1,64,258]{2,1,0:T(8,128)S(1)} %copy.252), channel_id=1, source_target_pairs={{0,4},{4,8},{8,12},{12,16},{16,20},{20,24},{24,28},{28,32},{32,36}... | collective-permute-start | bytes 198152 | tf_op jit(solution)/shard_map/ppermute | solution.py:471
  117.1 5.9 %collective-permute-start.5 = (f32[1,64,258]{2,1,0:T(8,128)S(1)}, f32[1,64,258]{2,1,0:T(8,128)S(1)}, u32[]{:S(2)}, u32[]{:S(2)}) collective-permute-start(f32[1,64,258]{2,1,0:T(8,128)S(1)} %copy.259), channel_id=1, source_target_pairs={{4,0},{8,4},{12,8},{16,12},{20,16},{24,20},{28,24},{32,28},{36,32}... | collective-permute-start | bytes 198152 | tf_op jit(solution)/shard_map/ppermute | solution.py:472
